TPU v7x, 128 devices: a whole 4x4x4 slice. The times are simulated.
128 devices in a mesh: neg: 16 (over y, z), rep: 8 (over x, core).
Axes of the slice: x: 4, y: 4, z: 4, core: 2. Of those that a mesh axis runs over, the one named last changes fastest.
Arguments:
- goal_states: bfloat16 [8, 128, 128, 512], P('rep', 'neg'), may hold values from -6 to 6
- premise_states: bfloat16 [8, 512, 128, 512], P('rep', 'neg'), may hold values from -6 to 6
- goal_ids: int32 [8, 128, 128], P('rep', 'neg'), may hold values from 0 to 31999, as said below
- premise_ids: int32 [8, 512, 128], P('rep', 'neg'), may hold values from 0 to 31999, as said below
- positives: int32 [8, 128], P('rep'), may hold values from 0 to 511
- depthwise_kernels: float32 [2, 3, 512], replicated, may hold values from -3.5 to 3.5
- block_norm_gains: float32 [2, 512], replicated, may hold values from 0.25 to 1.75
- pointwise_weights: bfloat16 [2, 512, 512], replicated, may hold values from -0.25 to 0.25
- head_weight: bfloat16 [512, 256], replicated, may hold values from -0.25 to 0.25
Outputs:
- goal_loss: float32 [8, 128], P('rep', 'neg')
- grad_depth: float32 [2, 3, 512], replicated
- grad_gain: float32 [2, 512], replicated
- grad_point: float32 [2, 512, 512], replicated
- grad_head: float32 [512, 256], replicated
Inputs may be any that keep to these rules, and one draw needn't show every extreme that they name: `goal_ids`: id 0 marks padding: a sequence's ids are nonzero on its first positions and 0 after them, with at least 16 nonzero ids. `premise_ids`: id 0 marks padding: a sequence's ids are nonzero on its first positions and 0 after them, with at least 16 nonzero ids.
All inputs are finite; a program needn't handle non-finite values.
Results may differ from a plain program's by a relative error of at most 0.022.
Values may be sent and summed in bfloat16 or wider, within the bound.
No kernel may reach another device: no remote copies, remote signals or barrier semaphores. Data moves between devices by JAX's collectives and lax.ppermute only.
A program may use at most 192 MiB of HBM per device.

v0:
```python
import jax
import jax.numpy as jnp
from jax import lax
from jax.sharding import PartitionSpec as P

LOWER_DILATION = 4
UPPER_DILATION = 8


logit_scale = 20.0


def shift_down(values, dilation):
    return jnp.pad(values, ((0, 0), (dilation, 0), (0, 0)))[:, : values.shape[1]]


def shift_up(values, dilation):
    return jnp.pad(values, ((0, 0), (0, dilation), (0, 0)))[:, dilation:]


def depth_conv(inputs, kernel, dilation):
    return (
        kernel[0] * shift_down(inputs, dilation)
        + kernel[1] * inputs
        + kernel[2] * shift_up(inputs, dilation)
    )


def conv_block_forward(hidden, kernel, gain, weight, token_valid_mask, dilation):
    widened = hidden.astype(jnp.float32)
    inverse = lax.rsqrt(jnp.mean(widened * widened, axis=-1, keepdims=True) + 1e-06)
    normed = widened * inverse * gain * token_valid_mask
    mixed = depth_conv(normed, kernel, dilation).astype(jnp.bfloat16)
    count, length, width = hidden.shape
    pre_act = jnp.dot(
        mixed.reshape(count * length, width), weight, preferred_element_type=jnp.float32
    ).reshape(count, length, width)
    output = (widened + jax.nn.gelu(pre_act, approximate=True)).astype(jnp.bfloat16)
    return (output, (inverse, mixed, pre_act))


def conv_block_backward(
    upstream, hidden, saved, kernel, gain, weight, token_valid_mask, dilation, need_input
):
    inverse, mixed, pre_act = saved
    widened = hidden.astype(jnp.float32)
    normed = widened * inverse * gain * token_valid_mask
    ignored_value, gelu_back = jax.vjp(lambda value: jax.nn.gelu(value, approximate=True), pre_act)
    act_grad = gelu_back(upstream)[0].astype(jnp.bfloat16)
    count, length, width = hidden.shape
    flat_grad = act_grad.reshape(count * length, width)
    grad_weight = jnp.dot(
        mixed.reshape(count * length, width).T, flat_grad, preferred_element_type=jnp.float32
    )
    conv_grad = jnp.dot(flat_grad, weight.T, preferred_element_type=jnp.float32).reshape(
        count, length, width
    )
    grad_kernel = jnp.stack(
        [
            jnp.sum(shift_down(normed, dilation) * conv_grad, axis=(0, 1)),
            jnp.sum(normed * conv_grad, axis=(0, 1)),
            jnp.sum(shift_up(normed, dilation) * conv_grad, axis=(0, 1)),
        ]
    )
    normed_grad = (
        kernel[0] * shift_up(conv_grad, dilation)
        + kernel[1] * conv_grad
        + kernel[2] * shift_down(conv_grad, dilation)
    ) * token_valid_mask
    grad_gain = jnp.sum(normed_grad * widened * inverse, axis=(0, 1))
    input_grad = None
    if need_input:
        scaled = normed_grad * gain
        input_grad = (
            upstream
            + inverse * scaled
            - widened * inverse**3 * jnp.mean(scaled * widened, axis=-1, keepdims=True)
        )
    return (input_grad, grad_kernel, grad_gain, grad_weight)


def pool_forward(hidden, token_valid_mask, head_weight):
    widened = hidden.astype(jnp.float32)
    counts = jnp.sum(token_valid_mask, axis=1)
    pooled = (jnp.sum(widened * token_valid_mask, axis=1) / counts).astype(jnp.bfloat16)
    embedded = jnp.dot(pooled, head_weight, preferred_element_type=jnp.float32)
    magnitude = jnp.sqrt(jnp.sum(embedded * embedded, axis=-1, keepdims=True) + 1e-06)
    unit = embedded / magnitude
    return (unit.astype(jnp.bfloat16), (counts, pooled, unit, magnitude))


def pool_backward(unit_grad, saved, token_valid_mask, head_weight):
    counts, pooled, unit, magnitude = saved
    embed_grad = (
        (unit_grad - unit * jnp.sum(unit * unit_grad, axis=-1, keepdims=True)) / magnitude
    ).astype(jnp.bfloat16)
    grad_head = jnp.dot(pooled.T, embed_grad, preferred_element_type=jnp.float32)
    pooled_grad = jnp.dot(embed_grad, head_weight.T, preferred_element_type=jnp.float32)
    hidden_gradient = (pooled_grad / counts)[:, None, :] * token_valid_mask
    return (hidden_gradient, grad_head)


def local(
    goal_states,
    premise_states,
    goal_ids,
    premise_ids,
    positives,
    depthwise_kernels,
    block_norm_gains,
    pointwise_weights,
    head_weight,
):
    goal_count = goal_states.shape[1]
    token_states = jnp.concatenate([goal_states[0], premise_states[0]], axis=0)
    token_ids = jnp.concatenate([goal_ids[0], premise_ids[0]], axis=0)
    token_valid_mask = (token_ids != 0).astype(jnp.float32)[..., None]
    first_hidden, lower_residuals = conv_block_forward(
        token_states,
        depthwise_kernels[0],
        block_norm_gains[0],
        pointwise_weights[0],
        token_valid_mask,
        LOWER_DILATION,
    )
    second_hidden, upper_residuals = conv_block_forward(
        first_hidden,
        depthwise_kernels[1],
        block_norm_gains[1],
        pointwise_weights[1],
        token_valid_mask,
        UPPER_DILATION,
    )
    units, saved_pool = pool_forward(second_hidden, token_valid_mask, head_weight)
    goal_units = units[:goal_count]
    premise_units = units[goal_count:]
    group_positive = positives[0]
    position = lax.axis_index("neg")
    group_premises = lax.all_gather(premise_units, "neg", axis=0, tiled=True)
    own_positive = lax.dynamic_slice_in_dim(group_positive, position * goal_count, goal_count)
    scores = logit_scale * lax.dot_general(
        goal_units, group_premises, (((1,), (1,)), ((), ())), preferred_element_type=jnp.float32
    )
    expon = jnp.exp(scores)
    total = jnp.sum(expon, axis=1, keepdims=True)
    columns = jnp.arange(group_premises.shape[0], dtype=jnp.int32)
    onehot = (columns[None, :] == own_positive[:, None]).astype(jnp.float32)
    losses = jnp.log(total[:, 0]) - jnp.sum(scores * onehot, axis=1)
    score_grad = ((expon / total - onehot) / goal_count).astype(jnp.bfloat16)
    goal_grad = logit_scale * jnp.dot(
        score_grad, group_premises, preferred_element_type=jnp.float32
    )
    premise_grad = lax.psum_scatter(
        logit_scale
        * lax.dot_general(
            score_grad, goal_units, (((0,), (0,)), ((), ())), preferred_element_type=jnp.float32
        ),
        "neg",
        scatter_dimension=0,
        tiled=True,
    )
    unit_grad = jnp.concatenate([goal_grad, premise_grad], axis=0)
    hidden_gradient, grad_head = pool_backward(unit_grad, saved_pool, token_valid_mask, head_weight)
    lower_gradient, upper_kernel, upper_gain, upper_weight = conv_block_backward(
        hidden_gradient,
        first_hidden,
        upper_residuals,
        depthwise_kernels[1],
        block_norm_gains[1],
        pointwise_weights[1],
        token_valid_mask,
        UPPER_DILATION,
        True,
    )
    ignored_value, lower_kernel, lower_gain, lower_weight = conv_block_backward(
        lower_gradient,
        token_states,
        lower_residuals,
        depthwise_kernels[0],
        block_norm_gains[0],
        pointwise_weights[0],
        token_valid_mask,
        LOWER_DILATION,
        False,
    )
    grad_head, upper_kernel, upper_gain, upper_weight, lower_kernel, lower_gain, lower_weight = (
        lax.psum(
            (
                grad_head,
                upper_kernel,
                upper_gain,
                upper_weight,
                lower_kernel,
                lower_gain,
                lower_weight,
            ),
            ("neg", "rep"),
        )
    )
    return (
        losses[None, :],
        jnp.stack([lower_kernel, upper_kernel]),
        jnp.stack([lower_gain, upper_gain]),
        jnp.stack([lower_weight, upper_weight]),
        grad_head,
    )


def solution(mesh):
    placed = (
        P("rep", "neg", None, None),
        P("rep", "neg", None, None),
        P("rep", "neg", None),
        P("rep", "neg", None),
        P("rep", None),
        P(),
        P(),
        P(),
        P(),
    )
    return jax.shard_map(
        local,
        mesh=mesh,
        in_specs=placed,
        out_specs=(P("rep", "neg"), P(), P(), P(), P()),
        check_vma=False,
    )
```

profile of v0, /device:TPU:1, one launch (start us, length us, event | category | flops | bytes accessed | tf_op | source)
XLA Modules:
  0.0 381.3 jit_solution(8069405610005554650)
XLA Ops:
  8.8 3.6 fusion.24
  13.1 4.0 %fusion.26 = f32[40,128,512]{2,1,0:T(8,128)S(1)} fusion(f32[40,128]{1,0:T(8,128)S(1)} %fusion.54, f32[512]{0:T(512)S(1)} %bitcast.95, f32[40,128]{1,0:T(8,128)S(1)} %add_rsqrt_fusion.1, bf16[32,128,512]{2,1,0:T(8,128)(2,1)} %bitcast.69, bf16[8,128,512]{2,1,0:T(8,128)(2,1)} %bitcast.75), kind=kLoop, calls=%fused_computation.51 | loop fusion | flops 13107200 | bytes 15771648 | tf_op jit(solution)/shard_map/mul | solution.py:32
  17.1 5.3 %copy-done.2 = f32[40,128,512]{2,1,0:T(8,128)} copy-done((f32[40,128,512]{2,1,0:T(8,128)}, f32[40,128,512]{2,1,0:T(8,128)S(1)}, u32[]{:S(2)}) %copy-start.2) | copy-done | bytes 10485784
  22.4 3.8 add_convert_fusion.1
  26.2 8.3 %fusion.33 = (f32[40,128]{1,0:T(8,128)S(1)}, bf16[40,128,512]{2,1,0:T(8,128)(2,1)S(1)}, f32[40,128,512]{2,1,0:T(8,128)}) fusion(bf16[32,128,512]{2,1,0:T(8,128)(2,1)S(1)} %bitcast.71, bf16[8,128,512]{2,1,0:T(8,128)(2,1)S(1)} %bitcast.76, bf16[40,128,512]{2,1,0:T(8,128)(2,1)S(1)} %add_convert_fusion.1, bf16[2,512,512]{2,1,0:T(8,128)(2,1)S(1)} %copy-done.9), kind=kOutput, calls=%fused_computation.58 | convolution fusion | flops 2723671040 | bytes 26759168 | tf_op jit(solution)/shard_map/dot_general | solution.py:35
  34.6 1.7 fusion.35
  36.3 4.0 %copy-done.3 = f32[40,128,512]{2,1,0:T(8,128)} copy-done((f32[40,128,512]{2,1,0:T(8,128)}, f32[40,128,512]{2,1,0:T(8,128)S(1)}, u32[]{:S(2)}) %copy-start.3) | copy-done | bytes 10485784
  40.3 4.4 %add_convert_fusion = bf16[40,128,512]{2,1,0:T(8,128)(2,1)S(1)} fusion(f32[40,128,512]{2,1,0:T(8,128)S(1)} %fusion.35, f32[512]{0:T(512)S(1)} %bitcast.85, f32[512]{0:T(512)S(1)} %bitcast.87, f32[512]{0:T(512)S(1)} %bitcast.83), kind=kLoop, calls=%fused_computation.73 | loop fusion | flops 15728640 | bytes 15734784 | tf_op jit(solution)/shard_map/convert_element_type | solution.py:33
  44.7 8.2 %multiply_reduce_fusion.6 = (f32[40,512]{1,0:T(8,128)S(1)}, f32[40,128,512]{2,1,0:T(8,128)}) fusion(f32[40,128]{1,0:T(8,128)S(1)} %fusion.54, bf16[40,128,512]{2,1,0:T(8,128)(2,1)S(1)} %get-tuple-element.34, bf16[40,128,512]{2,1,0:T(8,128)(2,1)S(1)} %add_convert_fusion, bf16[2,512,512]{2,1,0:T(8,128)(2,1)S(1)} %copy-done.9), kind=kOutput, calls=%fused_computation.72 | convolution fusion | flops 2721034240 | bytes 21598208 | tf_op jit(solution)/shard_map/dot_general | solution.py:35
  53.5 20.8 %all_gather.3 = bf16[512,256]{1,0:T(8,128)(2,1)S(1)} all-gather(bf16[32,256]{1,0:T(8,128)(2,1)S(1)} %slice.111), channel_id=1, replica_groups=mesh['neg'=16,'rep'=8] {'neg'}, dimensions={0}, use_global_device_ids=true | all-gather | bytes 278528 | tf_op jit(solution)/shard_map/all_gather | solution.py:139
  74.8 1.2 convolution_multiply_fusion
  76.9 74.6 %reduce-scatter.2.cloned.1.call-done = f32[32,256]{1,0:T(8,128)} async-done(((f32[512,256]{1,0:T(8,128)}), f32[32,256]{1,0:T(8,128)}) %reduce-scatter.2.cloned.1.call-update) | async-done | bytes 32784 | tf_op jit(solution)/shard_map/reduce_scatter | solution.py:153
  153.4 9.4 %fusion.23 = bf16[40,128,512]{2,1,0:T(8,128)(2,1)S(1)} fusion(f32[40,128,512]{2,1,0:T(8,128)} %get-tuple-element.47, f32[40,512]{1,0:T(8,128)S(1)} %convolution_divide_fusion, f32[40,128]{1,0:T(8,128)S(1)} %fusion.54), kind=kLoop, calls=%fused_computation.48 | loop fusion | flops 55050240 | bytes 15831040 | tf_op jit(solution)/shard_map/convert_element_type | solution.py:49
  162.8 3.9 %convolution_bitcast_fusion = f32[1,512,512]{2,1,0:T(8,128)} fusion(bf16[40,128,512]{2,1,0:T(8,128)(2,1)S(1)} %bitcast.73, bf16[40,128,512]{2,1,0:T(8,128)(2,1)S(1)} %fusion.23), kind=kOutput, calls=%fused_computation.78 | convolution fusion | flops 2684354560 | bytes 11534336 | tf_op jit(solution)/shard_map/dot_general | solution.py:52
  166.7 5.4 %fusion.42 = f32[40,128,512]{2,1,0:T(8,128)} fusion(bf16[40,128,512]{2,1,0:T(8,128)(2,1)S(1)} %fusion.23, bf16[2,512,512]{2,1,0:T(8,128)(2,1)S(1)} %copy-done.10), kind=kOutput, calls=%fused_computation.84 | convolution fusion | flops 2684354560 | bytes 16252928 | tf_op jit(solution)/shard_map/dot_general | solution.py:55
  172.1 18.8 %multiply_reduce_fusion.2 = (f32[512]{0:T(512)S(1)}, f32[512]{0:T(512)S(1)}, f32[512]{0:T(512)S(1)}, f32[40,128]{1,0:T(8,128)S(1)}, f32[512]{0:T(512)S(1)}, /*index=5*/f32[40,128,512]{2,1,0:T(8,128)}) fusion(f32[40,128,512]{2,1,0:T(8,128)} %fusion.42, f32[40,128,512]{2,1,0:T(8,128)S(1)} %bitcast.65, f32[40,128]{1,0:T(8,128)S(1)} %fusion.54, ...), kind=kLoop, calls=%fused_computation.68 | loop fusion | flops 57664512 | bytes 36777984 | tf_op jit(solution)/shard_map/reduce_sum | solution.py:60
  191.0 12.0 %fusion.16 = bf16[40,128,512]{2,1,0:T(8,128)(2,1)S(1)} fusion(f32[40,128,512]{2,1,0:T(8,128)} %get-tuple-element.45, bf16[40,128,512]{2,1,0:T(8,128)(2,1)S(1)} %bitcast.67, f32[40,128,512]{2,1,0:T(8,128)} %get-tuple-element.32, f32[40,128]{1,0:T(8,128)S(1)} %broadcast_multiply_fusion, f32[40,128]{1,0:T(8,128)S(1)} %get-tuple-element.35, ...), kind=kLoop, calls=%fused_computation.41 | loop fusion | flops 73400320 | bytes 31623168 | tf_op jit(solution)/shard_map/convert_element_type | solution.py:49
  203.0 6.4 %convolution_bitcast_fusion.1 = f32[1,512,512]{2,1,0:T(8,128)} fusion(bf16[40,128,512]{2,1,0:T(8,128)(2,1)} %copy-done.6, bf16[40,128,512]{2,1,0:T(8,128)(2,1)S(1)} %fusion.16), kind=kOutput, calls=%fused_computation.79 | convolution fusion | flops 2684354560 | bytes 11534336 | tf_op jit(solution)/shard_map/dot_general | solution.py:52
  209.4 5.5 %fusion.46 = f32[40,128,512]{2,1,0:T(8,128)} fusion(bf16[40,128,512]{2,1,0:T(8,128)(2,1)S(1)} %fusion.16, bf16[2,512,512]{2,1,0:T(8,128)(2,1)S(1)} %copy-done.11), kind=kOutput, calls=%fused_computation.88 | convolution fusion | flops 2684354560 | bytes 16252928 | tf_op jit(solution)/shard_map/dot_general | solution.py:55
  216.0 27.2 %fusion.41 = (f32[512]{0:T(512)S(1)}, f32[512]{0:T(512)S(1)}, f32[512]{0:T(512)S(1)}, f32[512]{0:T(512)S(1)}) fusion(f32[40,128,512]{2,1,0:T(8,128)} %fusion.46, f32[512]{0:T(512)S(1)} %bitcast.90, f32[512]{0:T(512)S(1)} %bitcast.92, f32[40,128]{1,0:T(8,128)S(1)} %fusion.54, f32[40,128]{1,0:T(8,128)S(1)} %add_rsqrt_fusion.1, f32[512]{0:T(512)S(1)} %bitcast.94, ...), kind=kLoop, calls=%fused_computation.75 | loop fusion | flops 52426752 | bytes 26271744 | tf_op jit(solution)/shard_map/reduce_sum | solution.py:70
  243.3 66.4 %all-reduce.8 = (f32[1,3,512]{2,1,0:T(4,128)S(1)}, f32[1,3,512]{2,1,0:T(4,128)S(1)}, f32[1,512]{1,0:T(1,128)S(1)}, f32[1,512]{1,0:T(1,128)S(1)}) all-reduce(f32[1,3,512]{2,1,0:T(4,128)S(1)} %get-tuple-element.52, f32[1,3,512]{2,1,0:T(4,128)S(1)} %get-tuple-element.51, ...), channel_id=1, replica_groups=mesh['neg'=16,'rep'=8] {'neg','rep'}, use_global_device_ids=true, to_apply=%region_17.18 | all-reduce | flops 4096 | bytes 32768 | tf_op jit(solution)/shard_map/psum | solution.py:187
  311.0 58.6 %all-reduce.12.cloned.1.call-done = (f32[1,512,512]{2,1,0:T(8,128)}, f32[1,512,512]{2,1,0:T(8,128)}, f32[512,256]{1,0:T(8,128)}) async-done(((f32[1,512,512]{2,1,0:T(8,128)}, f32[1,512,512]{2,1,0:T(8,128)}, f32[512,256]{1,0:T(8,128)}), (f32[1,512,512]{2,1,0:T(8,128)}, f32[1,512,512]{2,1,0:T(8,128)}, f32[512,256]{1,0:T(8,128)})) %all-reduce.12.cloned.1.call-update) | async-done | bytes 2621456 | tf_op jit(solution)/shard_map/psum | solution.py:187
  369.6 3.0 pad_maximum_fusion.1
  372.6 1.9 copy.24
  (73 shorter events, 8.6 us)
Async XLA Ops:
  7.2 45.9 %copy-start = (bf16[512,256]{1,0:T(8,128)(2,1)S(1)}, bf16[512,256]{1,0:T(8,128)(2,1)}, u32[]{:S(2)}) copy-start(bf16[512,256]{1,0:T(8,128)(2,1)} %param.17) | copy-start | bytes 786436
  7.2 144.3 %reduce-scatter.2.cloned.1.call-start = ((), (), s32[]{:S(2)}) async-start(), calls=%async_computation.1 | async-start | bytes 557056 | tf_op jit(solution)/shard_map/reduce_scatter | solution.py:153
  17.1 5.3 %copy-start.2 = (f32[40,128,512]{2,1,0:T(8,128)}, f32[40,128,512]{2,1,0:T(8,128)S(1)}, u32[]{:S(2)}) copy-start(f32[40,128,512]{2,1,0:T(8,128)S(1)} %fusion.26) | copy-start | bytes 31457284
  17.1 9.1 %copy-start.5 = (bf16[1,32,128,512]{3,2,1,0:T(8,128)(2,1)S(1)}, bf16[1,32,128,512]{3,2,1,0:T(8,128)(2,1)}, u32[]{:S(2)}) copy-start(bf16[1,32,128,512]{3,2,1,0:T(8,128)(2,1)} %param.10) | copy-start | bytes 12582916
  17.1 9.1 %copy-start.8 = (bf16[1,8,128,512]{3,2,1,0:T(8,128)(2,1)S(1)}, bf16[1,8,128,512]{3,2,1,0:T(8,128)(2,1)}, u32[]{:S(2)}) copy-start(bf16[1,8,128,512]{3,2,1,0:T(8,128)(2,1)} %param.9) | copy-start | bytes 3145732
  17.1 9.1 %copy-start.9 = (bf16[2,512,512]{2,1,0:T(8,128)(2,1)S(1)}, bf16[2,512,512]{2,1,0:T(8,128)(2,1)}, u32[]{:S(2)}) copy-start(bf16[2,512,512]{2,1,0:T(8,128)(2,1)} %param.16) | copy-start | bytes 3145732
  26.2 8.3 %copy-start.6 = (bf16[40,128,512]{2,1,0:T(8,128)(2,1)}, bf16[40,128,512]{2,1,0:T(8,128)(2,1)S(1)}, u32[]{:S(2)}) copy-start(bf16[40,128,512]{2,1,0:T(8,128)(2,1)S(1)} %add_convert_fusion.1) | copy-start | bytes 15728644
  34.6 10.1 %copy-start.4 = (bf16[40,128,512]{2,1,0:T(8,128)(2,1)}, bf16[40,128,512]{2,1,0:T(8,128)(2,1)S(1)}, u32[]{:S(2)}) copy-start(bf16[40,128,512]{2,1,0:T(8,128)(2,1)S(1)} %get-tuple-element.34) | copy-start | bytes 15728644
  36.3 4.0 %copy-start.3 = (f32[40,128,512]{2,1,0:T(8,128)}, f32[40,128,512]{2,1,0:T(8,128)S(1)}, u32[]{:S(2)}) copy-start(f32[40,128,512]{2,1,0:T(8,128)S(1)} %fusion.35) | copy-start | bytes 31457284
  44.7 8.3 %copy-start.7 = (bf16[40,128,512]{2,1,0:T(8,128)(2,1)}, bf16[40,128,512]{2,1,0:T(8,128)(2,1)S(1)}, u32[]{:S(2)}) copy-start(bf16[40,128,512]{2,1,0:T(8,128)(2,1)S(1)} %add_convert_fusion) | copy-start | bytes 15728644
  44.7 8.3 %copy-start.12 = (s32[1,32,128]{2,1,0:T(8,128)S(1)}, s32[1,32,128]{2,1,0:T(8,128)}, u32[]{:S(2)}) copy-start(s32[1,32,128]{2,1,0:T(8,128)} %param.12) | copy-start | bytes 49156
  44.7 8.3 %copy-start.14 = (s32[1,8,128]{2,1,0:T(8,128)S(1)}, s32[1,8,128]{2,1,0:T(8,128)}, u32[]{:S(2)}) copy-start(s32[1,8,128]{2,1,0:T(8,128)} %param.11) | copy-start | bytes 12292
  44.7 29.6 %copy-start.15 = (s32[1,128]{1,0:T(1,128)S(1)}, s32[1,128]{1,0:T(1,128)}, u32[]{:S(2)}) copy-start(s32[1,128]{1,0:T(1,128)} %param.13) | copy-start | bytes 1540
  53.0 109.8 %slice-start.5 = ((s8[5242880]{0:T(1024)(128)(4,1)}), s8[1048576]{0:T(1024)(128)(4,1)S(1)}, s32[]{:S(2)}) async-start(s8[5242880]{0:T(1024)(128)(4,1)} %bitcast.72), calls=%async_computation.8 | async-start | bytes 2097152
  75.9 293.6 %all-reduce.12.cloned.1.call-start = ((), (), s32[]{:S(2)}) async-start(), calls=%async_computation.2 | async-start | bytes 5242880 | tf_op jit(solution)/shard_map/psum | solution.py:187
  153.4 9.4 %slice-start.6 = ((s8[5242880]{0:T(1024)(128)(4,1)}), s8[4194304]{0:T(1024)(128)(4,1)S(1)}, s32[]{:S(2)}) async-start(s8[5242880]{0:T(1024)(128)(4,1)} %bitcast.72), calls=%async_computation.9 | async-start | bytes 8388608
  162.8 9.3 %slice-start = ((s8[10485760]{0:T(1024)(128)(4,1)}), s8[4194304]{0:T(1024)(128)(4,1)S(1)}, s32[]{:S(2)}) async-start(s8[10485760]{0:T(1024)(128)(4,1)} %bitcast.64), calls=%async_computation.3 | async-start | bytes 8388608
  162.8 9.3 %slice-start.1 = ((s8[10485760]{0:T(1024)(128)(4,1)}), s8[4194304]{0:T(1024)(128)(4,1)S(1)}, s32[]{:S(2)}) async-start(s8[10485760]{0:T(1024)(128)(4,1)} %bitcast.64), calls=%async_computation.4 | async-start | bytes 8388608
  162.8 9.3 %slice-start.3 = ((s8[5242880]{0:T(1024)(128)(4,1)}), s8[4194304]{0:T(1024)(128)(4,1)S(1)}, s32[]{:S(2)}) async-start(s8[5242880]{0:T(1024)(128)(4,1)} %bitcast.66), calls=%async_computation.6 | async-start | bytes 8388608
  166.7 5.4 %slice-start.2 = ((s8[10485760]{0:T(1024)(128)(4,1)}), s8[2097152]{0:T(1024)(128)(4,1)S(1)}, s32[]{:S(2)}) async-start(s8[10485760]{0:T(1024)(128)(4,1)} %bitcast.64), calls=%async_computation.5 | async-start | bytes 4194304
  166.7 5.4 %slice-start.4 = ((s8[5242880]{0:T(1024)(128)(4,1)}), s8[1048576]{0:T(1024)(128)(4,1)S(1)}, s32[]{:S(2)}) async-start(s8[5242880]{0:T(1024)(128)(4,1)} %bitcast.66), calls=%async_computation.7 | async-start | bytes 2097152
  203.0 6.5 %copy-start.11 = (bf16[2,512,512]{2,1,0:T(8,128)(2,1)S(1)}, bf16[2,512,512]{2,1,0:T(8,128)(2,1)}, u32[]{:S(2)}) copy-start(bf16[2,512,512]{2,1,0:T(8,128)(2,1)} %param.16) | copy-start | bytes 3145732
  209.4 5.5 %copy-start.13 = (f32[32,256]{1,0:T(8,128)S(1)}, f32[32,256]{1,0:T(8,128)}, u32[]{:S(2)}) copy-start(f32[32,256]{1,0:T(8,128)} %reduce-scatter.2.cloned.1.call-done) | copy-start | bytes 98308
  216.0 158.4 %copy-start.1 = (bf16[512,256]{1,0:T(8,128)(2,1)S(1)}, bf16[512,256]{1,0:T(8,128)(2,1)}, u32[]{:S(2)}) copy-start(bf16[512,256]{1,0:T(8,128)(2,1)} %param.17) | copy-start | bytes 786436
  (1 other events, 3.9 us)
Sparse Core Ops, SparseCore 0:
  76.1 75.3 reduce-scatter.1
  216.1 153.3 all-reduce.11
where the time goes:
time: 382 us; the launch traced here: 381 us
  waiting for transfers between devices  133 us (35%)
  other arithmetic  91 us (24%)
  blocking collectives  87.3 us (23%)
  matrix products  41.7 us (11%)
  between operations  14.4 us (4%)
  local copies, waits for them, and re-layouts  13.4 us (4%)
    reduce_scatter x1, waiting for transfers between devices, local(): lax.psum_scatter(logit_scale * lax.dot_general(score_grad, goal_units, ((...  74.6 us
    psum x1, blocking collectives, local(): lax.psum((grad_head, upper_kernel, upper_gain, upper_weight, lower_kernel...  66.4 us
    psum x1, waiting for transfers between devices, local(): lax.psum((grad_head, upper_kernel, upper_gain, upper_weight, lower_kernel...  58.6 us
    reduce_sum x1, other arithmetic, conv_block_backward(): grad_gain = jnp.sum(normed_grad * widened * inverse, axis=(0, 1))  27.2 us
    convert_element_type x2, other arithmetic, conv_block_backward(): act_grad = gelu_back(upstream)[0].astype(jnp.bfloat16)  21.4 us
    all_gather x1, blocking collectives, local(): group_premises = lax.all_gather(premise_units, 'neg', axis=0, tiled=True)  20.8 us
    reduce_sum x1, other arithmetic, conv_block_backward(): jnp.sum(shift_down(normed, dilation) * conv_grad, axis=(0, 1))  18.8 us
    dot_general x2, matrix products, conv_block_forward(): jnp.dot(mixed.reshape(count * length, width), weight, preferred_element_t...  16.5 us
  transfers between devices with their start and end apart: 2, of which 2 were waited for; matrix products, arithmetic and copies ran while one was open for 8% of the time, Pallas kernels for 0%

commit v1 on v0

--- a/solution.py
+++ b/solution.py
@@ -7,7 +7,45 @@
 UPPER_DILATION = 8
 
 
+N_NEG = 16
+N_REP = 8
+LANES = 128
 logit_scale = 20.0
+
+
+def to_rows(matrix):
+    rows, columns = matrix.shape
+    tiles = matrix.reshape(rows // 8, 8, columns // LANES, LANES)
+    return tiles.transpose(0, 2, 1, 3).reshape(rows * columns // LANES, LANES)
+
+
+def from_rows(flat, shape):
+    rows, columns = shape
+    tiles = flat.reshape(rows // 8, columns // LANES, 8, LANES)
+    return tiles.transpose(0, 2, 1, 3).reshape(rows, columns)
+
+
+def reduce_everywhere(arrays):
+    devices = N_NEG * N_REP
+    flat = [to_rows(array.astype(jnp.bfloat16)) for array in arrays]
+    used = sum(piece.shape[0] for piece in flat)
+    slice_rows = -(-used // (devices * 8)) * 8
+    flat.append(jnp.zeros((devices * slice_rows - used, LANES), jnp.bfloat16))
+    packed = jnp.concatenate(flat, axis=0).reshape(devices, slice_rows, LANES)
+    axes = ("neg", "rep")
+    received = lax.all_to_all(packed, axes, 0, 0)
+    own = jnp.sum(received.astype(jnp.float32), axis=0).astype(jnp.bfloat16)
+    spread = lax.all_to_all(
+        jnp.broadcast_to(own[None], (devices, slice_rows, LANES)), axes, 0, 0
+    )
+    rows = spread.reshape(devices * slice_rows, LANES)
+    results, start = [], 0
+    for array in arrays:
+        count = array.size // LANES
+        piece = rows[start : start + count]
+        results.append(from_rows(piece, array.shape).astype(jnp.float32))
+        start += count
+    return results
 
 
 def shift_down(values, dilation):
@@ -136,28 +174,31 @@
     premise_units = units[goal_count:]
     group_positive = positives[0]
     position = lax.axis_index("neg")
-    group_premises = lax.all_gather(premise_units, "neg", axis=0, tiled=True)
-    own_positive = lax.dynamic_slice_in_dim(group_positive, position * goal_count, goal_count)
+    gathered = lax.all_to_all(
+        jnp.broadcast_to(units[None], (N_NEG,) + units.shape), "neg", 0, 0
+    )
+    group_goals = gathered[:, :goal_count].reshape(N_NEG * goal_count, -1)
+    group_premises = gathered[:, goal_count:].reshape(-1, units.shape[1])
+    premise_count = units.shape[0] - goal_count
     scores = logit_scale * lax.dot_general(
-        goal_units, group_premises, (((1,), (1,)), ((), ())), preferred_element_type=jnp.float32
+        group_goals, group_premises, (((1,), (1,)), ((), ())), preferred_element_type=jnp.float32
     )
     expon = jnp.exp(scores)
     total = jnp.sum(expon, axis=1, keepdims=True)
     columns = jnp.arange(group_premises.shape[0], dtype=jnp.int32)
-    onehot = (columns[None, :] == own_positive[:, None]).astype(jnp.float32)
-    losses = jnp.log(total[:, 0]) - jnp.sum(scores * onehot, axis=1)
+    onehot = (columns[None, :] == group_positive[:, None]).astype(jnp.float32)
+    group_losses = jnp.log(total[:, 0]) - jnp.sum(scores * onehot, axis=1)
+    losses = lax.dynamic_slice_in_dim(group_losses, position * goal_count, goal_count)
     score_grad = ((expon / total - onehot) / goal_count).astype(jnp.bfloat16)
+    own_rows = lax.dynamic_slice_in_dim(score_grad, position * goal_count, goal_count, 0)
+    own_columns = lax.dynamic_slice_in_dim(
+        score_grad, position * premise_count, premise_count, 1
+    )
     goal_grad = logit_scale * jnp.dot(
-        score_grad, group_premises, preferred_element_type=jnp.float32
-    )
-    premise_grad = lax.psum_scatter(
-        logit_scale
-        * lax.dot_general(
-            score_grad, goal_units, (((0,), (0,)), ((), ())), preferred_element_type=jnp.float32
-        ),
-        "neg",
-        scatter_dimension=0,
-        tiled=True,
+        own_rows, group_premises, preferred_element_type=jnp.float32
+    )
+    premise_grad = logit_scale * lax.dot_general(
+        own_columns, group_goals, (((0,), (0,)), ((), ())), preferred_element_type=jnp.float32
     )
     unit_grad = jnp.concatenate([goal_grad, premise_grad], axis=0)
     hidden_gradient, grad_head = pool_backward(unit_grad, saved_pool, token_valid_mask, head_weight)
@@ -183,26 +224,24 @@
         LOWER_DILATION,
         False,
     )
-    grad_head, upper_kernel, upper_gain, upper_weight, lower_kernel, lower_gain, lower_weight = (
-        lax.psum(
-            (
-                grad_head,
-                upper_kernel,
-                upper_gain,
-                upper_weight,
-                lower_kernel,
-                lower_gain,
-                lower_weight,
+    sums = reduce_everywhere(
+        [
+            lower_weight,
+            upper_weight,
+            grad_head,
+            jnp.concatenate(
+                [lower_kernel, upper_kernel, lower_gain[None], upper_gain[None]], axis=0
             ),
-            ("neg", "rep"),
-        )
-    )
+        ]
+    )
+    weights = jnp.stack(sums[:2])
+    small = sums[3]
     return (
         losses[None, :],
-        jnp.stack([lower_kernel, upper_kernel]),
-        jnp.stack([lower_gain, upper_gain]),
-        jnp.stack([lower_weight, upper_weight]),
-        grad_head,
+        small[:6].reshape(2, 3, -1),
+        small[6:8],
+        weights,
+        sums[2],
     )
 
 

time: 382 us -> 214 us (0.56)
  waiting for transfers between devices: 133 us -> 32.2 us
  blocking collectives: 87.3 us -> 32.6 us
  between operations: 14.4 us -> 1.55 us
  starting transfers between devices: 0.26 us -> 13 us
  other arithmetic: 91 us -> 80.8 us
  matrix products: 41.7 us -> 37.2 us
    reduce_scatter x1 -> x0, waiting for transfers between devices: 74.6 us -> none  [local(): lax.psum_scatter(logit_scale * lax.dot_general(score_grad, goal_units, ((...]
    psum x1 -> x0, blocking collectives: 66.4 us -> none  [local(): lax.psum((grad_head, upper_kernel, upper_gain, upper_weight, lower_kernel...]
    psum x1 -> x0, waiting for transfers between devices: 58.6 us -> none  [local(): lax.psum((grad_head, upper_kernel, upper_gain, upper_weight, lower_kernel...]
    all_to_all x0 -> x1, blocking collectives: none -> 32.6 us  [reduce_everywhere(): received = lax.all_to_all(packed, axes, 0, 0)]
    all_to_all x0 -> x2, waiting for transfers between devices: none -> 32.2 us  [the longest x1 24.4 us: reduce_everywhere(): lax.all_to_all(jnp.broadcast_to(own[None], (devices, slice_rows, LANES)),...]
    all_gather x1 -> x0, blocking collectives: 20.8 us -> none  [local(): group_premises = lax.all_gather(premise_units, 'neg', axis=0, tiled=True)]
    all_to_all x0 -> x2, starting transfers between devices: none -> 13 us  [the longest x1 8.6 us: local(): lax.all_to_all(jnp.broadcast_to(units[None], (N_NEG,) + units.shape), 'ne...]
    reduce_sum x1, other arithmetic: 27.2 us -> 20.7 us  [conv_block_backward(): grad_gain = jnp.sum(normed_grad * widened * inverse, axis=(0, 1))]
  transfers between devices with their start and end apart: 2 -> 2, of which waited for: 2 -> 2; matrix products, arithmetic and copies ran while one was open for 8% -> 0% of each run, Pallas kernels for 0% -> 0%
where the time goes in v1:
time: 214 us; the launch traced here: 213 us
  other arithmetic  80.8 us (38%)
  matrix products  37.2 us (17%)
  blocking collectives  32.6 us (15%)
  waiting for transfers between devices  32.2 us (15%)
  local copies, waits for them, and re-layouts  15.2 us (7%)
  starting transfers between devices  13 us (6%)
    all_to_all x1, blocking collectives, reduce_everywhere(): received = lax.all_to_all(packed, axes, 0, 0)  32.6 us
    all_to_all x1, waiting for transfers between devices, reduce_everywhere(): lax.all_to_all(jnp.broadcast_to(own[None], (devices, slice_rows, LANES)),...  24.4 us
    convert_element_type x2, other arithmetic, conv_block_backward(): act_grad = gelu_back(upstream)[0].astype(jnp.bfloat16)  22.4 us
    reduce_sum x1, other arithmetic, conv_block_backward(): grad_gain = jnp.sum(normed_grad * widened * inverse, axis=(0, 1))  20.7 us
    dot_general x2, matrix products, conv_block_forward(): jnp.dot(mixed.reshape(count * length, width), weight, preferred_element_t...  16.6 us
    reduce_sum x1, other arithmetic, conv_block_backward(): jnp.sum(shift_up(normed, dilation) * conv_grad, axis=(0, 1))  15 us
    unnamed x110, local copies, waits for them, and re-layouts  10.2 us
    dot_general x2, matrix products, conv_block_backward(): jnp.dot(mixed.reshape(count * length, width).T, flat_grad, preferred_elem...  9.21 us
  transfers between devices with their start and end apart: 2, of which 2 were waited for; matrix products, arithmetic and copies ran while one was open for 0% of the time, Pallas kernels for 0%

profile of v1, /device:TPU:1, one launch (start us, length us, event | category | flops | bytes accessed | tf_op | source)
XLA Modules:
  0.0 212.6 jit_solution(18006311778629445365)
XLA Ops:
  2.3 3.6 %fusion.24 = f32[40,128]{1,0:T(8,128)S(1)} fusion(bf16[32,128,512]{2,1,0:T(8,128)(2,1)} %bitcast.126, bf16[8,128,512]{2,1,0:T(8,128)(2,1)} %bitcast.130), kind=kLoop, calls=%fused_computation.49 | loop fusion | flops 10480640 | bytes 5263360 | tf_op jit(solution)/shard_map/reduce_sum | solution.py:69
  6.6 4.0 %fusion.26 = f32[40,128,512]{2,1,0:T(8,128)S(1)} fusion(f32[40,128]{1,0:T(8,128)S(1)} %fusion.57, f32[512]{0:T(512)S(1)} %bitcast.166, f32[40,128]{1,0:T(8,128)S(1)} %add_rsqrt_fusion.1, bf16[32,128,512]{2,1,0:T(8,128)(2,1)} %bitcast.127, bf16[8,128,512]{2,1,0:T(8,128)(2,1)} %bitcast.131), kind=kLoop, calls=%fused_computation.51 | loop fusion | flops 13107200 | bytes 15771648 | tf_op jit(solution)/shard_map/mul | solution.py:70
  10.7 5.2 %copy-done.2 = f32[40,128,512]{2,1,0:T(8,128)} copy-done((f32[40,128,512]{2,1,0:T(8,128)}, f32[40,128,512]{2,1,0:T(8,128)S(1)}, u32[]{:S(2)}) %copy-start.2) | copy-done | bytes 10485784
  15.9 3.8 %add_convert_fusion.1 = bf16[40,128,512]{2,1,0:T(8,128)(2,1)S(1)} fusion(f32[40,128,512]{2,1,0:T(8,128)S(1)} %fusion.26, f32[512]{0:T(512)S(1)} %bitcast.154, f32[512]{0:T(512)S(1)} %bitcast.156, f32[512]{0:T(512)S(1)} %bitcast.158), kind=kLoop, calls=%fused_computation.74 | loop fusion | flops 15728640 | bytes 15734784 | tf_op jit(solution)/shard_map/convert_element_type | solution.py:71
  19.8 8.3 %fusion.33 = (f32[40,128]{1,0:T(8,128)S(1)}, bf16[40,128,512]{2,1,0:T(8,128)(2,1)S(1)}, f32[40,128,512]{2,1,0:T(8,128)}) fusion(bf16[32,128,512]{2,1,0:T(8,128)(2,1)S(1)} %bitcast.128, bf16[8,128,512]{2,1,0:T(8,128)(2,1)S(1)} %bitcast.132, bf16[40,128,512]{2,1,0:T(8,128)(2,1)S(1)} %add_convert_fusion.1, bf16[2,512,512]{2,1,0:T(8,128)(2,1)S(1)} %copy-done.11), kind=kOutput, calls=%fused_computation.58 | convolution fusion | flops 2723671040 | bytes 26759168 | tf_op jit(solution)/shard_map/dot_general | solution.py:73
  28.8 1.7 fusion.35
  30.5 3.9 %copy-done.3 = f32[40,128,512]{2,1,0:T(8,128)} copy-done((f32[40,128,512]{2,1,0:T(8,128)}, f32[40,128,512]{2,1,0:T(8,128)S(1)}, u32[]{:S(2)}) %copy-start.3) | copy-done | bytes 10485784
  34.4 4.4 %add_convert_fusion = bf16[40,128,512]{2,1,0:T(8,128)(2,1)S(1)} fusion(f32[40,128,512]{2,1,0:T(8,128)S(1)} %fusion.35, f32[512]{0:T(512)S(1)} %bitcast.162, f32[512]{0:T(512)S(1)} %bitcast.164, f32[512]{0:T(512)S(1)} %bitcast.160), kind=kLoop, calls=%fused_computation.73 | loop fusion | flops 15728640 | bytes 15734784 | tf_op jit(solution)/shard_map/convert_element_type | solution.py:71
  38.9 8.2 %multiply_reduce_fusion.6 = (f32[40,512]{1,0:T(8,128)S(1)}, f32[40,128,512]{2,1,0:T(8,128)}) fusion(f32[40,128]{1,0:T(8,128)S(1)} %fusion.57, bf16[40,128,512]{2,1,0:T(8,128)(2,1)S(1)} %get-tuple-element.32, bf16[40,128,512]{2,1,0:T(8,128)(2,1)S(1)} %add_convert_fusion, bf16[2,512,512]{2,1,0:T(8,128)(2,1)S(1)} %copy-done.11), kind=kOutput, calls=%fused_computation.72 | convolution fusion | flops 2721034240 | bytes 21598208 | tf_op jit(solution)/shard_map/dot_general | solution.py:73
  48.4 8.6 %all-to-all-start = ((bf16[16,40,256]{2,1,0:T(8,128)(2,1)}), bf16[16,40,256]{2,1,0:T(8,128)(2,1)S(1)}, u32[]{:S(2)}, u32[]{:S(2)}) async-start(bf16[16,40,256]{2,1,0:T(8,128)(2,1)} %broadcast_in_dim.8), calls=%async_computation | async-start | bytes 655360 | tf_op jit(solution)/shard_map/all_to_all | solution.py:177
  57.0 7.8 %all-to-all-done = bf16[16,40,256]{2,1,0:T(8,128)(2,1)S(1)} async-done(((bf16[16,40,256]{2,1,0:T(8,128)(2,1)}), bf16[16,40,256]{2,1,0:T(8,128)(2,1)S(1)}, u32[]{:S(2)}, u32[]{:S(2)}) %all-to-all-start) | async-done | bytes 327712 | tf_op jit(solution)/shard_map/all_to_all | solution.py:177
  67.7 9.4 %fusion.23 = bf16[40,128,512]{2,1,0:T(8,128)(2,1)S(1)} fusion(f32[40,128,512]{2,1,0:T(8,128)} %get-tuple-element.47, f32[40,512]{1,0:T(8,128)S(1)} %convolution_divide_fusion, f32[40,128]{1,0:T(8,128)S(1)} %fusion.57), kind=kLoop, calls=%fused_computation.48 | loop fusion | flops 55050240 | bytes 15831040 | tf_op jit(solution)/shard_map/convert_element_type | solution.py:87
  77.2 3.7 %fusion.43 = bf16[512,512]{1,0:T(8,128)(2,1)} fusion(bf16[40,128,512]{2,1,0:T(8,128)(2,1)S(1)} %bitcast.138, bf16[40,128,512]{2,1,0:T(8,128)(2,1)S(1)} %fusion.23), kind=kOutput, calls=%fused_computation.80 | convolution fusion | flops 2684616704 | bytes 11010048 | tf_op jit(solution)/shard_map/dot_general | solution.py:90
  80.9 2.9 %fusion.44 = f32[40,128,512]{2,1,0:T(8,128)S(1)} fusion(bf16[40,128,512]{2,1,0:T(8,128)(2,1)S(1)} %fusion.23, bf16[2,512,512]{2,1,0:T(8,128)(2,1)S(1)} %copy-done.12), kind=kOutput, calls=%fused_computation.88 | convolution fusion | flops 2684354560 | bytes 16252928 | tf_op jit(solution)/shard_map/dot_general | solution.py:93
  83.8 15.0 %multiply_reduce_fusion = (bf16[512]{0:T(512)(128)(2,1)}, bf16[512]{0:T(512)(128)(2,1)}, bf16[512]{0:T(512)(128)(2,1)}, f32[40,128]{1,0:T(8,128)}, bf16[512]{0:T(512)(128)(2,1)}, /*index=5*/f32[40,128,512]{2,1,0:T(8,128)}) fusion(f32[40,128,512]{2,1,0:T(8,128)S(1)} %fusion.44, f32[40,128,512]{2,1,0:T(8,128)S(1)} %bitcast.125, f32[40,128]{1,0:T(8,128)S(1)} %fusion.57, ...), kind=kLoop, calls=%fused_computation.66 | loop fusion | flops 57664512 | bytes 36773888 | tf_op jit(solution)/shard_map/reduce_sum | solution.py:100
  99.6 13.0 %fusion.16 = bf16[40,128,512]{2,1,0:T(8,128)(2,1)S(1)} fusion(f32[40,128,512]{2,1,0:T(8,128)} %get-tuple-element.45, bf16[40,128,512]{2,1,0:T(8,128)(2,1)} %copy-done.4, f32[40,128,512]{2,1,0:T(8,128)} %get-tuple-element.30, f32[40,128]{1,0:T(8,128)S(1)} %broadcast_multiply_fusion, f32[40,128]{1,0:T(8,128)} %get-tuple-element.35, f32[40,512]{1,0:T(8,128)} %copy-done.15, ...), kind=kLoop, calls=%fused_computation.41 | loop fusion | flops 73400320 | bytes 31623168 | tf_op jit(solution)/shard_map/convert_element_type | solution.py:87
  112.6 5.5 %fusion.42 = bf16[512,512]{1,0:T(8,128)(2,1)S(1)} fusion(bf16[40,128,512]{2,1,0:T(8,128)(2,1)} %copy-done.9, bf16[40,128,512]{2,1,0:T(8,128)(2,1)S(1)} %fusion.16), kind=kOutput, calls=%fused_computation.79 | convolution fusion | flops 2684616704 | bytes 11010048 | tf_op jit(solution)/shard_map/dot_general | solution.py:90
  118.3 5.7 %fusion.48 = f32[40,128,512]{2,1,0:T(8,128)} fusion(bf16[40,128,512]{2,1,0:T(8,128)(2,1)S(1)} %fusion.16, bf16[2,512,512]{2,1,0:T(8,128)(2,1)S(1)} %copy-done.13), kind=kOutput, calls=%fused_computation.92 | convolution fusion | flops 2684354560 | bytes 16252928 | tf_op jit(solution)/shard_map/dot_general | solution.py:93
  124.2 20.7 %fusion.41 = (bf16[512]{0:T(512)(128)(2,1)S(1)}, bf16[512]{0:T(512)(128)(2,1)S(1)}, bf16[512]{0:T(512)(128)(2,1)S(1)}, bf16[512]{0:T(512)(128)(2,1)S(1)}) fusion(f32[40,128,512]{2,1,0:T(8,128)} %fusion.48, f32[512]{0:T(512)S(1)} %bitcast.155, f32[512]{0:T(512)S(1)} %bitcast.157, f32[40,128]{1,0:T(8,128)S(1)} %fusion.57, f32[40,128]{1,0:T(8,128)S(1)} %copy-done.18, ...), kind=kLoop, calls=%fused_computation.75 | loop fusion | flops 57669632 | bytes 26267648 | tf_op jit(solution)/shard_map/reduce_sum | solution.py:108
  145.3 32.6 %all_to_all.15 = bf16[128,48,128]{2,1,0:T(8,128)(2,1)S(1)} all-to-all(bf16[128,48,128]{2,1,0:T(8,128)(2,1)S(1)} %bitcast.139), channel_id=1, replica_groups=mesh['neg'=16,'rep'=8] {'neg','rep'}, dimensions={0} | all-to-all | bytes 3145728 | tf_op jit(solution)/shard_map/all_to_all | solution.py:36
  178.2 1.3 broadcast_in_dim.11
  179.6 4.3 %all-to-all-start.2 = ((bf16[128,48,128]{2,1,0:T(8,128)(2,1)}), bf16[128,48,128]{2,1,0:T(8,128)(2,1)S(1)}, u32[]{:S(2)}, u32[]{:S(2)}) async-start(bf16[128,48,128]{2,1,0:T(8,128)(2,1)} %broadcast_in_dim.11), calls=%async_computation.2 | async-start | bytes 3145728 | tf_op jit(solution)/shard_map/all_to_all | solution.py:38
  184.6 24.4 %all-to-all-done.2 = bf16[128,48,128]{2,1,0:T(8,128)(2,1)S(1)} async-done(((bf16[128,48,128]{2,1,0:T(8,128)(2,1)}), bf16[128,48,128]{2,1,0:T(8,128)(2,1)S(1)}, u32[]{:S(2)}, u32[]{:S(2)}) %all-to-all-start.2) | async-done | bytes 1572896 | tf_op jit(solution)/shard_map/all_to_all | solution.py:38
  211.2 1.5 maximum_convert_fusion
  (142 shorter events, 11.3 us)
Async XLA Ops:
  0.6 46.6 %copy-start = (bf16[512,256]{1,0:T(8,128)(2,1)S(1)}, bf16[512,256]{1,0:T(8,128)(2,1)}, u32[]{:S(2)}) copy-start(bf16[512,256]{1,0:T(8,128)(2,1)} %param.17) | copy-start | bytes 786436
  1.4 27.3 %copy-start.20 = (f32[1,512]{1,0:T(1,128)}, f32[1,512]{1,0:T(1,128)S(1)}, u32[]{:S(2)}) copy-start(f32[1,512]{1,0:T(1,128)S(1)} %get-tuple-element.43) | copy-start | bytes 6148
  2.2 28.2 %copy-start.27 = (f32[1,1,512]{2,0,1:T(1,128)}, f32[1,1,512]{2,0,1:T(1,128)S(1)}, u32[]{:S(2)}) copy-start(f32[1,1,512]{2,0,1:T(1,128)S(1)} %get-tuple-element.37) | copy-start | bytes 6148
  2.3 28.2 %copy-start.28 = (f32[1,1,512]{2,0,1:T(1,128)}, f32[1,1,512]{2,0,1:T(1,128)S(1)}, u32[]{:S(2)}) copy-start(f32[1,1,512]{2,0,1:T(1,128)S(1)} %get-tuple-element.41) | copy-start | bytes 6148
  2.3 28.2 %copy-start.29 = (f32[1,1,512]{2,0,1:T(1,128)}, f32[1,1,512]{2,0,1:T(1,128)S(1)}, u32[]{:S(2)}) copy-start(f32[1,1,512]{2,0,1:T(1,128)S(1)} %get-tuple-element.42) | copy-start | bytes 6148
  5.9 13.8 %copy-start.17 = (f32[40,128]{1,0:T(8,128)}, f32[40,128]{1,0:T(8,128)S(1)}, u32[]{:S(2)}) copy-start(f32[40,128]{1,0:T(8,128)S(1)} %add_rsqrt_fusion.1) | copy-start | bytes 61444
  28.1 19.1 %copy-start.4 = (bf16[40,128,512]{2,1,0:T(8,128)(2,1)}, bf16[40,128,512]{2,1,0:T(8,128)(2,1)S(1)}, u32[]{:S(2)}) copy-start(bf16[40,128,512]{2,1,0:T(8,128)(2,1)S(1)} %get-tuple-element.32) | copy-start | bytes 15728644
  38.9 26.0 %copy-start.37 = (s32[1,128]{1,0:T(1,128)S(1)}, s32[1,128]{1,0:T(1,128)}, u32[]{:S(2)}) copy-start(s32[1,128]{1,0:T(1,128)} %param.13) | copy-start | bytes 1540
  47.3 29.9 %slice-start.6 = ((s8[5242880]{0:T(1024)(128)(4,1)}), s8[1048576]{0:T(1024)(128)(4,1)S(1)}, s32[]{:S(2)}) async-start(s8[5242880]{0:T(1024)(128)(4,1)} %bitcast.137), calls=%async_computation.9 | async-start | bytes 2097152
  48.4 16.4 %all-to-all-start = ((bf16[16,40,256]{2,1,0:T(8,128)(2,1)}), bf16[16,40,256]{2,1,0:T(8,128)(2,1)S(1)}, u32[]{:S(2)}, u32[]{:S(2)}) async-start(bf16[16,40,256]{2,1,0:T(8,128)(2,1)} %broadcast_in_dim.8), calls=%async_computation | async-start | bytes 655360 | tf_op jit(solution)/shard_map/all_to_all | solution.py:177
  65.7 11.4 %copy-start.38 = (f32[128]{0:T(128)}, f32[128]{0:T(128)S(1)}, u32[]{:S(2)}) copy-start(f32[128]{0:T(128)S(1)} %get-tuple-element.28) | copy-start | bytes 1540
  66.7 10.4 %copy-start.15 = (f32[40,512]{1,0:T(8,128)}, f32[40,512]{1,0:T(8,128)S(1)}, u32[]{:S(2)}) copy-start(f32[40,512]{1,0:T(8,128)S(1)} %convolution_divide_fusion) | copy-start | bytes 245764
  112.6 11.4 %slice-start = ((s8[10485760]{0:T(1024)(128)(4,1)}), s8[4194304]{0:T(1024)(128)(4,1)S(1)}, s32[]{:S(2)}) async-start(s8[10485760]{0:T(1024)(128)(4,1)} %bitcast.122), calls=%async_computation.3 | async-start | bytes 8388608
  112.6 11.4 %slice-start.1 = ((s8[10485760]{0:T(1024)(128)(4,1)}), s8[4194304]{0:T(1024)(128)(4,1)S(1)}, s32[]{:S(2)}) async-start(s8[10485760]{0:T(1024)(128)(4,1)} %bitcast.122), calls=%async_computation.4 | async-start | bytes 8388608
  124.1 20.9 %copy-start.14 = (bf16[512,512]{1,0:T(8,128)(2,1)S(1)}, bf16[512,512]{1,0:T(8,128)(2,1)}, u32[]{:S(2)}) copy-start(bf16[512,512]{1,0:T(8,128)(2,1)} %fusion.43) | copy-start | bytes 1572868
  124.2 20.9 %copy-start.16 = (bf16[512,256]{1,0:T(8,128)(2,1)S(1)}, bf16[512,256]{1,0:T(8,128)(2,1)}, u32[]{:S(2)}) copy-start(bf16[512,256]{1,0:T(8,128)(2,1)} %convolution_convert_fusion) | copy-start | bytes 786436
  124.2 21.0 %copy-start.36 = (bf16[512]{0:T(512)(128)(2,1)S(1)}, bf16[512]{0:T(512)(128)(2,1)}, u32[]{:S(2)}) copy-start(bf16[512]{0:T(512)(128)(2,1)} %get-tuple-element.16) | copy-start | bytes 3076
  124.2 21.0 %copy-start.35 = (bf16[512]{0:T(512)(128)(2,1)S(1)}, bf16[512]{0:T(512)(128)(2,1)}, u32[]{:S(2)}) copy-start(bf16[512]{0:T(512)(128)(2,1)} %get-tuple-element.25) | copy-start | bytes 3076
  124.2 21.0 %copy-start.34 = (bf16[512]{0:T(512)(128)(2,1)S(1)}, bf16[512]{0:T(512)(128)(2,1)}, u32[]{:S(2)}) copy-start(bf16[512]{0:T(512)(128)(2,1)} %get-tuple-element.15) | copy-start | bytes 3076
  124.2 21.1 %copy-start.33 = (bf16[512]{0:T(512)(128)(2,1)S(1)}, bf16[512]{0:T(512)(128)(2,1)}, u32[]{:S(2)}) copy-start(bf16[512]{0:T(512)(128)(2,1)} %get-tuple-element.27) | copy-start | bytes 3076
  124.2 88.4 %copy-start.1 = (bf16[512,256]{1,0:T(8,128)(2,1)S(1)}, bf16[512,256]{1,0:T(8,128)(2,1)}, u32[]{:S(2)}) copy-start(bf16[512,256]{1,0:T(8,128)(2,1)} %param.17) | copy-start | bytes 786436
  145.0 39.0 %copy-start.39 = (f32[128]{0:T(128)S(1)}, f32[128]{0:T(128)}, u32[]{:S(2)}) copy-start(f32[128]{0:T(128)} %copy-done.38) | copy-start | bytes 1540
  145.0 39.0 %copy-start.40 = (f32[128]{0:T(128)S(1)}, f32[128]{0:T(128)}, u32[]{:S(2)}) copy-start(f32[128]{0:T(128)} %get-tuple-element.29) | copy-start | bytes 1540
  179.6 29.4 %all-to-all-start.2 = ((bf16[128,48,128]{2,1,0:T(8,128)(2,1)}), bf16[128,48,128]{2,1,0:T(8,128)(2,1)S(1)}, u32[]{:S(2)}, u32[]{:S(2)}) async-start(bf16[128,48,128]{2,1,0:T(8,128)(2,1)} %broadcast_in_dim.11), calls=%async_computation.2 | async-start | bytes 3145728 | tf_op jit(solution)/shard_map/all_to_all | solution.py:38
  (27 other events, 186.2 us)

commit v2 on v1

v2 whole, which is shorter than its diff:
```python
import functools

import jax
import jax.numpy as jnp
from jax import lax
from jax.experimental import pallas as pl
from jax.experimental.pallas import tpu as pltpu
from jax.sharding import PartitionSpec as P

LOWER_DILATION = 4
UPPER_DILATION = 8
N_NEG = 16
N_REP = 8
LANES = 128
PAD = 8
TILE = 16
SEQS = 4
EPS = 1e-06
GELU_C = 0.7978845608028654
GELU_A = 0.044715
logit_scale = 20.0
F32 = jnp.float32
BF16 = jnp.bfloat16


def gelu_parts(x):
    square = x * x
    half = 0.5 + 0.5 * jnp.tanh(x * (GELU_C + (GELU_C * GELU_A) * square))
    value = x * half
    slope = half + value * (1.0 - half) * (
        2.0 * GELU_C + (6.0 * GELU_C * GELU_A) * square
    )
    return value, slope


def forward_kernel(
    lengths,
    goal_ref,
    premise_ref,
    mix_gain_ref,
    weight_ref,
    head_ref,
    shifted_ref,
    slope_low_ref,
    normed_up_ref,
    mixed_up_ref,
    slope_up_ref,
    inverse_ref,
    pooled_ref,
    unit_ref,
    magnitude_ref,
    spread_ref,
    states,
    padded,
    mixed,
    pre_act,
    hidden,
):
    step = pl.program_id(0)
    length, width = states.shape[1], states.shape[2]
    tiles = range(0, length, TILE)
    rows = lax.broadcasted_iota(jnp.int32, (TILE, 1), 0)

    @pl.when(step == 0)
    def _():
        zeros = jnp.zeros((SEQS, PAD, width), F32)
        padded[:, :PAD, :] = zeros
        padded[:, PAD + length :, :] = zeros

    def norm(values, valid):
        mean = jnp.mean(values * values, axis=-1, keepdims=True)
        inverse = jnp.where(valid, lax.rsqrt(mean + EPS), 0.0)
        return values * inverse, inverse

    def norm_inputs(source):
        def body(seq, carry):
            count = lengths[step * SEQS + seq]
            for start in tiles:
                raw = source[0, seq, pl.ds(start, TILE), :]
                states[seq, pl.ds(start, TILE), :] = raw
                normed, _ = norm(raw.astype(F32), rows < count - start)
                padded[seq, pl.ds(PAD + start, TILE), :] = normed
            return carry

        lax.fori_loop(0, SEQS, body, 0)

    goal_steps = goal_total // SEQS

    @pl.when(step < goal_steps)
    def _():
        norm_inputs(goal_ref)

    @pl.when(step >= goal_steps)
    def _():
        norm_inputs(premise_ref)

    def mix_low(seq, carry):
        for start in tiles:
            window = [
                padded[seq, pl.ds(PAD + start + tap * LOWER_DILATION, TILE), :]
                for tap in (-1, 0, 1)
            ]
            total = 0.0
            for tap in range(3):
                total = total + mix_gain_ref[0, tap : tap + 1, :] * window[tap]
                shifted_ref[seq, pl.ds(start, TILE), tap * width : (tap + 1) * width] = (
                    window[tap].astype(BF16)
                )
            mixed[seq, pl.ds(start, TILE), :] = total.astype(BF16)
        return carry

    lax.fori_loop(0, SEQS, mix_low, 0)
    pre_act[...] = jnp.dot(
        mixed[...].reshape(SEQS * length, width), weight_ref[0], preferred_element_type=F32
    ).reshape(SEQS, length, width)

    def act_low(seq, carry):
        count = lengths[step * SEQS + seq]
        for start in tiles:
            at = pl.ds(start, TILE)
            value, slope = gelu_parts(pre_act[seq, at, :])
            slope_low_ref[seq, at, :] = slope.astype(BF16)
            out = states[seq, at, :].astype(F32) + value
            hidden[seq, at, :] = out
            normed, inverse = norm(out, rows < count - start)
            padded[seq, pl.ds(PAD + start, TILE), :] = normed
            normed_up_ref[seq, at, :] = normed.astype(BF16)
            inverse_ref[seq, at, :] = jnp.broadcast_to(inverse, (TILE, LANES))
        return carry

    lax.fori_loop(0, SEQS, act_low, 0)

    def mix_up(seq, carry):
        for start in tiles:
            at = pl.ds(start, TILE)
            total = 0.0
            for tap in range(3):
                total = total + mix_gain_ref[1, tap : tap + 1, :] * (
                    padded[seq, pl.ds(PAD + start + (tap - 1) * UPPER_DILATION, TILE), :]
                )
            mixed_up_ref[seq, at, :] = total.astype(BF16)
        return carry

    lax.fori_loop(0, SEQS, mix_up, 0)
    pre_act[...] = jnp.dot(
        mixed_up_ref[...].reshape(SEQS * length, width),
        weight_ref[1],
        preferred_element_type=F32,
    ).reshape(SEQS, length, width)

    def act_up(seq, carry):
        count = lengths[step * SEQS + seq]
        pooled = jnp.zeros((TILE, width), F32)
        for start in tiles:
            at = pl.ds(start, TILE)
            valid = rows < count - start
            value, slope = gelu_parts(pre_act[seq, at, :])
            slope_up_ref[seq, at, :] = jnp.where(valid, slope, 0.0).astype(BF16)
            pooled = pooled + jnp.where(valid, hidden[seq, at, :] + value, 0.0)
        pooled_ref[pl.ds(step * SEQS + seq, 1), :] = (
            jnp.sum(pooled, axis=0, keepdims=True) / count.astype(F32)
        )
        return carry

    lax.fori_loop(0, SEQS, act_up, 0)

    @pl.when(step == pl.num_programs(0) - 1)
    def _():
        embedded = jnp.dot(
            pooled_ref[...].astype(BF16), head_ref[...], preferred_element_type=F32
        )
        magnitude = jnp.sqrt(jnp.sum(embedded * embedded, axis=-1, keepdims=True) + EPS)
        unit = embedded / magnitude
        unit_ref[...] = unit
        magnitude_ref[...] = jnp.broadcast_to(magnitude, magnitude_ref.shape)
        rounded = unit.astype(BF16)
        for peer in range(N_NEG):
            spread_ref[peer] = rounded


def backward_kernel(
    lengths,
    gathered_ref,
    own_unit_ref,
    unit_ref,
    magnitude_ref,
    pooled_ref,
    own_target_ref,
    own_index_ref,
    own_count_ref,
    column_target_ref,
    head_ref,
    mix_gain_ref,
    weight_ref,
    weight_turned_ref,
    shifted_ref,
    slope_low_ref,
    normed_up_ref,
    mixed_up_ref,
    slope_up_ref,
    inverse_ref,
    loss_ref,
    head_grad_ref,
    point_up_ref,
    corr_up_ref,
    point_low_ref,
    corr_low_ref,
    upstream,
    act_grad,
    conv_grad,
    corr,
    point_up,
    moments,
):
    step = pl.program_id(0)
    last = pl.num_programs(0) - 1
    length, width = act_grad.shape[1], act_grad.shape[2]
    tiles = range(0, length, TILE)

    @pl.when(step == 0)
    def _():
        zeros = jnp.zeros((SEQS, PAD, width), F32)
        conv_grad[:, :PAD, :] = zeros
        conv_grad[:, PAD + length :, :] = zeros
        corr[...] = jnp.zeros_like(corr)
        point_up[...] = jnp.zeros_like(point_up)
        moments[...] = jnp.zeros_like(moments)
        every = gathered_ref[...]
        total_count = every.shape[0]
        own_count = own_unit_ref.shape[0]
        contract = (((1,), (1,)), ((), ()))
        gram = lax.dot_general(every, every, contract, preferred_element_type=F32)
        row_of = lax.broadcasted_iota(jnp.int32, (total_count, 1), 0)
        row_goal = lax.rem(row_of, own_count) < goal_total
        expon = jnp.where(row_goal, 0.0, jnp.exp(logit_scale * gram))
        column_total = jnp.sum(expon, axis=0, keepdims=True)
        scores = logit_scale * lax.dot_general(
            own_unit_ref[...], every, contract, preferred_element_type=F32
        )
        own_expon = jnp.exp(scores)
        column_of = lax.broadcasted_iota(jnp.int32, (own_count, total_count), 1)
        column_goal = lax.rem(column_of, own_count) < goal_total
        own_goal = lax.broadcasted_iota(jnp.int32, (own_count, total_count), 0) < goal_total
        own_total = jnp.sum(
            jnp.where(column_goal, 0.0, own_expon), axis=1, keepdims=True
        )
        hit_goal = column_of == own_target_ref[...]
        hit_premise = column_target_ref[...] == own_index_ref[...]
        of_goal = own_expon / own_total - jnp.where(hit_goal, 1.0, 0.0)
        of_premise = own_expon / column_total - jnp.where(hit_premise, 1.0, 0.0)
        score_grad = jnp.where(
            own_goal,
            jnp.where(column_goal, 0.0, of_goal),
            jnp.where(column_goal, of_premise, 0.0),
        )
        score_grad = (score_grad / float(goal_total)).astype(BF16)
        chosen = jnp.sum(jnp.where(hit_goal, scores, 0.0), axis=1, keepdims=True)
        loss_ref[...] = jnp.broadcast_to(jnp.log(own_total) - chosen, loss_ref.shape)
        unit_grad = logit_scale * jnp.dot(score_grad, every, preferred_element_type=F32)
        unit = unit_ref[...]
        along = jnp.sum(unit * unit_grad, axis=-1, keepdims=True)
        embed_grad = ((unit_grad - unit * along) / magnitude_ref[:, :1]).astype(BF16)
        head_grad_ref[...] = lax.dot_general(
            pooled_ref[...].astype(BF16),
            embed_grad,
            (((0,), (0,)), ((), ())),
            preferred_element_type=F32,
        ).astype(head_grad_ref.dtype)
        pooled_grad = lax.dot_general(
            embed_grad, head_ref[...], contract, preferred_element_type=F32
        )
        upstream[...] = pooled_grad / own_count_ref[:, :1]

    def grad_up(seq, carry):
        above = upstream[pl.ds(step * SEQS + seq, 1), :]
        for start in tiles:
            at = pl.ds(start, TILE)
            act_grad[seq, at, :] = (slope_up_ref[seq, at, :].astype(F32) * above).astype(BF16)
        return carry

    lax.fori_loop(0, SEQS, grad_up, 0)
    flat = act_grad[...].reshape(SEQS * length, width)
    conv_grad[:, PAD : PAD + length, :] = lax.dot_general(
        flat, weight_ref[1], (((1,), (1,)), ((), ())), preferred_element_type=F32
    ).reshape(SEQS, length, width)
    over_tokens = (((0,), (0,)), ((), ()))
    point_up[...] += lax.dot_general(
        mixed_up_ref[...].reshape(SEQS * length, width),
        flat,
        over_tokens,
        preferred_element_type=F32,
    )

    def norm_up(seq, carry):
        above = upstream[pl.ds(step * SEQS + seq, 1), :]
        sums = [corr[tap] for tap in range(3)]
        for start in tiles:
            at = pl.ds(start, TILE)
            normed = normed_up_ref[seq, at, :].astype(F32)
            inverse = inverse_ref[seq, at, :][:, :1]
            scaled = 0.0
            for tap in range(3):
                part = conv_grad[seq, pl.ds(PAD + start + (1 - tap) * UPPER_DILATION, TILE), :]
                scaled = scaled + mix_gain_ref[1, tap : tap + 1, :] * part
                product = part * normed
                sums[tap] = sums[tap] + product[:8] + product[8:]
            mean = jnp.mean(scaled * normed, axis=-1, keepdims=True)
            below = jnp.where(inverse > 0.0, above, 0.0) + inverse * (scaled - normed * mean)
            act_grad[seq, at, :] = (below * slope_low_ref[seq, at, :].astype(F32)).astype(BF16)
        for tap in range(3):
            corr[tap] = sums[tap]
        return carry

    lax.fori_loop(0, SEQS, norm_up, 0)
    moments[...] += lax.dot_general(
        act_grad[...].reshape(SEQS * length, width),
        shifted_ref[...].reshape(SEQS * length, 3 * width),
        over_tokens,
        preferred_element_type=F32,
    )

    @pl.when(step == last)
    def _():
        point_up_ref[...] = point_up[...].astype(point_up_ref.dtype)
        point = 0.0
        for tap in range(3):
            corr_up_ref[tap : tap + 1, :] = jnp.sum(corr[tap], axis=0, keepdims=True)
            part = moments[:, tap * width : (tap + 1) * width]
            corr_low_ref[tap : tap + 1, :] = jnp.sum(
                part * weight_turned_ref[...].astype(F32), axis=0, keepdims=True
            )
            point = point + mix_gain_ref[0, tap : tap + 1, :] * part
        point_low_ref[...] = point.T.astype(point_low_ref.dtype)


goal_total = 8


def whole(shape):
    return pl.BlockSpec(shape, lambda i, *_: (0,) * len(shape))


def chunk(length, width):
    return pl.BlockSpec((SEQS, length, width), lambda i, *_: (i, 0, 0))


def run_forward(goal_states, premise_states, lengths, mix_gain, weights, head_weight):
    goals, length, width = goal_states.shape[1:]
    premises = premise_states.shape[1]
    count = goals + premises
    embed = head_weight.shape[1]
    goal_steps = goals // SEQS
    tokens = lambda w, t: jax.ShapeDtypeStruct((count, length, w), t)
    outs = [
        (tokens(3 * width, BF16), chunk(length, 3 * width)),
        (tokens(width, BF16), chunk(length, width)),
        (tokens(width, BF16), chunk(length, width)),
        (tokens(width, BF16), chunk(length, width)),
        (tokens(width, BF16), chunk(length, width)),
        (tokens(LANES, F32), chunk(length, LANES)),
        (jax.ShapeDtypeStruct((count, width), F32), whole((count, width))),
        (jax.ShapeDtypeStruct((count, embed), F32), whole((count, embed))),
        (jax.ShapeDtypeStruct((count, LANES), F32), whole((count, LANES))),
        (
            jax.ShapeDtypeStruct((N_NEG, count, embed), BF16),
            whole((N_NEG, count, embed)),
        ),
    ]
    return pl.pallas_call(
        forward_kernel,
        name="forward",
        out_shape=[o[0] for o in outs],
        grid_spec=pltpu.PrefetchScalarGridSpec(
            num_scalar_prefetch=1,
            grid=(count // SEQS,),
            in_specs=[
                pl.BlockSpec(
                    (1, SEQS, length, width),
                    lambda i, *_: (0, jnp.minimum(i, goal_steps - 1), 0, 0),
                ),
                pl.BlockSpec(
                    (1, SEQS, length, width),
                    lambda i, *_: (0, jnp.maximum(i - goal_steps, 0), 0, 0),
                ),
                whole(mix_gain.shape),
                whole(weights.shape),
                whole(head_weight.shape),
            ],
            out_specs=[o[1] for o in outs],
            scratch_shapes=[
                pltpu.VMEM((SEQS, length, width), BF16),
                pltpu.VMEM((SEQS, length + 2 * PAD, width), F32),
                pltpu.VMEM((SEQS, length, width), BF16),
                pltpu.VMEM((SEQS, length, width), F32),
                pltpu.VMEM((SEQS, length, width), F32),
            ],
        ),
        compiler_params=pltpu.CompilerParams(
            dimension_semantics=("arbitrary",), vmem_limit_bytes=50 << 20
        ),
    )(lengths, goal_states, premise_states, mix_gain, weights, head_weight)


def run_backward(lengths, tables, head_weight, mix_gain, weights, turned, residuals):
    count, length, width = residuals[1].shape
    embed = head_weight.shape[1]
    singles = list(tables) + [head_weight, mix_gain, weights, turned]
    outs = [
        jax.ShapeDtypeStruct((count, LANES), F32),
        jax.ShapeDtypeStruct((width, embed), BF16),
        jax.ShapeDtypeStruct((width, width), BF16),
        jax.ShapeDtypeStruct((3, width), F32),
        jax.ShapeDtypeStruct((width, width), BF16),
        jax.ShapeDtypeStruct((3, width), F32),
    ]
    return pl.pallas_call(
        backward_kernel,
        name="backward",
        out_shape=outs,
        grid_spec=pltpu.PrefetchScalarGridSpec(
            num_scalar_prefetch=1,
            grid=(count // SEQS,),
            in_specs=[whole(s.shape) for s in singles]
            + [chunk(length, r.shape[2]) for r in residuals],
            out_specs=[whole(o.shape) for o in outs],
            scratch_shapes=[
                pltpu.VMEM((count, width), F32),
                pltpu.VMEM((SEQS, length, width), BF16),
                pltpu.VMEM((SEQS, length + 2 * PAD, width), F32),
                pltpu.VMEM((3, 8, width), F32),
                pltpu.VMEM((width, width), F32),
                pltpu.VMEM((width, 3 * width), F32),
            ],
        ),
        compiler_params=pltpu.CompilerParams(
            dimension_semantics=("arbitrary",), vmem_limit_bytes=50 << 20
        ),
    )(lengths, *singles, *residuals)


def to_rows(matrix):
    rows, columns = matrix.shape
    tiles = matrix.reshape(rows // 8, 8, columns // LANES, LANES)
    return tiles.transpose(0, 2, 1, 3).reshape(rows * columns // LANES, LANES)


def from_rows(flat, shape):
    rows, columns = shape
    tiles = flat.reshape(rows // 8, columns // LANES, 8, LANES)
    return tiles.transpose(0, 2, 1, 3).reshape(rows, columns)


def reduce_everywhere(arrays):
    devices = N_NEG * N_REP
    flat = [to_rows(array.astype(jnp.bfloat16)) for array in arrays]
    used = sum(piece.shape[0] for piece in flat)
    slice_rows = -(-used // (devices * 8)) * 8
    flat.append(jnp.zeros((devices * slice_rows - used, LANES), jnp.bfloat16))
    packed = jnp.concatenate(flat, axis=0).reshape(devices, slice_rows, LANES)
    axes = ("neg", "rep")
    received = lax.all_to_all(packed, axes, 0, 0)
    own = jnp.sum(received.astype(jnp.float32), axis=0).astype(jnp.bfloat16)
    spread = lax.all_to_all(
        jnp.broadcast_to(own[None], (devices, slice_rows, LANES)), axes, 0, 0
    )
    rows = spread.reshape(devices * slice_rows, LANES)
    results, start = [], 0
    for array in arrays:
        count = array.size // LANES
        piece = rows[start : start + count]
        results.append(from_rows(piece, array.shape).astype(jnp.float32))
        start += count
    return results


def local(
    goal_states,
    premise_states,
    goal_ids,
    premise_ids,
    positives,
    depthwise_kernels,
    block_norm_gains,
    pointwise_weights,
    head_weight,
):
    goals = goal_states.shape[1]
    premises = premise_states.shape[1]
    count = goals + premises
    lengths = jnp.sum(
        (jnp.concatenate([goal_ids[0], premise_ids[0]], axis=0) != 0).astype(jnp.int32), axis=1
    )
    mix_gain = depthwise_kernels * block_norm_gains[:, None, :]
    outs = run_forward(
        goal_states, premise_states, lengths, mix_gain, pointwise_weights, head_weight
    )
    residuals, (pooled, unit, magnitude, spread) = outs[:6], outs[6:]
    gathered = lax.all_to_all(spread, "neg", 0, 0).reshape(N_NEG * count, -1)
    position = lax.axis_index("neg")
    slot = positives[0] // premises * count + goals + positives[0] % premises
    slot = jnp.concatenate(
        [
            slot.reshape(N_NEG, goals).astype(jnp.int32),
            jnp.full((N_NEG, premises), -1, jnp.int32),
        ],
        axis=1,
    )
    own_target = lax.dynamic_slice_in_dim(slot, position, 1, 0).reshape(count, 1)
    own_index = (position * count + jnp.arange(count, dtype=jnp.int32)).reshape(count, 1)
    own_count = lengths.astype(F32).reshape(count, 1)
    tables = (
        gathered,
        spread[0],
        unit,
        magnitude,
        pooled,
        own_target,
        own_index,
        own_count,
        slot.reshape(1, N_NEG * count),
    )
    loss, head_grad, point_up, corr_up, point_low, corr_low = run_backward(
        lengths,
        tables,
        head_weight,
        mix_gain,
        pointwise_weights,
        pointwise_weights[0].T,
        residuals,
    )
    corr = jnp.stack([corr_low, corr_up])
    kernel_grad = corr * block_norm_gains[:, None, :]
    gain_grad = jnp.sum(corr * depthwise_kernels, axis=1)
    sums = reduce_everywhere(
        [
            point_low,
            point_up,
            head_grad,
            jnp.concatenate([kernel_grad.reshape(6, -1), gain_grad], axis=0),
        ]
    )
    small = sums[3]
    return (
        loss[:goals, 0][None, :],
        small[:6].reshape(2, 3, -1),
        small[6:8],
        jnp.stack(sums[:2]),
        sums[2],
    )


def solution(mesh):
    placed = (
        P("rep", "neg", None, None),
        P("rep", "neg", None, None),
        P("rep", "neg", None),
        P("rep", "neg", None),
        P("rep", None),
        P(),
        P(),
        P(),
        P(),
    )
    return jax.shard_map(
        local,
        mesh=mesh,
        in_specs=placed,
        out_specs=(P("rep", "neg"), P(), P(), P(), P()),
        check_vma=False,
    )
```

time: 214 us -> 174 us (0.81)
  Pallas kernels: 0 us -> 77.7 us
  other arithmetic: 80.8 us -> 4.85 us
  matrix products: 37.2 us -> 0 us
  waiting for transfers between devices: 32.2 us -> 28.4 us
    pallas_call x0 -> x2, Pallas kernels: none -> 77.7 us  [the longest x1 43 us: run_forward(): pl.pallas_call(forward_kernel, name='forward', out_shape=[o[0] for o in o...]
    reduce_sum x5 -> x1, other arithmetic: 39.7 us -> 0.83 us  [local(): jnp.sum((jnp.concatenate([goal_ids[0], premise_ids[0]], axis=0) != 0).ast...]
    dot_general x12 -> x0, matrix products: 37.2 us -> none  [the longest x2 16.6 us: conv_block_forward(): jnp.dot(mixed.reshape(count * length, width), weight, preferred_element_t...]
    convert_element_type x7 -> x1, other arithmetic: 31.5 us -> 0.01 us  [local(): own_count = lengths.astype(F32).reshape(count, 1)]
    mul x2 -> x1, other arithmetic: 5.67 us -> 0.72 us  [local(): mix_gain = depthwise_kernels * block_norm_gains[:, None, :]]
    all_to_all x1, waiting for transfers between devices: 7.81 us -> 4.62 us  [local(): gathered = lax.all_to_all(spread, 'neg', 0, 0).reshape(N_NEG * count, -1)]
    unnamed x110 -> x43, local copies, waits for them, and re-layouts: 10.2 us -> 11.1 us
  transfers between devices with their start and end apart: 2 -> 2, of which waited for: 2 -> 2; matrix products, arithmetic and copies ran while one was open for 0% -> 3% of each run, Pallas kernels for 0% -> 0%
where the time goes in v2:
time: 174 us
  Pallas kernels  77.7 us (45%)
  blocking collectives  32.6 us (19%)
  waiting for transfers between devices  28.4 us (16%)
  local copies, waits for them, and re-layouts  16.2 us (9%)
  starting transfers between devices  13.1 us (8%)
  other arithmetic  4.85 us (3%)
    pallas_call x1, Pallas kernels, run_forward(): pl.pallas_call(forward_kernel, name='forward', out_shape=[o[0] for o in o...  43 us
    pallas_call x1, Pallas kernels, run_backward(): pl.pallas_call(backward_kernel, name='backward', out_shape=outs, grid_spe...  34.6 us
    all_to_all x1, blocking collectives, reduce_everywhere(): received = lax.all_to_all(packed, axes, 0, 0)  32.6 us
    all_to_all x1, waiting for transfers between devices, reduce_everywhere(): lax.all_to_all(jnp.broadcast_to(own[None], (devices, slice_rows, LANES)),...  23.7 us
    unnamed x43, local copies, waits for them, and re-layouts  11.1 us
    all_to_all x1, starting transfers between devices, local(): gathered = lax.all_to_all(spread, 'neg', 0, 0).reshape(N_NEG * count, -1)  8.73 us
    all_to_all x1, waiting for transfers between devices, local(): gathered = lax.all_to_all(spread, 'neg', 0, 0).reshape(N_NEG * count, -1)  4.62 us
    all_to_all x1, starting transfers between devices, reduce_everywhere(): lax.all_to_all(jnp.broadcast_to(own[None], (devices, slice_rows, LANES)),...  4.35 us
  transfers between devices with their start and end apart: 2, of which 2 were waited for; matrix products, arithmetic and copies ran while one was open for 3% of the time, Pallas kernels for 0%

profile of v2, /device:TPU:1, one launch (start us, length us, event | category | flops | bytes accessed | tf_op | source)
XLA Modules:
  0.0 173.6 jit_solution(7952615938781817915)
XLA Ops:
  0.6 0.8 convert_reduce_fusion.lengths
  1.5 0.7 copy_multiply_fusion.1.mix_gain_ref
  2.2 1.2 copy-done
  3.4 0.9 copy-done.2
  4.4 1.2 copy-done.4
  5.6 43.0 %forward.1 = (bf16[40,128,1536]{2,1,0:T(8,128)(2,1)}, bf16[40,128,512]{2,1,0:T(8,128)(2,1)}, bf16[40,128,512]{2,1,0:T(8,128)(2,1)}, bf16[40,128,512]{2,1,0:T(8,1...) custom-call(s32[40]{0:T(128)S(1)} %convert_reduce_fusion.lengths, ...), custom_call_target="tpu_custom_call" | custom-call | tf_op jit(solution)/shard_map/forward/pallas_call | solution.py:369
  48.6 0.6 copy-done.5
  50.5 8.7 %all-to-all-start = ((bf16[16,40,256]{2,1,0:T(8,128)(2,1)}), bf16[16,40,256]{2,1,0:T(8,128)(2,1)S(1)}, u32[]{:S(2)}, u32[]{:S(2)}) async-start(bf16[16,40,256]{2,1,0:T(8,128)(2,1)} %get-tuple-element.21), calls=%async_computation | async-start | bytes 655360 | tf_op jit(solution)/shard_map/all_to_all | solution.py:498
  59.8 0.7 reduce.6
  61.1 1.3 slice_bitcast_fusion.own_unit_ref
  62.4 4.6 %all-to-all-done = bf16[16,40,256]{2,1,0:T(8,128)(2,1)S(1)} async-done(((bf16[16,40,256]{2,1,0:T(8,128)(2,1)}), bf16[16,40,256]{2,1,0:T(8,128)(2,1)S(1)}, u32[]{:S(2)}, u32[]{:S(2)}) %all-to-all-start) | async-done | bytes 327712 | tf_op jit(solution)/shard_map/all_to_all | solution.py:498
  67.1 0.9 copy-done.6
  68.0 0.7 copy-done.7
  68.7 0.8 copy-done.9
  69.5 0.7 copy-done.11
  70.2 0.7 copy-done.13
  70.8 34.6 %backward.1 = (f32[40,128]{1,0:T(8,128)S(1)}, bf16[512,256]{1,0:T(8,128)(2,1)S(1)}, bf16[512,512]{1,0:T(8,128)(2,1)S(1)}, f32[3,512]{1,0:T(4,128)S(1)}, bf16[512...) custom-call(s32[40]{0:T(128)S(1)} %copy-done.13, bf16[640,256]{1,0:T(8,128)(2,1)S(1)} %bitcast.63, ...), custom_call_target="tpu_custom_call" | custom-call | tf_op jit(solution)/shard_map/backward/pallas_call | solution.py:416
  106.4 32.6 %all_to_all.15 = bf16[128,48,128]{2,1,0:T(8,128)(2,1)S(1)} all-to-all(bf16[128,48,128]{2,1,0:T(8,128)(2,1)S(1)} %bitcast.72), channel_id=1, replica_groups=mesh['neg'=16,'rep'=8] {'neg','rep'}, dimensions={0} | all-to-all | bytes 3145728 | tf_op jit(solution)/shard_map/all_to_all | solution.py:461
  139.2 1.3 broadcast_in_dim.5
  140.6 4.3 %all-to-all-start.2 = ((bf16[128,48,128]{2,1,0:T(8,128)(2,1)}), bf16[128,48,128]{2,1,0:T(8,128)(2,1)S(1)}, u32[]{:S(2)}, u32[]{:S(2)}) async-start(bf16[128,48,128]{2,1,0:T(8,128)(2,1)} %broadcast_in_dim.5), calls=%async_computation.2 | async-start | bytes 3145728 | tf_op jit(solution)/shard_map/all_to_all | solution.py:463
  144.9 1.3 slice_reduce_fusion
  146.3 23.7 %all-to-all-done.2 = bf16[128,48,128]{2,1,0:T(8,128)(2,1)S(1)} async-done(((bf16[128,48,128]{2,1,0:T(8,128)(2,1)}), bf16[128,48,128]{2,1,0:T(8,128)(2,1)S(1)}, u32[]{:S(2)}, u32[]{:S(2)}) %all-to-all-start.2) | async-done | bytes 1572896 | tf_op jit(solution)/shard_map/all_to_all | solution.py:463
  171.3 0.8 convert_bitcast_fusion
  172.2 1.5 maximum_convert_fusion
  (57 shorter events, 4.8 us)
Async XLA Ops:
  1.5 57.8 %copy-start.12 = (s32[40]{0:T(128)}, s32[40]{0:T(128)S(1)}, u32[]{:S(2)}) copy-start(s32[40]{0:T(128)S(1)} %convert_reduce_fusion.lengths) | copy-start | bytes 484
  2.2 1.2 copy-start
  3.4 0.9 copy-start.2
  4.4 1.2 copy-start.4
  5.6 54.2 %copy-start.17 = (s32[1,128]{1,0:T(1,128)S(1)}, s32[1,128]{1,0:T(1,128)}, u32[]{:S(2)}) copy-start(s32[1,128]{1,0:T(1,128)} %param.13) | copy-start | bytes 1540
  48.6 0.6 copy-start.5
  49.3 0.6 copy-start.8
  49.9 0.6 copy-start.10
  50.5 10.4 %slice-start = ((bf16[2,512,512]{2,1,0:T(8,128)(2,1)}), bf16[1,512,512]{2,1,0:T(8,128)(2,1)S(1)}, s32[]{:S(2)}) async-start(bf16[2,512,512]{2,1,0:T(8,128)(2,1)} %weight_ref.3), calls=%async_computation.3 | async-start | bytes 1048576 | tf_op jit(solution)/shard_map/slice | solution.py:528
  50.5 16.6 %copy-start.1 = (bf16[2,512,512]{2,1,0:T(8,128)(2,1)S(1)}, bf16[2,512,512]{2,1,0:T(8,128)(2,1)}, u32[]{:S(2)}) copy-start(bf16[2,512,512]{2,1,0:T(8,128)(2,1)} %weight_ref.3) | copy-start | bytes 3145732
  50.5 16.6 %copy-start.3 = (bf16[512,256]{1,0:T(8,128)(2,1)S(1)}, bf16[512,256]{1,0:T(8,128)(2,1)}, u32[]{:S(2)}) copy-start(bf16[512,256]{1,0:T(8,128)(2,1)} %head_ref.3) | copy-start | bytes 786436
  50.5 16.6 %all-to-all-start = ((bf16[16,40,256]{2,1,0:T(8,128)(2,1)}), bf16[16,40,256]{2,1,0:T(8,128)(2,1)S(1)}, u32[]{:S(2)}, u32[]{:S(2)}) async-start(bf16[16,40,256]{2,1,0:T(8,128)(2,1)} %get-tuple-element.21), calls=%async_computation | async-start | bytes 655360 | tf_op jit(solution)/shard_map/all_to_all | solution.py:498
  67.1 0.9 copy-start.6
  68.0 0.7 copy-start.7
  68.7 0.8 copy-start.9
  69.5 0.7 copy-start.11
  70.2 0.7 copy-start.13
  70.8 34.6 %copy-start.15 = (f32[2,3,512]{2,0,1:T(2,128)S(1)}, f32[2,3,512]{2,0,1:T(2,128)}, u32[]{:S(2)}) copy-start(f32[2,3,512]{2,0,1:T(2,128)} %param.14) | copy-start | bytes 36868
  70.8 34.7 %copy-start.16 = (f32[2,512]{1,0:T(2,128)S(1)}, f32[2,512]{1,0:T(2,128)}, u32[]{:S(2)}) copy-start(f32[2,512]{1,0:T(2,128)} %param.15) | copy-start | bytes 12292
  105.5 0.6 copy-start.14
  140.6 29.4 %all-to-all-start.2 = ((bf16[128,48,128]{2,1,0:T(8,128)(2,1)}), bf16[128,48,128]{2,1,0:T(8,128)(2,1)S(1)}, u32[]{:S(2)}, u32[]{:S(2)}) async-start(bf16[128,48,128]{2,1,0:T(8,128)(2,1)} %broadcast_in_dim.5), calls=%async_computation.2 | async-start | bytes 3145728 | tf_op jit(solution)/shard_map/all_to_all | solution.py:463

commit v3 on v2

v3 whole, which is shorter than its diff:
```python
import functools

import jax
import jax.numpy as jnp
from jax import lax
from jax.experimental import pallas as pl
from jax.experimental.pallas import tpu as pltpu
from jax.sharding import Mesh
from jax.sharding import PartitionSpec as P

LOWER_DILATION = 4
UPPER_DILATION = 8
N_NEG = 16
N_REP = 8
LANES = 128
PAD = 8
TILE = 16
SEQS = 4
SLICE = 48
EPS = 1e-06
GELU_C = 0.7978845608028654
GELU_A = 0.044715
logit_scale = 20.0
F32 = jnp.float32
BF16 = jnp.bfloat16


def gelu_parts(x):
    square = x * x
    half = 0.5 + 0.5 * jnp.tanh(x * (GELU_C + (GELU_C * GELU_A) * square))
    value = x * half
    slope = half + value * (1.0 - half) * (
        2.0 * GELU_C + (6.0 * GELU_C * GELU_A) * square
    )
    return value, slope


def forward_kernel(
    lengths,
    goal_ref,
    premise_ref,
    depth_ref,
    gain_ref,
    weight_ref,
    head_ref,
    shifted_ref,
    slope_low_ref,
    normed_up_ref,
    mixed_up_ref,
    slope_up_ref,
    inverse_ref,
    summary_ref,
    spread_ref,
    states,
    padded,
    mixed,
    pre_act,
    hidden,
    mix_gain,
):
    step = pl.program_id(0)
    length, width = states.shape[1], states.shape[2]
    tiles = range(0, length, TILE)
    rows = lax.broadcasted_iota(jnp.int32, (TILE, 1), 0)

    @pl.when(step == 0)
    def _():
        zeros = jnp.zeros((SEQS, PAD, width), F32)
        padded[:, :PAD, :] = zeros
        padded[:, PAD + length :, :] = zeros
        mix_gain[...] = depth_ref[...] * gain_ref[...]

    def norm(values, valid):
        mean = jnp.mean(values * values, axis=-1, keepdims=True)
        inverse = jnp.where(valid, lax.rsqrt(mean + EPS), 0.0)
        return values * inverse, inverse

    def norm_inputs(source):
        def body(seq, carry):
            count = lengths[step * SEQS + seq]
            for start in tiles:
                raw = source[0, seq, pl.ds(start, TILE), :]
                states[seq, pl.ds(start, TILE), :] = raw
                normed, _ = norm(raw.astype(F32), rows < count - start)
                padded[seq, pl.ds(PAD + start, TILE), :] = normed
            return carry

        lax.fori_loop(0, SEQS, body, 0)

    goal_steps = goal_total // SEQS

    @pl.when(step < goal_steps)
    def _():
        norm_inputs(goal_ref)

    @pl.when(step >= goal_steps)
    def _():
        norm_inputs(premise_ref)

    def mix_low(seq, carry):
        for start in tiles:
            window = [
                padded[seq, pl.ds(PAD + start + tap * LOWER_DILATION, TILE), :]
                for tap in (-1, 0, 1)
            ]
            total = 0.0
            for tap in range(3):
                total = total + mix_gain[tap, 0:1, :] * window[tap]
                shifted_ref[seq, pl.ds(start, TILE), tap * width : (tap + 1) * width] = (
                    window[tap].astype(BF16)
                )
            mixed[seq, pl.ds(start, TILE), :] = total.astype(BF16)
        return carry

    lax.fori_loop(0, SEQS, mix_low, 0)
    pre_act[...] = jnp.dot(
        mixed[...].reshape(SEQS * length, width), weight_ref[0], preferred_element_type=F32
    ).reshape(SEQS, length, width)

    def act_low(seq, carry):
        count = lengths[step * SEQS + seq]
        for start in tiles:
            at = pl.ds(start, TILE)
            value, slope = gelu_parts(pre_act[seq, at, :])
            slope_low_ref[seq, at, :] = slope.astype(BF16)
            out = states[seq, at, :].astype(F32) + value
            hidden[seq, at, :] = out
            normed, inverse = norm(out, rows < count - start)
            padded[seq, pl.ds(PAD + start, TILE), :] = normed
            normed_up_ref[seq, at, :] = normed.astype(BF16)
            inverse_ref[seq, at, :] = jnp.broadcast_to(inverse, (TILE, LANES))
        return carry

    lax.fori_loop(0, SEQS, act_low, 0)

    def mix_up(seq, carry):
        for start in tiles:
            at = pl.ds(start, TILE)
            total = 0.0
            for tap in range(3):
                total = total + mix_gain[tap, 1:2, :] * (
                    padded[seq, pl.ds(PAD + start + (tap - 1) * UPPER_DILATION, TILE), :]
                )
            mixed_up_ref[seq, at, :] = total.astype(BF16)
        return carry

    lax.fori_loop(0, SEQS, mix_up, 0)
    pre_act[...] = jnp.dot(
        mixed_up_ref[...].reshape(SEQS * length, width),
        weight_ref[1],
        preferred_element_type=F32,
    ).reshape(SEQS, length, width)

    def act_up(seq, carry):
        count = lengths[step * SEQS + seq]
        pooled = jnp.zeros((TILE, width), F32)
        for start in tiles:
            at = pl.ds(start, TILE)
            valid = rows < count - start
            value, slope = gelu_parts(pre_act[seq, at, :])
            slope_up_ref[seq, at, :] = jnp.where(valid, slope, 0.0).astype(BF16)
            pooled = pooled + jnp.where(valid, hidden[seq, at, :] + value, 0.0)
        summary_ref[pl.ds(step * SEQS + seq, 1), :width] = (
            jnp.sum(pooled, axis=0, keepdims=True) / count.astype(F32)
        )
        return carry

    lax.fori_loop(0, SEQS, act_up, 0)

    @pl.when(step == pl.num_programs(0) - 1)
    def _():
        embedded = jnp.dot(
            summary_ref[:, :width].astype(BF16), head_ref[...], preferred_element_type=F32
        )
        magnitude = jnp.sqrt(jnp.sum(embedded * embedded, axis=-1, keepdims=True) + EPS)
        unit = embedded / magnitude
        embed = unit.shape[1]
        summary_ref[:, width : width + embed] = unit
        summary_ref[:, width + embed :] = jnp.broadcast_to(magnitude, (unit.shape[0], LANES))
        rounded = unit.astype(BF16)
        for peer in range(N_NEG):
            spread_ref[peer] = rounded


def backward_kernel(
    scalars,
    gathered_ref,
    summary_ref,
    column_target_ref,
    head_ref,
    depth_ref,
    gain_ref,
    weight_ref,
    weight_turned_ref,
    shifted_ref,
    slope_low_ref,
    normed_up_ref,
    mixed_up_ref,
    slope_up_ref,
    inverse_ref,
    loss_ref,
    keep_ref,
    send_ref,
    upstream,
    act_grad,
    conv_grad,
    corr,
    point_up,
    moments,
    head_grad,
    mix_gain,
):
    step = pl.program_id(0)
    last = pl.num_programs(0) - 1
    count = summary_ref.shape[0]
    position, core = scalars[count], scalars[count + 1]
    length, width = act_grad.shape[1], act_grad.shape[2]
    tiles = range(0, length, TILE)

    @pl.when(step == 0)
    def _():
        zeros = jnp.zeros((SEQS, PAD, width), F32)
        conv_grad[:, :PAD, :] = zeros
        conv_grad[:, PAD + length :, :] = zeros
        corr[...] = jnp.zeros_like(corr)
        point_up[...] = jnp.zeros_like(point_up)
        moments[...] = jnp.zeros_like(moments)
        every = gathered_ref[...]
        total_count = every.shape[0]
        own_count = count
        embed = every.shape[1]
        mix_gain[...] = depth_ref[...] * gain_ref[...]
        unit = summary_ref[:, width : width + embed]
        magnitude = summary_ref[:, width + embed : width + embed + 1]
        contract = (((1,), (1,)), ((), ()))
        gram = lax.dot_general(every, every, contract, preferred_element_type=F32)
        row_of = lax.broadcasted_iota(jnp.int32, (total_count, 1), 0)
        row_goal = lax.rem(row_of, own_count) < goal_total
        expon = jnp.where(row_goal, 0.0, jnp.exp(logit_scale * gram))
        column_total = jnp.sum(expon, axis=0, keepdims=True)
        scores = logit_scale * lax.dot_general(
            unit.astype(BF16), every, contract, preferred_element_type=F32
        )
        own_expon = jnp.exp(scores)
        column_of = lax.broadcasted_iota(jnp.int32, (own_count, total_count), 1)
        column_goal = lax.rem(column_of, own_count) < goal_total
        own_goal = lax.broadcasted_iota(jnp.int32, (own_count, total_count), 0) < goal_total
        own_total = jnp.sum(
            jnp.where(column_goal, 0.0, own_expon), axis=1, keepdims=True
        )
        own_index = position * own_count + lax.broadcasted_iota(
            jnp.int32, (own_count, total_count), 0
        )
        targets = column_target_ref[...]
        own_target = jnp.sum(
            jnp.where(column_of == own_index, targets.astype(F32), 0.0), axis=1, keepdims=True
        ).astype(jnp.int32)
        hit_goal = column_of == own_target
        hit_premise = targets == own_index
        of_goal = own_expon / own_total - jnp.where(hit_goal, 1.0, 0.0)
        of_premise = own_expon / column_total - jnp.where(hit_premise, 1.0, 0.0)
        score_grad = jnp.where(
            own_goal,
            jnp.where(column_goal, 0.0, of_goal),
            jnp.where(column_goal, of_premise, 0.0),
        )
        score_grad = (score_grad / float(goal_total)).astype(BF16)
        chosen = jnp.sum(jnp.where(hit_goal, scores, 0.0), axis=1, keepdims=True)
        loss_ref[...] = jnp.broadcast_to(jnp.log(own_total) - chosen, loss_ref.shape)
        unit_grad = logit_scale * jnp.dot(score_grad, every, preferred_element_type=F32)
        along = jnp.sum(unit * unit_grad, axis=-1, keepdims=True)
        embed_grad = ((unit_grad - unit * along) / magnitude).astype(BF16)
        head_grad[...] = lax.dot_general(
            summary_ref[:, :width].astype(BF16),
            embed_grad,
            (((0,), (0,)), ((), ())),
            preferred_element_type=F32,
        ).astype(BF16)
        upstream[...] = lax.dot_general(
            embed_grad, head_ref[...], contract, preferred_element_type=F32
        )

    def grad_up(seq, carry):
        row = pl.ds(step * SEQS + seq, 1)
        above = upstream[row, :] / scalars[step * SEQS + seq].astype(F32)
        upstream[row, :] = above
        for start in tiles:
            at = pl.ds(start, TILE)
            act_grad[seq, at, :] = (slope_up_ref[seq, at, :].astype(F32) * above).astype(BF16)
        return carry

    lax.fori_loop(0, SEQS, grad_up, 0)
    flat = act_grad[...].reshape(SEQS * length, width)
    conv_grad[:, PAD : PAD + length, :] = lax.dot_general(
        flat, weight_ref[0], (((1,), (1,)), ((), ())), preferred_element_type=F32
    ).reshape(SEQS, length, width)
    over_tokens = (((0,), (0,)), ((), ()))
    point_up[...] += lax.dot_general(
        mixed_up_ref[...].reshape(SEQS * length, width),
        flat,
        over_tokens,
        preferred_element_type=F32,
    )

    def norm_up(seq, carry):
        above = upstream[pl.ds(step * SEQS + seq, 1), :]
        sums = [corr[tap] for tap in range(3)]
        for start in tiles:
            at = pl.ds(start, TILE)
            normed = normed_up_ref[seq, at, :].astype(F32)
            inverse = inverse_ref[seq, at, :][:, :1]
            scaled = 0.0
            for tap in range(3):
                part = conv_grad[seq, pl.ds(PAD + start + (1 - tap) * UPPER_DILATION, TILE), :]
                scaled = scaled + mix_gain[tap, 1:2, :] * part
                product = part * normed
                sums[tap] = sums[tap] + product[:8] + product[8:]
            mean = jnp.mean(scaled * normed, axis=-1, keepdims=True)
            below = jnp.where(inverse > 0.0, above, 0.0) + inverse * (scaled - normed * mean)
            act_grad[seq, at, :] = (below * slope_low_ref[seq, at, :].astype(F32)).astype(BF16)
        for tap in range(3):
            corr[tap] = sums[tap]
        return carry

    lax.fori_loop(0, SEQS, norm_up, 0)
    moments[...] += lax.dot_general(
        act_grad[...].reshape(SEQS * length, width),
        shifted_ref[...].reshape(SEQS * length, 3 * width),
        over_tokens,
        preferred_element_type=F32,
    )

    def emit(low_ref, up_ref):
        point, rows = 0.0, []
        for tap in range(3):
            part = moments[:, tap * width : (tap + 1) * width]
            rows.append(
                jnp.sum(part * weight_turned_ref[...].astype(F32), axis=0, keepdims=True)
            )
            point = point + mix_gain[tap, 0:1, :] * part
        rows += [jnp.sum(corr[tap], axis=0, keepdims=True) for tap in range(3)]
        rows.append(jnp.zeros((2, width), F32))
        small = jnp.concatenate(rows, axis=0)
        low = point.T.astype(BF16)
        up = point_up[...].astype(BF16)
        for part in range(width // LANES):
            lanes = slice(part * LANES, (part + 1) * LANES)
            low_ref[part * width : (part + 1) * width, :] = low[:, lanes]
            up_ref[part * width : (part + 1) * width, :] = up[:, lanes]
        base = width * width // LANES
        for part in range(head_grad.shape[1] // LANES):
            lanes = slice(part * LANES, (part + 1) * LANES)
            low_ref[base + part * width : base + (part + 1) * width, :] = head_grad[:, lanes]
        tail = [small[:, part * LANES : (part + 1) * LANES] for part in range(width // LANES)]
        up_ref[base : base + 32, :] = jnp.concatenate(tail, axis=0).astype(BF16)
        up_ref[base + 32 :, :] = jnp.zeros((up_ref.shape[0] - base - 32, LANES), BF16)

    @pl.when((step == last) & (core == 0))
    def _():
        emit(keep_ref, send_ref)

    @pl.when((step == last) & (core == 1))
    def _():
        emit(send_ref, keep_ref)


def spread_kernel(parts_ref, spread_ref):
    total = parts_ref[0].astype(F32)
    for peer in range(1, parts_ref.shape[0]):
        total = total + parts_ref[peer].astype(F32)
    total = total.astype(BF16)
    for peer in range(parts_ref.shape[0]):
        spread_ref[peer] = total


def unpack_kernel(
    scalars,
    mine_ref,
    other_ref,
    depth_ref,
    gain_ref,
    depth_out,
    gain_out,
    point_out,
    head_out,
):
    core = scalars[scalars.shape[0] - 1]
    width = gain_ref.shape[1]
    base = width * width // LANES

    def emit(low_ref, up_ref):
        for part in range(width // LANES):
            lanes = slice(part * LANES, (part + 1) * LANES)
            rows = slice(part * width, (part + 1) * width)
            point_out[0, :, lanes] = low_ref[rows, :].astype(F32)
            point_out[1, :, lanes] = up_ref[rows, :].astype(F32)
        for part in range(head_out.shape[1] // LANES):
            lanes = slice(part * LANES, (part + 1) * LANES)
            head_out[:, lanes] = low_ref[
                base + part * width : base + (part + 1) * width, :
            ].astype(F32)
        small = up_ref[base : base + 32, :].astype(F32)
        for part in range(width // LANES):
            lanes = slice(part * LANES, (part + 1) * LANES)
            rows = small[part * 8 : (part + 1) * 8, :]
            for block in range(2):
                total = 0.0
                for tap in range(3):
                    row = rows[block * 3 + tap : block * 3 + tap + 1, :]
                    depth_out[tap, block : block + 1, lanes] = (
                        row * gain_ref[block : block + 1, lanes]
                    )
                    total = total + row * depth_ref[tap, block : block + 1, lanes]
                gain_out[block : block + 1, lanes] = total

    @pl.when(core == 0)
    def _():
        emit(mine_ref, other_ref)

    @pl.when(core == 1)
    def _():
        emit(other_ref, mine_ref)


goal_total = 8


def whole(shape):
    return pl.BlockSpec(shape, lambda i, *_: (0,) * len(shape))


def chunk(length, width):
    return pl.BlockSpec((SEQS, length, width), lambda i, *_: (i, 0, 0))


def run_forward(scalars, goal_states, premise_states, depth, gains, weights, head_weight):
    goals, length, width = goal_states.shape[1:]
    premises = premise_states.shape[1]
    count = goals + premises
    embed = head_weight.shape[1]
    goal_steps = goals // SEQS
    tokens = lambda w, t: jax.ShapeDtypeStruct((count, length, w), t)
    summary = (count, width + embed + LANES)
    outs = [
        (tokens(3 * width, BF16), chunk(length, 3 * width)),
        (tokens(width, BF16), chunk(length, width)),
        (tokens(width, BF16), chunk(length, width)),
        (tokens(width, BF16), chunk(length, width)),
        (tokens(width, BF16), chunk(length, width)),
        (tokens(LANES, F32), chunk(length, LANES)),
        (jax.ShapeDtypeStruct(summary, F32), whole(summary)),
        (
            jax.ShapeDtypeStruct((N_NEG, count, embed), BF16),
            whole((N_NEG, count, embed)),
        ),
    ]
    return pl.pallas_call(
        forward_kernel,
        name="forward",
        out_shape=[o[0] for o in outs],
        grid_spec=pltpu.PrefetchScalarGridSpec(
            num_scalar_prefetch=1,
            grid=(count // SEQS,),
            in_specs=[
                pl.BlockSpec(
                    (1, SEQS, length, width),
                    lambda i, *_: (0, jnp.minimum(i, goal_steps - 1), 0, 0),
                ),
                pl.BlockSpec(
                    (1, SEQS, length, width),
                    lambda i, *_: (0, jnp.maximum(i - goal_steps, 0), 0, 0),
                ),
                whole(depth.shape),
                whole(gains.shape),
                whole(weights.shape),
                whole(head_weight.shape),
            ],
            out_specs=[o[1] for o in outs],
            scratch_shapes=[
                pltpu.VMEM((SEQS, length, width), BF16),
                pltpu.VMEM((SEQS, length + 2 * PAD, width), F32),
                pltpu.VMEM((SEQS, length, width), BF16),
                pltpu.VMEM((SEQS, length, width), F32),
                pltpu.VMEM((SEQS, length, width), F32),
                pltpu.VMEM(depth.shape, F32),
            ],
        ),
        compiler_params=pltpu.CompilerParams(
            dimension_semantics=("arbitrary",), vmem_limit_bytes=60 << 20
        ),
    )(scalars, goal_states, premise_states, depth, gains, weights, head_weight)


def run_backward(scalars, tables, residuals):
    count, length, width = residuals[1].shape
    embed = tables[0].shape[1]
    depth = tables[4]
    half = (N_NEG * N_REP // 2 * SLICE, LANES)
    outs = [
        jax.ShapeDtypeStruct((count, LANES), F32),
        jax.ShapeDtypeStruct(half, BF16),
        jax.ShapeDtypeStruct(half, BF16),
    ]
    specs = [whole(t.shape) for t in tables]
    specs[6] = pl.BlockSpec((1, width, width), lambda i, *_: (1, 0, 0))
    return pl.pallas_call(
        backward_kernel,
        name="backward",
        out_shape=outs,
        grid_spec=pltpu.PrefetchScalarGridSpec(
            num_scalar_prefetch=1,
            grid=(count // SEQS,),
            in_specs=specs + [chunk(length, r.shape[2]) for r in residuals],
            out_specs=[whole(o.shape) for o in outs],
            scratch_shapes=[
                pltpu.VMEM((count, width), F32),
                pltpu.VMEM((SEQS, length, width), BF16),
                pltpu.VMEM((SEQS, length + 2 * PAD, width), F32),
                pltpu.VMEM((3, 8, width), F32),
                pltpu.VMEM((width, width), F32),
                pltpu.VMEM((width, 3 * width), F32),
                pltpu.VMEM((width, embed), BF16),
                pltpu.VMEM(depth.shape, F32),
            ],
        ),
        compiler_params=pltpu.CompilerParams(
            dimension_semantics=("arbitrary",), vmem_limit_bytes=60 << 20
        ),
    )(scalars, *tables, *residuals)


def reduce_everywhere(scalars, keep, send, depth, gains, embed):
    peers = N_NEG * N_REP // 2
    axes = ("neg", "chip")
    swap = [(0, 1), (1, 0)]
    width = gains.shape[1]
    got = lax.ppermute(send, "core", swap)
    pair = (keep.astype(F32) + got.astype(F32)).astype(BF16)
    parts = lax.all_to_all(pair.reshape(peers, SLICE, LANES), axes, 0, 0)
    spread = pl.pallas_call(
        spread_kernel, name="spread", out_shape=jax.ShapeDtypeStruct(parts.shape, BF16)
    )(parts)
    mine = lax.all_to_all(spread, axes, 0, 0).reshape(peers * SLICE, LANES)
    other = lax.ppermute(mine, "core", swap)
    vmem = pl.BlockSpec(memory_space=pltpu.VMEM)
    return pl.pallas_call(
        unpack_kernel,
        name="unpack",
        in_specs=[pl.BlockSpec(memory_space=pltpu.SMEM)] + [vmem] * 4,
        out_specs=[vmem] * 4,
        out_shape=[
            jax.ShapeDtypeStruct(depth.shape, F32),
            jax.ShapeDtypeStruct(gains.shape, F32),
            jax.ShapeDtypeStruct((2, width, width), F32),
            jax.ShapeDtypeStruct((width, embed), F32),
        ],
    )(scalars, mine, other, depth, gains)


def local(
    goal_states,
    premise_states,
    goal_ids,
    premise_ids,
    positives,
    depthwise_kernels,
    block_norm_gains,
    pointwise_weights,
    head_weight,
):
    goals = goal_states.shape[1]
    premises = premise_states.shape[1]
    count = goals + premises
    position = lax.axis_index("neg")
    lengths = jnp.sum(
        (jnp.concatenate([goal_ids[0], premise_ids[0]], axis=0) != 0).astype(jnp.int32), axis=1
    )
    scalars = jnp.concatenate(
        [lengths, jnp.stack([position, lax.axis_index("core")]).astype(jnp.int32)]
    )
    depth = depthwise_kernels.transpose(1, 0, 2)
    outs = run_forward(
        scalars,
        goal_states,
        premise_states,
        depth,
        block_norm_gains,
        pointwise_weights,
        head_weight,
    )
    residuals, (summary, spread) = outs[:6], outs[6:]
    gathered = lax.all_to_all(spread, "neg", 0, 0).reshape(N_NEG * count, -1)
    slot = positives[0] // premises * count + goals + positives[0] % premises
    slot = jnp.concatenate(
        [
            slot.reshape(N_NEG, goals).astype(jnp.int32),
            jnp.full((N_NEG, premises), -1, jnp.int32),
        ],
        axis=1,
    )
    tables = (
        gathered,
        summary,
        slot.reshape(1, N_NEG * count),
        head_weight,
        depth,
        block_norm_gains,
        pointwise_weights,
        pointwise_weights[0].T,
    )
    loss, keep, send = run_backward(scalars, tables, residuals)
    depth_grad, gain_grad, point_grad, head_grad = reduce_everywhere(
        scalars, keep, send, depth, block_norm_gains, head_weight.shape[1]
    )
    return (
        loss[:goals, 0][None, :],
        depth_grad.transpose(1, 0, 2),
        gain_grad,
        point_grad,
        head_grad,
    )


def solution(mesh):
    split = Mesh(mesh.devices.reshape(N_NEG, N_REP // 2, 2), ("neg", "chip", "core"))
    group = ("chip", "core")
    placed = (
        P(group, "neg", None, None),
        P(group, "neg", None, None),
        P(group, "neg", None),
        P(group, "neg", None),
        P(group, None),
        P(),
        P(),
        P(),
        P(),
    )
    return jax.shard_map(
        local,
        mesh=split,
        in_specs=placed,
        out_specs=(P(group, "neg"), P(), P(), P(), P()),
        check_vma=False,
    )
```

time: 174 us -> 159 us (0.914)
  waiting for transfers between devices: 28.4 us -> 7.58 us
  local copies, waits for them, and re-layouts: 16.2 us -> 5.23 us
  Pallas kernels: 77.7 us -> 86.9 us
  blocking collectives: 32.6 us -> 40.8 us
    all_to_all x1 -> x0, waiting for transfers between devices: 23.7 us -> none  [reduce_everywhere(): lax.all_to_all(jnp.broadcast_to(own[None], (devices, slice_rows, LANES)),...]
    all_to_all x1 -> x2, blocking collectives: 32.6 us -> 40.8 us  [the longest x1 21.9 us: reduce_everywhere(): parts = lax.all_to_all(pair.reshape(peers, SLICE, LANES), axes, 0, 0)]
    unnamed x43 -> x10, local copies, waits for them, and re-layouts: 11.1 us -> 3.17 us
    pallas_call x0 -> x2, Pallas kernels: none -> 5.38 us  [the longest x1 3.21 us: reduce_everywhere(): pl.pallas_call(unpack_kernel, name='unpack', in_specs=[pl.BlockSpec(memor...]
    ppermute x0 -> x2, starting transfers between devices: none -> 5.19 us  [the longest x1 2.89 us: reduce_everywhere(): other = lax.ppermute(mine, 'core', swap)]
    all_to_all x1 -> x0, starting transfers between devices: 4.35 us -> none  [reduce_everywhere(): lax.all_to_all(jnp.broadcast_to(own[None], (devices, slice_rows, LANES)),...]
    pallas_call x1, Pallas kernels: 34.6 us -> 37.5 us  [run_backward(): pl.pallas_call(backward_kernel, name='backward', out_shape=outs, grid_spe...]
    ppermute x0 -> x2, waiting for transfers between devices: none -> 2.74 us  [the longest x1 2.12 us: reduce_everywhere(): got = lax.ppermute(send, 'core', swap)]
  transfers between devices with their start and end apart: 2 -> 3, of which waited for: 2 -> 3; matrix products, arithmetic and copies ran while one was open for 3% -> 3% of each run, Pallas kernels for 0% -> 0%
where the time goes in v3:
time: 159 us
  Pallas kernels  86.9 us (55%)
  blocking collectives  40.8 us (26%)
  starting transfers between devices  13.8 us (9%)
  waiting for transfers between devices  7.58 us (5%)
  local copies, waits for them, and re-layouts  5.23 us (3%)
  other arithmetic  3.57 us (2%)
    pallas_call x1, Pallas kernels, run_forward(): pl.pallas_call(forward_kernel, name='forward', out_shape=[o[0] for o in o...  44 us
    pallas_call x1, Pallas kernels, run_backward(): pl.pallas_call(backward_kernel, name='backward', out_shape=outs, grid_spe...  37.5 us
    all_to_all x1, blocking collectives, reduce_everywhere(): parts = lax.all_to_all(pair.reshape(peers, SLICE, LANES), axes, 0, 0)  21.9 us
    all_to_all x1, blocking collectives, reduce_everywhere(): mine = lax.all_to_all(spread, axes, 0, 0).reshape(peers * SLICE, LANES)  18.9 us
    all_to_all x1, starting transfers between devices, local(): gathered = lax.all_to_all(spread, 'neg', 0, 0).reshape(N_NEG * count, -1)  8.61 us
    all_to_all x1, waiting for transfers between devices, local(): gathered = lax.all_to_all(spread, 'neg', 0, 0).reshape(N_NEG * count, -1)  4.84 us
    pallas_call x1, Pallas kernels, reduce_everywhere(): pl.pallas_call(unpack_kernel, name='unpack', in_specs=[pl.BlockSpec(memor...  3.21 us
  transfers between devices with their start and end apart: 3, of which 3 were waited for; matrix products, arithmetic and copies ran while one was open for 3% of the time, Pallas kernels for 0%

profile of v3, /device:TPU:1, one launch (start us, length us, event | category | flops | bytes accessed | tf_op | source)
XLA Modules:
  0.0 158.6 jit_solution(17323256326988093725)
XLA Ops:
  0.6 0.0 slice-start
  0.7 0.9 convert_reduce_fusion
  1.5 0.7 pad_add_fusion.lengths.scalars
  2.2 44.0 %forward.1 = (bf16[40,128,1536]{2,1,0:T(8,128)(2,1)}, bf16[40,128,512]{2,1,0:T(8,128)(2,1)}, bf16[40,128,512]{2,1,0:T(8,128)(2,1)}, bf16[40,128,512]{2,1,0:T(8,1...) custom-call(s32[42]{0:T(128)} %pad_add_fusion.lengths.scalars, ...), custom_call_target="tpu_custom_call" | custom-call | tf_op jit(solution)/shard_map/forward/pallas_call | solution.py:457
  46.2 8.6 %all-to-all-start = ((bf16[16,40,256]{2,1,0:T(8,128)(2,1)}), bf16[16,40,256]{2,1,0:T(8,128)(2,1)S(1)}, u32[]{:S(2)}, u32[]{:S(2)}) async-start(bf16[16,40,256]{2,1,0:T(8,128)(2,1)} %get-tuple-element.20), calls=%async_computation | async-start | bytes 655360 | tf_op jit(solution)/shard_map/all_to_all | solution.py:592
  54.8 0.5 broadcast.32
  55.3 0.7 reduce.5
  56.0 0.1 squeeze.15
  56.1 0.7 reshape.25.column_target_ref
  56.8 1.0 copy.16
  57.8 4.8 %all-to-all-done = bf16[16,40,256]{2,1,0:T(8,128)(2,1)S(1)} async-done(((bf16[16,40,256]{2,1,0:T(8,128)(2,1)}), bf16[16,40,256]{2,1,0:T(8,128)(2,1)S(1)}, u32[]{:S(2)}, u32[]{:S(2)}) %all-to-all-start) | async-done | bytes 327712 | tf_op jit(solution)/shard_map/all_to_all | solution.py:592
  62.6 0.7 copy-done.1
  63.4 37.5 %backward.1 = (f32[40,128]{1,0:T(8,128)}, bf16[3072,128]{1,0:T(8,128)(2,1)}, bf16[3072,128]{1,0:T(8,128)(2,1)}) custom-call(s32[42]{0:T(128)} %pad_add_fusion.lengths.scalars, bf16[640,256]{1,0:T(8,128)(2,1)} %bitcast.17, f32[40,896]{1,0:T(8,128)} %get-tuple-element.21.summary_ref, s32[1,640]{1,0:T(1,128)} %reshape.25.column_target_ref, ...), custom_call_target="tpu_custom_call" | custom-call | tf_op jit(solution)/shard_map/backward/pallas_call | solution.py:506
  100.9 2.3 %collective-permute-start = (bf16[3072,128]{1,0:T(8,128)(2,1)}, bf16[3072,128]{1,0:T(8,128)(2,1)S(1)}, u32[]{:S(2)}, u32[]{:S(2)}) collective-permute-start(bf16[3072,128]{1,0:T(8,128)(2,1)} %get-tuple-element.30), channel_id=1, source_target_pairs={{0,1},{1,0},{2,3},{3,2},{4,5},{5,4},{6,7},{7,6},{8,9},{9,8},{10,11... | collective-permute-start | bytes 2359304 | tf_op jit(solution)/shard_map/ppermute | solution.py:537
  103.2 2.1 %collective-permute-done = bf16[3072,128]{1,0:T(8,128)(2,1)S(1)} collective-permute-done((bf16[3072,128]{1,0:T(8,128)(2,1)}, bf16[3072,128]{1,0:T(8,128)(2,1)S(1)}, u32[]{:S(2)}, u32[]{:S(2)}) %collective-permute-start) | collective-permute-done | bytes 786464 | tf_op jit(solution)/shard_map/ppermute | solution.py:537
  105.3 1.3 add_convert_fusion
  106.7 21.9 %all_to_all.15.parts_ref = bf16[64,48,128]{2,1,0:T(8,128)(2,1)} all-to-all(bf16[64,48,128]{2,1,0:T(8,128)(2,1)S(1)} %bitcast.15), channel_id=1, replica_groups=mesh['neg'=16,'chip'=4,'core'=2] {'neg','chip'}, dimensions={0} | all-to-all | bytes 1572864 | tf_op jit(solution)/shard_map/all_to_all | solution.py:539
  128.6 2.2 %spread.1 = bf16[64,48,128]{2,1,0:T(8,128)(2,1)} custom-call(bf16[64,48,128]{2,1,0:T(8,128)(2,1)} %all_to_all.15.parts_ref), custom_call_target="tpu_custom_call" | custom-call | tf_op jit(solution)/shard_map/spread/pallas_call | solution.py:540
  130.7 18.9 %all_to_all.16 = bf16[64,48,128]{2,1,0:T(8,128)(2,1)S(1)} all-to-all(bf16[64,48,128]{2,1,0:T(8,128)(2,1)} %spread.1), channel_id=1, replica_groups=mesh['neg'=16,'chip'=4,'core'=2] {'neg','chip'}, dimensions={0} | all-to-all | bytes 1572864 | tf_op jit(solution)/shard_map/all_to_all | solution.py:543
  149.7 2.9 %collective-permute-start.1 = (bf16[3072,128]{1,0:T(8,128)(2,1)S(1)}, bf16[3072,128]{1,0:T(8,128)(2,1)S(1)}, u32[]{:S(2)}, u32[]{:S(2)}) collective-permute-start(bf16[3072,128]{1,0:T(8,128)(2,1)S(1)} %bitcast.13), channel_id=1, source_target_pairs={{0,1},{1,0},{2,3},{3,2},{4,5},{5,4},{6,7},{7,6},{8,9},{9,8},{10,11... | collective-permute-start | bytes 2359304 | tf_op jit(solution)/shard_map/ppermute | solution.py:544
  152.6 1.3 slice_reduce_fusion
  153.9 0.6 collective-permute-done.1.other_ref
  154.5 0.9 copy-done.2
  155.4 3.2 %unpack.1 = (f32[3,2,512]{2,1,0:T(2,128)}, f32[2,512]{1,0:T(2,128)}, f32[2,512,512]{2,1,0:T(8,128)}, f32[512,256]{1,0:T(8,128)}) custom-call(s32[42]{0:T(128)} %pad_add_fusion.lengths.scalars, bf16[3072,128]{1,0:T(8,128)(2,1)} %bitcast.14, bf16[3072,128]{1,0:T(8,128)(2,1)} %copy-done.2, f32[3,2,512]{2,1,0:T(2,128)} %bitcast.20, f32[2,512]{1,0:T(2,128)} %gain_ref.5), custom_call_target="tpu_custom_call" | custom-call | tf_op jit(solution)/shard_map/unpack/pallas_call | solution.py:546
  (9 shorter events, 0.0 us)
Async XLA Ops:
  0.6 56.2 %slice-start = ((bf16[2,512,512]{2,1,0:T(8,128)(2,1)}), bf16[1,512,512]{2,1,0:T(8,128)(2,1)S(1)}, s32[]{:S(2)}) async-start(bf16[2,512,512]{2,1,0:T(8,128)(2,1)} %weight_ref.3), calls=%async_computation.3 | async-start | bytes 1048576 | tf_op jit(solution)/shard_map/slice | solution.py:609
  0.6 54.7 %copy-start.3 = (s32[1,128]{1,0:T(1,128)S(1)}, s32[1,128]{1,0:T(1,128)}, u32[]{:S(2)}) copy-start(s32[1,128]{1,0:T(1,128)} %param.13) | copy-start | bytes 1540
  46.2 16.4 %all-to-all-start = ((bf16[16,40,256]{2,1,0:T(8,128)(2,1)}), bf16[16,40,256]{2,1,0:T(8,128)(2,1)S(1)}, u32[]{:S(2)}, u32[]{:S(2)}) async-start(bf16[16,40,256]{2,1,0:T(8,128)(2,1)} %get-tuple-element.20), calls=%async_computation | async-start | bytes 655360 | tf_op jit(solution)/shard_map/all_to_all | solution.py:592
  62.6 0.7 copy-start.1
  100.9 4.4 %collective-permute-start = (bf16[3072,128]{1,0:T(8,128)(2,1)}, bf16[3072,128]{1,0:T(8,128)(2,1)S(1)}, u32[]{:S(2)}, u32[]{:S(2)}) collective-permute-start(bf16[3072,128]{1,0:T(8,128)(2,1)} %get-tuple-element.30), channel_id=1, source_target_pairs={{0,1},{1,0},{2,3},{3,2},{4,5},{5,4},{6,7},{7,6},{8,9},{9,8},{10,11... | collective-permute-start | bytes 2359304 | tf_op jit(solution)/shard_map/ppermute | solution.py:537
  149.7 4.8 %copy-start = (bf16[64,48,128]{2,1,0:T(8,128)(2,1)}, bf16[64,48,128]{2,1,0:T(8,128)(2,1)S(1)}, u32[]{:S(2)}) copy-start(bf16[64,48,128]{2,1,0:T(8,128)(2,1)S(1)} %all_to_all.16) | copy-start | bytes 2359300
  149.7 4.8 %collective-permute-start.1 = (bf16[3072,128]{1,0:T(8,128)(2,1)S(1)}, bf16[3072,128]{1,0:T(8,128)(2,1)S(1)}, u32[]{:S(2)}, u32[]{:S(2)}) collective-permute-start(bf16[3072,128]{1,0:T(8,128)(2,1)S(1)} %bitcast.13), channel_id=1, source_target_pairs={{0,1},{1,0},{2,3},{3,2},{4,5},{5,4},{6,7},{7,6},{8,9},{9,8},{10,11... | collective-permute-start | bytes 2359304 | tf_op jit(solution)/shard_map/ppermute | solution.py:544
  154.5 0.9 copy-start.2

commit v4 on v3

--- a/solution.py
+++ b/solution.py
@@ -15,7 +15,10 @@
 LANES = 128
 PAD = 8
 TILE = 16
-SEQS = 4
+CHUNK = 512
+PART = 64
+SUB = 256
+EDGE = 16
 SLICE = 48
 EPS = 1e-06
 GELU_C = 0.7978845608028654
@@ -35,148 +38,235 @@
     return value, slope
 
 
+def table_of(scalars, start, count, shape, axis):
+    place = lax.broadcasted_iota(jnp.int32, shape, axis)
+    table = jnp.zeros(shape, jnp.int32)
+    for seq in range(count):
+        table = jnp.where(lax.rem(place, count) == seq, scalars[start + seq], table)
+    return table
+
+
+def last_chunk(scalars, count):
+    return (scalars[2 * count] + CHUNK - 1) // CHUNK - 1
+
+
+def wide(column):
+    return jnp.concatenate([column] * 4, axis=1)
+
+
 def forward_kernel(
-    lengths,
+    scalars,
     goal_ref,
     premise_ref,
     depth_ref,
     gain_ref,
     weight_ref,
     head_ref,
-    shifted_ref,
+    normed_low_ref,
     slope_low_ref,
     normed_up_ref,
+    inverse_ref,
     mixed_up_ref,
     slope_up_ref,
-    inverse_ref,
     summary_ref,
     spread_ref,
+    arrived,
     states,
-    padded,
+    valid_rows,
+    padded_low,
+    padded_up,
+    hidden,
     mixed,
+    squares,
     pre_act,
-    hidden,
+    pooling,
     mix_gain,
+    semaphores,
 ):
     step = pl.program_id(0)
-    length, width = states.shape[1], states.shape[2]
-    tiles = range(0, length, TILE)
-    rows = lax.broadcasted_iota(jnp.int32, (TILE, 1), 0)
+    goals, premises = goal_ref.shape[1], premise_ref.shape[1]
+    count = goals + premises
+    length, width = arrived.shape[1:]
+    last = last_chunk(scalars, count)
+    row_of = lax.broadcasted_iota(jnp.int32, (PART, LANES), 0)
+    ones = jnp.ones((width, LANES), BF16)
 
     @pl.when(step == 0)
     def _():
-        zeros = jnp.zeros((SEQS, PAD, width), F32)
-        padded[:, :PAD, :] = zeros
-        padded[:, PAD + length :, :] = zeros
-        mix_gain[...] = depth_ref[...] * gain_ref[...]
-
-    def norm(values, valid):
-        mean = jnp.mean(values * values, axis=-1, keepdims=True)
-        inverse = jnp.where(valid, lax.rsqrt(mean + EPS), 0.0)
-        return values * inverse, inverse
-
-    def norm_inputs(source):
-        def body(seq, carry):
-            count = lengths[step * SEQS + seq]
-            for start in tiles:
-                raw = source[0, seq, pl.ds(start, TILE), :]
-                states[seq, pl.ds(start, TILE), :] = raw
-                normed, _ = norm(raw.astype(F32), rows < count - start)
-                padded[seq, pl.ds(PAD + start, TILE), :] = normed
+        for group in range(count // goals):
+            source = goal_ref.at[0] if group == 0 else premise_ref.at[
+                0, pl.ds((group - 1) * goals, goals)
+            ]
+            pltpu.make_async_copy(
+                source, arrived.at[pl.ds(group * goals, goals)], semaphores.at[group]
+            ).start()
+        end = (last + 1) * CHUNK
+        edge = jnp.zeros((EDGE, width), BF16)
+        padded_low[:EDGE, :] = edge
+        padded_up[:EDGE, :] = edge
+        padded_up[pl.ds(pl.multiple_of(EDGE + end, EDGE), EDGE), :] = edge
+        padded_low[pl.ds(pl.multiple_of(EDGE + end, EDGE), EDGE), :] = edge
+        mix_gain[...] = (depth_ref[...] * gain_ref[...]).astype(BF16)
+        summary_ref[...] = jnp.zeros_like(summary_ref)
+        pooling[0] = table_of(scalars, 0, count, (count, 1), 0)
+        pooling[1] = table_of(scalars, count, count, (count, 1), 0)
+
+        def clear(at):
+            at = pl.multiple_of(at, TILE)
+            states[pl.ds(at, TILE), :] = jnp.zeros((TILE, width), BF16)
+            valid_rows[pl.ds(at, TILE), :] = jnp.zeros((TILE, LANES), F32)
+
+        def one_sequence(seq, carry):
+            @pl.when(lax.rem(seq, goals) == 0)
+            def _():
+                pltpu.make_async_copy(
+                    goal_ref.at[0],
+                    arrived.at[pl.ds(seq, goals)],
+                    semaphores.at[lax.div(seq, goals)],
+                ).wait()
+
+            used, offset = scalars[seq], scalars[count + seq]
+
+            def part(index, carry):
+                start = pl.multiple_of(index * PART, PART)
+                at = pl.ds(pl.multiple_of(offset + start, TILE), PART)
+                states[at, :] = arrived[seq, pl.ds(start, PART), :]
+                valid_rows[at, :] = jnp.where(row_of < used - start, 1.0, 0.0)
+                return carry
+
+            parts = (used + PART - 1) // PART
+            lax.fori_loop(0, parts, part, 0)
+            clear(offset + parts * PART)
             return carry
 
-        lax.fori_loop(0, SEQS, body, 0)
-
-    goal_steps = goal_total // SEQS
-
-    @pl.when(step < goal_steps)
-    def _():
-        norm_inputs(goal_ref)
-
-    @pl.when(step >= goal_steps)
-    def _():
-        norm_inputs(premise_ref)
-
-    def mix_low(seq, carry):
-        for start in tiles:
-            window = [
-                padded[seq, pl.ds(PAD + start + tap * LOWER_DILATION, TILE), :]
-                for tap in (-1, 0, 1)
-            ]
-            total = 0.0
-            for tap in range(3):
-                total = total + mix_gain[tap, 0:1, :] * window[tap]
-                shifted_ref[seq, pl.ds(start, TILE), tap * width : (tap + 1) * width] = (
-                    window[tap].astype(BF16)
-                )
-            mixed[seq, pl.ds(start, TILE), :] = total.astype(BF16)
-        return carry
-
-    lax.fori_loop(0, SEQS, mix_low, 0)
-    pre_act[...] = jnp.dot(
-        mixed[...].reshape(SEQS * length, width), weight_ref[0], preferred_element_type=F32
-    ).reshape(SEQS, length, width)
-
-    def act_low(seq, carry):
-        count = lengths[step * SEQS + seq]
-        for start in tiles:
-            at = pl.ds(start, TILE)
-            value, slope = gelu_parts(pre_act[seq, at, :])
-            slope_low_ref[seq, at, :] = slope.astype(BF16)
-            out = states[seq, at, :].astype(F32) + value
-            hidden[seq, at, :] = out
-            normed, inverse = norm(out, rows < count - start)
-            padded[seq, pl.ds(PAD + start, TILE), :] = normed
-            normed_up_ref[seq, at, :] = normed.astype(BF16)
-            inverse_ref[seq, at, :] = jnp.broadcast_to(inverse, (TILE, LANES))
-        return carry
-
-    lax.fori_loop(0, SEQS, act_low, 0)
-
-    def mix_up(seq, carry):
-        for start in tiles:
-            at = pl.ds(start, TILE)
-            total = 0.0
-            for tap in range(3):
-                total = total + mix_gain[tap, 1:2, :] * (
-                    padded[seq, pl.ds(PAD + start + (tap - 1) * UPPER_DILATION, TILE), :]
-                )
-            mixed_up_ref[seq, at, :] = total.astype(BF16)
-        return carry
-
-    lax.fori_loop(0, SEQS, mix_up, 0)
-    pre_act[...] = jnp.dot(
-        mixed_up_ref[...].reshape(SEQS * length, width),
-        weight_ref[1],
-        preferred_element_type=F32,
-    ).reshape(SEQS, length, width)
-
-    def act_up(seq, carry):
-        count = lengths[step * SEQS + seq]
-        pooled = jnp.zeros((TILE, width), F32)
-        for start in tiles:
-            at = pl.ds(start, TILE)
-            valid = rows < count - start
-            value, slope = gelu_parts(pre_act[seq, at, :])
-            slope_up_ref[seq, at, :] = jnp.where(valid, slope, 0.0).astype(BF16)
-            pooled = pooled + jnp.where(valid, hidden[seq, at, :] + value, 0.0)
-        summary_ref[pl.ds(step * SEQS + seq, 1), :width] = (
-            jnp.sum(pooled, axis=0, keepdims=True) / count.astype(F32)
-        )
-        return carry
-
-    lax.fori_loop(0, SEQS, act_up, 0)
+        lax.fori_loop(0, count, one_sequence, 0)
+
+        def clear_tail(tile, carry):
+            clear(scalars[2 * count] + tile * TILE)
+            return carry
+
+        lax.fori_loop(0, (end - scalars[2 * count]) // TILE, clear_tail, 0)
+
+    def staged(first, second):
+        for block in range(0, CHUNK + SUB, SUB):
+            if block < CHUNK:
+                first(block)
+            if block:
+                second(block - SUB)
+
+    def rows_of(block):
+        return range(block, block + SUB, TILE)
+
+    def window_of(padded, base, start):
+        return padded[pl.ds(pl.multiple_of(base + start, TILE), TILE + 2 * EDGE), :]
+
+    def inverse_of(base, block):
+        mean = jnp.dot(
+            squares[block : block + SUB, :], ones, preferred_element_type=F32
+        ) * (1.0 / width)
+        place = pl.ds(pl.multiple_of(base + block, TILE), SUB)
+        return (lax.rsqrt(mean + EPS) * valid_rows[place, :]).astype(BF16)
+
+    @pl.when(step <= last)
+    def _():
+        base = step * CHUNK
+
+        def square(block):
+            raw = states[pl.ds(pl.multiple_of(base + block, TILE), SUB), :]
+            squares[block : block + SUB, :] = raw * raw
+
+        def scale(block):
+            inverse = wide(inverse_of(base, block))
+            raw = states[pl.ds(pl.multiple_of(base + block, TILE), SUB), :]
+            padded_low[pl.ds(pl.multiple_of(EDGE + base + block, EDGE), SUB), :] = raw * inverse
+
+        staged(square, scale)
+
+    @pl.when((step >= 1) & (step <= last + 1))
+    def _():
+        base = (step - 1) * CHUNK
+        slot = lax.rem(step + 1, 2)
+
+        def mix_low(block):
+            for start in rows_of(block):
+                window = window_of(padded_low, base, start)
+                at = pl.ds(start, TILE)
+                total = None
+                for tap in range(3):
+                    first = EDGE + (tap - 1) * LOWER_DILATION
+                    values = window[first : first + TILE]
+                    term = mix_gain[tap, 0:1, :] * values
+                    total = term if total is None else total + term
+                    if tap == 1:
+                        normed_low_ref[at, :] = values
+                mixed[at, :] = total
+            at = pl.ds(block, SUB)
+            pre_act[at, :] = jnp.dot(
+                mixed[at, :], weight_ref[0], preferred_element_type=F32
+            ).astype(BF16)
+
+        def act_low(block):
+            for start in rows_of(block):
+                at = pl.ds(start, TILE)
+                place = pl.ds(pl.multiple_of(base + start, TILE), TILE)
+                value, slope = gelu_parts(pre_act[at, :])
+                slope_low_ref[at, :] = slope
+                out = states[place, :] + value
+                hidden[slot, at, :] = out
+                squares[at, :] = out * out
+            at = pl.ds(block, SUB)
+            inverse = inverse_of(base, block)
+            inverse_ref[at, :] = inverse
+            normed = hidden[slot, at, :] * wide(inverse)
+            padded_up[pl.ds(pl.multiple_of(EDGE + base + block, EDGE), SUB), :] = normed
+            normed_up_ref[at, :] = normed
+
+        staged(mix_low, act_low)
+
+    @pl.when((step >= 2) & (step <= last + 2))
+    def _():
+        base = (step - 2) * CHUNK
+        slot = lax.rem(step, 2)
+
+        def mix_up(block):
+            for start in rows_of(block):
+                window = window_of(padded_up, base, start)
+                total = None
+                for tap in range(3):
+                    first = EDGE + (tap - 1) * UPPER_DILATION
+                    term = mix_gain[tap, 1:2, :] * window[first : first + TILE]
+                    total = term if total is None else total + term
+                mixed_up_ref[pl.ds(start, TILE), :] = total
+            at = pl.ds(block, SUB)
+            pre_act[at, :] = jnp.dot(
+                mixed_up_ref[at, :], weight_ref[1], preferred_element_type=F32
+            ).astype(BF16)
+
+        def act_up(block):
+            for start in rows_of(block):
+                at = pl.ds(start, TILE)
+                value, slope = gelu_parts(pre_act[at, :])
+                slope_up_ref[at, :] = slope
+                mixed[at, :] = hidden[slot, at, :] + value
+
+        staged(mix_up, act_up)
+        place = base + lax.broadcasted_iota(jnp.int32, (count, CHUNK), 1)
+        begin = pooling[1]
+        member = (place >= begin) & (place < begin + pooling[0])
+        summary_ref[:, :width] += jnp.dot(
+            jnp.where(member, 1.0, 0.0).astype(BF16), mixed[...], preferred_element_type=F32
+        )
 
     @pl.when(step == pl.num_programs(0) - 1)
     def _():
-        embedded = jnp.dot(
-            summary_ref[:, :width].astype(BF16), head_ref[...], preferred_element_type=F32
-        )
+        pooled = summary_ref[:, :width] / pooling[0].astype(F32)
+        summary_ref[:, :width] = pooled
+        embedded = jnp.dot(pooled.astype(BF16), head_ref[...], preferred_element_type=F32)
         magnitude = jnp.sqrt(jnp.sum(embedded * embedded, axis=-1, keepdims=True) + EPS)
         unit = embedded / magnitude
         embed = unit.shape[1]
         summary_ref[:, width : width + embed] = unit
-        summary_ref[:, width + embed :] = jnp.broadcast_to(magnitude, (unit.shape[0], LANES))
+        summary_ref[:, width + embed :] = jnp.broadcast_to(magnitude, (count, LANES))
         rounded = unit.astype(BF16)
         for peer in range(N_NEG):
             spread_ref[peer] = rounded
@@ -192,36 +282,57 @@
     gain_ref,
     weight_ref,
     weight_turned_ref,
-    shifted_ref,
+    normed_low_ref,
     slope_low_ref,
     normed_up_ref,
+    inverse_ref,
     mixed_up_ref,
     slope_up_ref,
-    inverse_ref,
     loss_ref,
     keep_ref,
     send_ref,
+    pooled_grad,
+    members,
     upstream,
-    act_grad,
+    grad_up,
+    grad_low,
     conv_grad,
+    normed_low,
+    shifted,
+    scaled,
+    products,
     corr,
     point_up,
     moments,
     head_grad,
     mix_gain,
+    mix_half,
+    semaphore,
 ):
     step = pl.program_id(0)
     last = pl.num_programs(0) - 1
     count = summary_ref.shape[0]
-    position, core = scalars[count], scalars[count + 1]
-    length, width = act_grad.shape[1], act_grad.shape[2]
-    tiles = range(0, length, TILE)
+    position, core = scalars[2 * count + 1], scalars[2 * count + 2]
+    width = grad_up.shape[1]
+    rows = normed_low_ref.shape[0]
+    final = last_chunk(scalars, count)
+
+    after = pl.multiple_of(EDGE + (final + 1) * CHUNK, EDGE)
+
+    def load_normed():
+        return pltpu.make_async_copy(
+            normed_low_ref, normed_low.at[pl.ds(EDGE, rows)], semaphore.at[0]
+        )
 
     @pl.when(step == 0)
     def _():
-        zeros = jnp.zeros((SEQS, PAD, width), F32)
-        conv_grad[:, :PAD, :] = zeros
-        conv_grad[:, PAD + length :, :] = zeros
+        load_normed().start()
+        zeros = jnp.zeros((EDGE, width), BF16)
+        conv_grad[:EDGE, :] = zeros
+        conv_grad[pl.ds(after, EDGE), :] = zeros
+        mix_half[...] = (depth_ref[...] * gain_ref[...]).astype(BF16)
+        members[0] = table_of(scalars, 0, count, (8, count), 1)
+        members[1] = table_of(scalars, count, count, (8, count), 1)
         corr[...] = jnp.zeros_like(corr)
         point_up[...] = jnp.zeros_like(point_up)
         moments[...] = jnp.zeros_like(moments)
@@ -276,59 +387,90 @@
             (((0,), (0,)), ((), ())),
             preferred_element_type=F32,
         ).astype(BF16)
-        upstream[...] = lax.dot_general(
+        used = table_of(scalars, 0, count, (count, 1), 0)
+        spread_back = lax.dot_general(
             embed_grad, head_ref[...], contract, preferred_element_type=F32
-        )
-
-    def grad_up(seq, carry):
-        row = pl.ds(step * SEQS + seq, 1)
-        above = upstream[row, :] / scalars[step * SEQS + seq].astype(F32)
-        upstream[row, :] = above
-        for start in tiles:
-            at = pl.ds(start, TILE)
-            act_grad[seq, at, :] = (slope_up_ref[seq, at, :].astype(F32) * above).astype(BF16)
-        return carry
-
-    lax.fori_loop(0, SEQS, grad_up, 0)
-    flat = act_grad[...].reshape(SEQS * length, width)
-    conv_grad[:, PAD : PAD + length, :] = lax.dot_general(
-        flat, weight_ref[0], (((1,), (1,)), ((), ())), preferred_element_type=F32
-    ).reshape(SEQS, length, width)
+        ) / used.astype(F32)
+        pooled_grad[...] = spread_back.astype(BF16)
+
     over_tokens = (((0,), (0,)), ((), ()))
-    point_up[...] += lax.dot_general(
-        mixed_up_ref[...].reshape(SEQS * length, width),
-        flat,
-        over_tokens,
-        preferred_element_type=F32,
-    )
-
-    def norm_up(seq, carry):
-        above = upstream[pl.ds(step * SEQS + seq, 1), :]
-        sums = [corr[tap] for tap in range(3)]
-        for start in tiles:
-            at = pl.ds(start, TILE)
-            normed = normed_up_ref[seq, at, :].astype(F32)
-            inverse = inverse_ref[seq, at, :][:, :1]
-            scaled = 0.0
-            for tap in range(3):
-                part = conv_grad[seq, pl.ds(PAD + start + (1 - tap) * UPPER_DILATION, TILE), :]
-                scaled = scaled + mix_gain[tap, 1:2, :] * part
-                product = part * normed
-                sums[tap] = sums[tap] + product[:8] + product[8:]
-            mean = jnp.mean(scaled * normed, axis=-1, keepdims=True)
-            below = jnp.where(inverse > 0.0, above, 0.0) + inverse * (scaled - normed * mean)
-            act_grad[seq, at, :] = (below * slope_low_ref[seq, at, :].astype(F32)).astype(BF16)
+    blocks = range(0, CHUNK, SUB)
+
+    @pl.when(step == 1)
+    def _():
+        load_normed().wait()
+        zeros = jnp.zeros((EDGE, width), BF16)
+        normed_low[:EDGE, :] = zeros
+        normed_low[pl.ds(after, EDGE), :] = zeros
+
+    @pl.when(step <= final)
+    def _():
+        base = step * CHUNK
+        slot = lax.rem(step, 2)
+        begin = members[1, 0:1, :]
+        end = begin + members[0, 0:1, :]
+        for block in blocks:
+            at = pl.ds(block, SUB)
+            place = base + block + lax.broadcasted_iota(jnp.int32, (SUB, count), 0)
+            member = jnp.where((place >= begin) & (place < end), 1.0, 0.0).astype(BF16)
+            above = jnp.dot(member, pooled_grad[...], preferred_element_type=F32).astype(BF16)
+            upstream[slot, at, :] = above
+            grad = slope_up_ref[at, :] * above
+            grad_up[at, :] = grad
+            conv_grad[pl.ds(pl.multiple_of(EDGE + base + block, EDGE), SUB), :] = (
+                lax.dot_general(
+                    grad, weight_ref[0], (((1,), (1,)), ((), ())), preferred_element_type=F32
+                ).astype(BF16)
+            )
+        point_up[...] += lax.dot_general(
+            mixed_up_ref[...], grad_up[...], over_tokens, preferred_element_type=F32
+        )
+
+    @pl.when((step >= 1) & (step <= final + 1))
+    def _():
+        base = (step - 1) * CHUNK
+        slot = lax.rem(step + 1, 2)
+        ones = jnp.ones((width, LANES), BF16)
+
+        def mix(block):
+            for start in range(block, block + SUB, TILE):
+                at = pl.ds(start, TILE)
+                place = pl.ds(pl.multiple_of(base + start, TILE), TILE + 2 * EDGE)
+                window = conv_grad[place, :]
+                states = normed_low[place, :]
+                normed = normed_up_ref[at, :]
+                total = None
+                for tap in range(3):
+                    first = EDGE + (1 - tap) * UPPER_DILATION
+                    part = window[first : first + TILE]
+                    term = mix_half[tap, 1:2, :] * part
+                    total = term if total is None else total + term
+                    products[tap, at, :] = part * normed
+                    first = EDGE + (tap - 1) * LOWER_DILATION
+                    shifted[at, tap * width : (tap + 1) * width] = states[first : first + TILE]
+                scaled[at, :] = total
+                products[3, at, :] = total * normed
+
+        def back(block):
+            at = pl.ds(block, SUB)
+            mean = (
+                jnp.dot(products[3, at, :], ones, preferred_element_type=F32) * (1.0 / width)
+            ).astype(BF16)
+            inner = scaled[at, :] - normed_up_ref[at, :] * wide(mean)
+            below = upstream[slot, at, :] + wide(inverse_ref[at, :]) * inner
+            grad_low[at, :] = below * slope_low_ref[at, :]
+
+        for block in range(0, CHUNK + SUB, SUB):
+            if block < CHUNK:
+                mix(block)
+            if block:
+                back(block - SUB)
+        every_row = jnp.ones((8, CHUNK), BF16)
         for tap in range(3):
-            corr[tap] = sums[tap]
-        return carry
-
-    lax.fori_loop(0, SEQS, norm_up, 0)
-    moments[...] += lax.dot_general(
-        act_grad[...].reshape(SEQS * length, width),
-        shifted_ref[...].reshape(SEQS * length, 3 * width),
-        over_tokens,
-        preferred_element_type=F32,
-    )
+            corr[tap] += jnp.dot(every_row, products[tap], preferred_element_type=F32)
+        moments[...] += lax.dot_general(
+            grad_low[...], shifted[...], over_tokens, preferred_element_type=F32
+        )
 
     def emit(low_ref, up_ref):
         point, rows = 0.0, []
@@ -338,7 +480,7 @@
                 jnp.sum(part * weight_turned_ref[...].astype(F32), axis=0, keepdims=True)
             )
             point = point + mix_gain[tap, 0:1, :] * part
-        rows += [jnp.sum(corr[tap], axis=0, keepdims=True) for tap in range(3)]
+        rows += [corr[tap, 0:1, :] for tap in range(3)]
         rows.append(jnp.zeros((2, width), F32))
         small = jnp.concatenate(rows, axis=0)
         low = point.T.astype(BF16)
@@ -429,47 +571,48 @@
     return pl.BlockSpec(shape, lambda i, *_: (0,) * len(shape))
 
 
-def chunk(length, width):
-    return pl.BlockSpec((SEQS, length, width), lambda i, *_: (i, 0, 0))
-
-
 def run_forward(scalars, goal_states, premise_states, depth, gains, weights, head_weight):
     goals, length, width = goal_states.shape[1:]
     premises = premise_states.shape[1]
     count = goals + premises
     embed = head_weight.shape[1]
-    goal_steps = goals // SEQS
-    tokens = lambda w, t: jax.ShapeDtypeStruct((count, length, w), t)
+    chunks = -(-count * (length + TILE) // CHUNK)
+    rows = chunks * CHUNK
     summary = (count, width + embed + LANES)
+
+    def lower(columns):
+        return pl.BlockSpec(
+            (CHUNK, columns), lambda i, s: (jnp.clip(i - 1, 0, last_chunk(s, count)), 0)
+        )
+
+    upper = pl.BlockSpec(
+        (CHUNK, width), lambda i, s: (jnp.clip(i - 2, 0, last_chunk(s, count)), 0)
+    )
+    packed = jax.ShapeDtypeStruct((rows, width), BF16)
     outs = [
-        (tokens(3 * width, BF16), chunk(length, 3 * width)),
-        (tokens(width, BF16), chunk(length, width)),
-        (tokens(width, BF16), chunk(length, width)),
-        (tokens(width, BF16), chunk(length, width)),
-        (tokens(width, BF16), chunk(length, width)),
-        (tokens(LANES, F32), chunk(length, LANES)),
+        (packed, lower(width)),
+        (packed, lower(width)),
+        (packed, lower(width)),
+        (jax.ShapeDtypeStruct((rows, LANES), BF16), lower(LANES)),
+        (packed, upper),
+        (packed, upper),
         (jax.ShapeDtypeStruct(summary, F32), whole(summary)),
         (
             jax.ShapeDtypeStruct((N_NEG, count, embed), BF16),
             whole((N_NEG, count, embed)),
         ),
     ]
+    raw = pl.BlockSpec(memory_space=pl.ANY)
     return pl.pallas_call(
         forward_kernel,
         name="forward",
         out_shape=[o[0] for o in outs],
         grid_spec=pltpu.PrefetchScalarGridSpec(
             num_scalar_prefetch=1,
-            grid=(count // SEQS,),
+            grid=(chunks + 2,),
             in_specs=[
-                pl.BlockSpec(
-                    (1, SEQS, length, width),
-                    lambda i, *_: (0, jnp.minimum(i, goal_steps - 1), 0, 0),
-                ),
-                pl.BlockSpec(
-                    (1, SEQS, length, width),
-                    lambda i, *_: (0, jnp.maximum(i - goal_steps, 0), 0, 0),
-                ),
+                raw,
+                raw,
                 whole(depth.shape),
                 whole(gains.shape),
                 whole(weights.shape),
@@ -477,12 +620,18 @@
             ],
             out_specs=[o[1] for o in outs],
             scratch_shapes=[
-                pltpu.VMEM((SEQS, length, width), BF16),
-                pltpu.VMEM((SEQS, length + 2 * PAD, width), F32),
-                pltpu.VMEM((SEQS, length, width), BF16),
-                pltpu.VMEM((SEQS, length, width), F32),
-                pltpu.VMEM((SEQS, length, width), F32),
-                pltpu.VMEM(depth.shape, F32),
+                pltpu.VMEM((count, length, width), BF16),
+                pltpu.VMEM((rows + PART + TILE, width), BF16),
+                pltpu.VMEM((rows + PART + TILE, LANES), F32),
+                pltpu.VMEM((rows + 2 * EDGE, width), BF16),
+                pltpu.VMEM((rows + 2 * EDGE, width), BF16),
+                pltpu.VMEM((2, CHUNK, width), BF16),
+                pltpu.VMEM((CHUNK, width), BF16),
+                pltpu.VMEM((CHUNK, width), BF16),
+                pltpu.VMEM((CHUNK, width), BF16),
+                pltpu.VMEM((2, count, 1), jnp.int32),
+                pltpu.VMEM(depth.shape, BF16),
+                pltpu.SemaphoreType.DMA((count // goals,)),
             ],
         ),
         compiler_params=pltpu.CompilerParams(
@@ -492,7 +641,8 @@
 
 
 def run_backward(scalars, tables, residuals):
-    count, length, width = residuals[1].shape
+    rows, width = residuals[1].shape
+    count = tables[1].shape[0]
     embed = tables[0].shape[1]
     depth = tables[4]
     half = (N_NEG * N_REP // 2 * SLICE, LANES)
@@ -503,24 +653,48 @@
     ]
     specs = [whole(t.shape) for t in tables]
     specs[6] = pl.BlockSpec((1, width, width), lambda i, *_: (1, 0, 0))
+
+    def early(array):
+        return pl.BlockSpec(
+            (CHUNK, array.shape[1]), lambda i, s: (jnp.minimum(i, last_chunk(s, count)), 0)
+        )
+
+    def late(array):
+        return pl.BlockSpec(
+            (CHUNK, array.shape[1]),
+            lambda i, s: (jnp.clip(i - 1, 0, last_chunk(s, count)), 0),
+        )
+
     return pl.pallas_call(
         backward_kernel,
         name="backward",
         out_shape=outs,
         grid_spec=pltpu.PrefetchScalarGridSpec(
             num_scalar_prefetch=1,
-            grid=(count // SEQS,),
-            in_specs=specs + [chunk(length, r.shape[2]) for r in residuals],
+            grid=(rows // CHUNK + 1,),
+            in_specs=specs
+            + [pl.BlockSpec(memory_space=pl.ANY)]
+            + [late(r) for r in residuals[1:4]]
+            + [early(r) for r in residuals[4:]],
             out_specs=[whole(o.shape) for o in outs],
             scratch_shapes=[
-                pltpu.VMEM((count, width), F32),
-                pltpu.VMEM((SEQS, length, width), BF16),
-                pltpu.VMEM((SEQS, length + 2 * PAD, width), F32),
+                pltpu.VMEM((count, width), BF16),
+                pltpu.VMEM((2, 8, count), jnp.int32),
+                pltpu.VMEM((2, CHUNK, width), BF16),
+                pltpu.VMEM((CHUNK, width), BF16),
+                pltpu.VMEM((CHUNK, width), BF16),
+                pltpu.VMEM((rows + 2 * EDGE, width), BF16),
+                pltpu.VMEM((rows + 2 * EDGE, width), BF16),
+                pltpu.VMEM((CHUNK, 3 * width), BF16),
+                pltpu.VMEM((CHUNK, width), BF16),
+                pltpu.VMEM((4, CHUNK, width), BF16),
                 pltpu.VMEM((3, 8, width), F32),
                 pltpu.VMEM((width, width), F32),
                 pltpu.VMEM((width, 3 * width), F32),
                 pltpu.VMEM((width, embed), BF16),
                 pltpu.VMEM(depth.shape, F32),
+                pltpu.VMEM(depth.shape, BF16),
+                pltpu.SemaphoreType.DMA((1,)),
             ],
         ),
         compiler_params=pltpu.CompilerParams(
@@ -575,9 +749,14 @@
     lengths = jnp.sum(
         (jnp.concatenate([goal_ids[0], premise_ids[0]], axis=0) != 0).astype(jnp.int32), axis=1
     )
+    room = (lengths + (PAD + TILE - 1)) // TILE * TILE
+    places = jnp.arange(count + 1)
+    starts = jnp.sum(
+        jnp.where(places[None, :count] < places[:, None], room[None, :], 0), axis=1
+    )
     scalars = jnp.concatenate(
-        [lengths, jnp.stack([position, lax.axis_index("core")]).astype(jnp.int32)]
-    )
+        [lengths, starts, jnp.stack([position, lax.axis_index("core")])]
+    ).astype(jnp.int32)
     depth = depthwise_kernels.transpose(1, 0, 2)
     outs = run_forward(
         scalars,

time: 159 us -> 133 us (0.84)
  Pallas kernels: 86.9 us -> 56 us
  starting transfers between devices: 13.8 us -> 15.9 us
  blocking collectives: 40.8 us -> 42.8 us
    pallas_call x1, Pallas kernels: 44 us -> 22.9 us  [run_forward(): pl.pallas_call(forward_kernel, name='forward', out_shape=[o[0] for o in o...]
    pallas_call x1, Pallas kernels: 37.5 us -> 27.7 us  [run_backward(): pl.pallas_call(backward_kernel, name='backward', out_shape=outs, grid_spe...]
    all_to_all x1, starting transfers between devices: 8.61 us -> 10.7 us  [local(): gathered = lax.all_to_all(spread, 'neg', 0, 0).reshape(N_NEG * count, -1)]
    all_to_all x1, blocking collectives: 21.9 us -> 23.8 us  [reduce_everywhere(): parts = lax.all_to_all(pair.reshape(peers, SLICE, LANES), axes, 0, 0)]
where the time goes in v4:
time: 133 us; the launch traced here: 132 us
  Pallas kernels  56 us (42%)
  blocking collectives  42.8 us (32%)
  starting transfers between devices  15.9 us (12%)
  waiting for transfers between devices  7.6 us (6%)
  local copies, waits for them, and re-layouts  5.21 us (4%)
  other arithmetic  3.64 us (3%)
    pallas_call x1, Pallas kernels, run_backward(): pl.pallas_call(backward_kernel, name='backward', out_shape=outs, grid_spe...  27.7 us
    all_to_all x1, blocking collectives, reduce_everywhere(): parts = lax.all_to_all(pair.reshape(peers, SLICE, LANES), axes, 0, 0)  23.8 us
    pallas_call x1, Pallas kernels, run_forward(): pl.pallas_call(forward_kernel, name='forward', out_shape=[o[0] for o in o...  22.9 us
    all_to_all x1, blocking collectives, reduce_everywhere(): mine = lax.all_to_all(spread, axes, 0, 0).reshape(peers * SLICE, LANES)  18.9 us
    all_to_all x1, starting transfers between devices, local(): gathered = lax.all_to_all(spread, 'neg', 0, 0).reshape(N_NEG * count, -1)  10.7 us
    all_to_all x1, waiting for transfers between devices, local(): gathered = lax.all_to_all(spread, 'neg', 0, 0).reshape(N_NEG * count, -1)  4.87 us
    pallas_call x1, Pallas kernels, reduce_everywhere(): pl.pallas_call(unpack_kernel, name='unpack', in_specs=[pl.BlockSpec(memor...  3.21 us
    unnamed x10, local copies, waits for them, and re-layouts  3.14 us
  transfers between devices with their start and end apart: 3, of which 3 were waited for; matrix products, arithmetic and copies ran while one was open for 3% of the time, Pallas kernels for 0%

profile of v4, /device:TPU:1, one launch (start us, length us, event | category | flops | bytes accessed | tf_op | source)
XLA Modules:
  0.0 131.8 jit_solution(11377636468679091403)
XLA Ops:
  0.7 0.9 convert_reduce_fusion
  1.6 0.1 select_reduce_fusion
  1.7 0.6 pad_add_fusion.scalars
  2.3 22.9 %forward.1 = (bf16[6144,512]{1,0:T(8,128)(2,1)}, bf16[6144,512]{1,0:T(8,128)(2,1)}, bf16[6144,512]{1,0:T(8,128)(2,1)}, bf16[6144,128]{1,0:T(8,128)(2,1)}, bf16[6...) custom-call(s32[83]{0:T(128)} %pad_add_fusion.scalars, ...), custom_call_target="tpu_custom_call" | custom-call | tf_op jit(solution)/shard_map/forward/pallas_call | solution.py:606
  25.2 10.7 %all-to-all-start = ((bf16[16,40,256]{2,1,0:T(8,128)(2,1)}), bf16[16,40,256]{2,1,0:T(8,128)(2,1)S(1)}, u32[]{:S(2)}, u32[]{:S(2)}) async-start(bf16[16,40,256]{2,1,0:T(8,128)(2,1)} %get-tuple-element.20), calls=%async_computation | async-start | bytes 655360 | tf_op jit(solution)/shard_map/all_to_all | solution.py:771
  35.9 0.5 broadcast.75
  36.4 0.7 reduce.5
  37.1 0.1 squeeze.15
  37.2 0.7 reshape.45.column_target_ref
  37.9 1.0 copy.17
  38.9 4.9 %all-to-all-done = bf16[16,40,256]{2,1,0:T(8,128)(2,1)S(1)} async-done(((bf16[16,40,256]{2,1,0:T(8,128)(2,1)}), bf16[16,40,256]{2,1,0:T(8,128)(2,1)S(1)}, u32[]{:S(2)}, u32[]{:S(2)}) %all-to-all-start) | async-done | bytes 327712 | tf_op jit(solution)/shard_map/all_to_all | solution.py:771
  43.8 0.7 copy-done.1
  44.5 27.7 %backward.1 = (f32[40,128]{1,0:T(8,128)}, bf16[3072,128]{1,0:T(8,128)(2,1)}, bf16[3072,128]{1,0:T(8,128)(2,1)}) custom-call(s32[83]{0:T(128)} %pad_add_fusion.scalars, bf16[640,256]{1,0:T(8,128)(2,1)} %bitcast.18, f32[40,896]{1,0:T(8,128)} %get-tuple-element.21.summary_ref, s32[1,640]{1,0:T(1,128)} %reshape.45.column_target_ref, bf16[512,256]{1,0:T(8,128)(2,1)} %head_ref.3, ...), custom_call_target="tpu_custom_call" | custom-call | tf_op jit(solution)/shard_map/backward/pallas_call | solution.py:668
  72.2 2.3 %collective-permute-start = (bf16[3072,128]{1,0:T(8,128)(2,1)}, bf16[3072,128]{1,0:T(8,128)(2,1)S(1)}, u32[]{:S(2)}, u32[]{:S(2)}) collective-permute-start(bf16[3072,128]{1,0:T(8,128)(2,1)} %get-tuple-element.30), channel_id=1, source_target_pairs={{0,1},{1,0},{2,3},{3,2},{4,5},{5,4},{6,7},{7,6},{8,9},{9,8},{10,11... | collective-permute-start | bytes 2359304 | tf_op jit(solution)/shard_map/ppermute | solution.py:711
  74.5 2.1 %collective-permute-done = bf16[3072,128]{1,0:T(8,128)(2,1)S(1)} collective-permute-done((bf16[3072,128]{1,0:T(8,128)(2,1)}, bf16[3072,128]{1,0:T(8,128)(2,1)S(1)}, u32[]{:S(2)}, u32[]{:S(2)}) %collective-permute-start) | collective-permute-done | bytes 786464 | tf_op jit(solution)/shard_map/ppermute | solution.py:711
  76.6 1.3 %add_convert_fusion = bf16[3072,128]{1,0:T(8,128)(2,1)S(1)} fusion(bf16[3072,128]{1,0:T(8,128)(2,1)S(1)} %collective-permute-done, bf16[3072,128]{1,0:T(8,128)(2,1)} %get-tuple-element.29), kind=kLoop, calls=%fused_computation | loop fusion | flops 1572864 | bytes 2359296 | tf_op jit(solution)/shard_map/convert_element_type | solution.py:712
  78.0 23.8 %all_to_all.15.parts_ref = bf16[64,48,128]{2,1,0:T(8,128)(2,1)} all-to-all(bf16[64,48,128]{2,1,0:T(8,128)(2,1)S(1)} %bitcast.16), channel_id=1, replica_groups=mesh['neg'=16,'chip'=4,'core'=2] {'neg','chip'}, dimensions={0} | all-to-all | bytes 1572864 | tf_op jit(solution)/shard_map/all_to_all | solution.py:713
  101.8 2.2 %spread.1 = bf16[64,48,128]{2,1,0:T(8,128)(2,1)} custom-call(bf16[64,48,128]{2,1,0:T(8,128)(2,1)} %all_to_all.15.parts_ref), custom_call_target="tpu_custom_call" | custom-call | tf_op jit(solution)/shard_map/spread/pallas_call | solution.py:714
  104.0 18.9 %all_to_all.16 = bf16[64,48,128]{2,1,0:T(8,128)(2,1)S(1)} all-to-all(bf16[64,48,128]{2,1,0:T(8,128)(2,1)} %spread.1), channel_id=1, replica_groups=mesh['neg'=16,'chip'=4,'core'=2] {'neg','chip'}, dimensions={0} | all-to-all | bytes 1572864 | tf_op jit(solution)/shard_map/all_to_all | solution.py:717
  122.9 2.9 %collective-permute-start.1 = (bf16[3072,128]{1,0:T(8,128)(2,1)S(1)}, bf16[3072,128]{1,0:T(8,128)(2,1)S(1)}, u32[]{:S(2)}, u32[]{:S(2)}) collective-permute-start(bf16[3072,128]{1,0:T(8,128)(2,1)S(1)} %bitcast.14), channel_id=1, source_target_pairs={{0,1},{1,0},{2,3},{3,2},{4,5},{5,4},{6,7},{7,6},{8,9},{9,8},{10,11... | collective-permute-start | bytes 2359304 | tf_op jit(solution)/shard_map/ppermute | solution.py:718
  125.8 1.3 slice_reduce_fusion
  127.1 0.6 collective-permute-done.1.other_ref
  127.7 0.9 copy-done.2
  128.6 3.2 %unpack.1 = (f32[3,2,512]{2,1,0:T(2,128)}, f32[2,512]{1,0:T(2,128)}, f32[2,512,512]{2,1,0:T(8,128)}, f32[512,256]{1,0:T(8,128)}) custom-call(s32[83]{0:T(128)} %pad_add_fusion.scalars, bf16[3072,128]{1,0:T(8,128)(2,1)} %bitcast.15, bf16[3072,128]{1,0:T(8,128)(2,1)} %copy-done.2, f32[3,2,512]{2,1,0:T(2,128)} %bitcast.21, f32[2,512]{1,0:T(2,128)} %gain_ref.5), custom_call_target="tpu_custom_call" | custom-call | tf_op jit(solution)/shard_map/unpack/pallas_call | solution.py:720
  (12 shorter events, 0.1 us)
Async XLA Ops:
  0.6 37.2 %slice-start = ((bf16[2,512,512]{2,1,0:T(8,128)(2,1)}), bf16[1,512,512]{2,1,0:T(8,128)(2,1)S(1)}, s32[]{:S(2)}) async-start(bf16[2,512,512]{2,1,0:T(8,128)(2,1)} %weight_ref.3), calls=%async_computation.3 | async-start | bytes 1048576 | tf_op jit(solution)/shard_map/slice | solution.py:788
  0.6 35.8 %copy-start.3 = (s32[1,128]{1,0:T(1,128)S(1)}, s32[1,128]{1,0:T(1,128)}, u32[]{:S(2)}) copy-start(s32[1,128]{1,0:T(1,128)} %param.13) | copy-start | bytes 1540
  25.2 18.5 %all-to-all-start = ((bf16[16,40,256]{2,1,0:T(8,128)(2,1)}), bf16[16,40,256]{2,1,0:T(8,128)(2,1)S(1)}, u32[]{:S(2)}, u32[]{:S(2)}) async-start(bf16[16,40,256]{2,1,0:T(8,128)(2,1)} %get-tuple-element.20), calls=%async_computation | async-start | bytes 655360 | tf_op jit(solution)/shard_map/all_to_all | solution.py:771
  43.8 0.7 copy-start.1
  72.2 4.5 %collective-permute-start = (bf16[3072,128]{1,0:T(8,128)(2,1)}, bf16[3072,128]{1,0:T(8,128)(2,1)S(1)}, u32[]{:S(2)}, u32[]{:S(2)}) collective-permute-start(bf16[3072,128]{1,0:T(8,128)(2,1)} %get-tuple-element.30), channel_id=1, source_target_pairs={{0,1},{1,0},{2,3},{3,2},{4,5},{5,4},{6,7},{7,6},{8,9},{9,8},{10,11... | collective-permute-start | bytes 2359304 | tf_op jit(solution)/shard_map/ppermute | solution.py:711
  122.9 4.8 %copy-start = (bf16[64,48,128]{2,1,0:T(8,128)(2,1)}, bf16[64,48,128]{2,1,0:T(8,128)(2,1)S(1)}, u32[]{:S(2)}) copy-start(bf16[64,48,128]{2,1,0:T(8,128)(2,1)S(1)} %all_to_all.16) | copy-start | bytes 2359300
  122.9 4.8 %collective-permute-start.1 = (bf16[3072,128]{1,0:T(8,128)(2,1)S(1)}, bf16[3072,128]{1,0:T(8,128)(2,1)S(1)}, u32[]{:S(2)}, u32[]{:S(2)}) collective-permute-start(bf16[3072,128]{1,0:T(8,128)(2,1)S(1)} %bitcast.14), channel_id=1, source_target_pairs={{0,1},{1,0},{2,3},{3,2},{4,5},{5,4},{6,7},{7,6},{8,9},{9,8},{10,11... | collective-permute-start | bytes 2359304 | tf_op jit(solution)/shard_map/ppermute | solution.py:718
  127.7 0.9 copy-start.2

commit v5 on v4

--- a/solution.py
+++ b/solution.py
@@ -18,6 +18,7 @@
 CHUNK = 512
 PART = 64
 SUB = 256
+GROUP = 64
 EDGE = 16
 SLICE = 48
 EPS = 1e-06
@@ -82,6 +83,7 @@
     pooling,
     mix_gain,
     semaphores,
+    next_sequence,
 ):
     step = pl.program_id(0)
     goals, premises = goal_ref.shape[1], premise_ref.shape[1]
@@ -110,13 +112,20 @@
         summary_ref[...] = jnp.zeros_like(summary_ref)
         pooling[0] = table_of(scalars, 0, count, (count, 1), 0)
         pooling[1] = table_of(scalars, count, count, (count, 1), 0)
-
+        next_sequence[0] = 0
+
+    @pl.when(step <= last)
+    def _():
         def clear(at):
             at = pl.multiple_of(at, TILE)
             states[pl.ds(at, TILE), :] = jnp.zeros((TILE, width), BF16)
             valid_rows[pl.ds(at, TILE), :] = jnp.zeros((TILE, LANES), F32)
 
-        def one_sequence(seq, carry):
+        def wanted(seq):
+            inside = jnp.minimum(seq, count - 1)
+            return (seq < count) & (scalars[count + inside] < (step + 1) * CHUNK)
+
+        def one_sequence(seq):
             @pl.when(lax.rem(seq, goals) == 0)
             def _():
                 pltpu.make_async_copy(
@@ -137,15 +146,18 @@
             parts = (used + PART - 1) // PART
             lax.fori_loop(0, parts, part, 0)
             clear(offset + parts * PART)
-            return carry
-
-        lax.fori_loop(0, count, one_sequence, 0)
-
-        def clear_tail(tile, carry):
-            clear(scalars[2 * count] + tile * TILE)
-            return carry
-
-        lax.fori_loop(0, (end - scalars[2 * count]) // TILE, clear_tail, 0)
+            return seq + 1
+
+        next_sequence[0] = lax.while_loop(wanted, one_sequence, next_sequence[0])
+
+        @pl.when(step == last)
+        def _():
+            def clear_tail(tile, carry):
+                clear(scalars[2 * count] + tile * TILE)
+                return carry
+
+            spare = (last + 1) * CHUNK - scalars[2 * count]
+            lax.fori_loop(0, lax.div(spare, TILE), clear_tail, 0)
 
     def staged(first, second):
         for block in range(0, CHUNK + SUB, SUB):
@@ -281,7 +293,6 @@
     depth_ref,
     gain_ref,
     weight_ref,
-    weight_turned_ref,
     normed_low_ref,
     slope_low_ref,
     normed_up_ref,
@@ -299,13 +310,14 @@
     conv_grad,
     normed_low,
     shifted,
+    mixed_low,
     scaled,
     products,
+    squares,
     corr,
     point_up,
-    moments,
+    point_low,
     head_grad,
-    mix_gain,
     mix_half,
     semaphore,
 ):
@@ -335,12 +347,11 @@
         members[1] = table_of(scalars, count, count, (8, count), 1)
         corr[...] = jnp.zeros_like(corr)
         point_up[...] = jnp.zeros_like(point_up)
-        moments[...] = jnp.zeros_like(moments)
+        point_low[...] = jnp.zeros_like(point_low)
         every = gathered_ref[...]
         total_count = every.shape[0]
         own_count = count
         embed = every.shape[1]
-        mix_gain[...] = depth_ref[...] * gain_ref[...]
         unit = summary_ref[:, width : width + embed]
         magnitude = summary_ref[:, width + embed : width + embed + 1]
         contract = (((1,), (1,)), ((), ()))
@@ -394,6 +405,7 @@
         pooled_grad[...] = spread_back.astype(BF16)
 
     over_tokens = (((0,), (0,)), ((), ()))
+    turned = (((1,), (1,)), ((), ()))
     blocks = range(0, CHUNK, SUB)
 
     @pl.when(step == 1)
@@ -419,7 +431,7 @@
             grad_up[at, :] = grad
             conv_grad[pl.ds(pl.multiple_of(EDGE + base + block, EDGE), SUB), :] = (
                 lax.dot_general(
-                    grad, weight_ref[0], (((1,), (1,)), ((), ())), preferred_element_type=F32
+                    grad, weight_ref[1], turned, preferred_element_type=F32
                 ).astype(BF16)
             )
         point_up[...] += lax.dot_general(
@@ -432,58 +444,78 @@
         slot = lax.rem(step + 1, 2)
         ones = jnp.ones((width, LANES), BF16)
 
+        def window_of(array, start):
+            place = pl.ds(pl.multiple_of(base + start, TILE), TILE + 2 * EDGE)
+            return array[place, :]
+
+        def gather(sums, first, start, tap, product):
+            sums[tap] = product if start % GROUP == 0 else sums[tap] + product
+            if (start + TILE) % GROUP == 0:
+                kept = start // GROUP * TILE
+                products[first + tap, kept : kept + TILE, :] = sums[tap]
+
         def mix(block):
+            sums = [None] * 3
             for start in range(block, block + SUB, TILE):
                 at = pl.ds(start, TILE)
-                place = pl.ds(pl.multiple_of(base + start, TILE), TILE + 2 * EDGE)
-                window = conv_grad[place, :]
-                states = normed_low[place, :]
+                window = window_of(conv_grad, start)
+                states = window_of(normed_low, start)
                 normed = normed_up_ref[at, :]
-                total = None
+                total = low = None
                 for tap in range(3):
                     first = EDGE + (1 - tap) * UPPER_DILATION
                     part = window[first : first + TILE]
                     term = mix_half[tap, 1:2, :] * part
                     total = term if total is None else total + term
-                    products[tap, at, :] = part * normed
+                    gather(sums, 3, start, tap, part * normed)
                     first = EDGE + (tap - 1) * LOWER_DILATION
-                    shifted[at, tap * width : (tap + 1) * width] = states[first : first + TILE]
+                    values = states[first : first + TILE]
+                    shifted[tap, at, :] = values
+                    term = mix_half[tap, 0:1, :] * values
+                    low = term if low is None else low + term
+                mixed_low[at, :] = low
                 scaled[at, :] = total
-                products[3, at, :] = total * normed
+                squares[at, :] = total * normed
 
         def back(block):
             at = pl.ds(block, SUB)
             mean = (
-                jnp.dot(products[3, at, :], ones, preferred_element_type=F32) * (1.0 / width)
+                jnp.dot(squares[at, :], ones, preferred_element_type=F32) * (1.0 / width)
             ).astype(BF16)
             inner = scaled[at, :] - normed_up_ref[at, :] * wide(mean)
             below = upstream[slot, at, :] + wide(inverse_ref[at, :]) * inner
-            grad_low[at, :] = below * slope_low_ref[at, :]
-
-        for block in range(0, CHUNK + SUB, SUB):
+            grad = below * slope_low_ref[at, :]
+            grad_low[at, :] = grad
+            scaled[at, :] = lax.dot_general(
+                grad, weight_ref[0], turned, preferred_element_type=F32
+            ).astype(BF16)
+
+        def correlate(block):
+            sums = [None] * 3
+            for start in range(block, block + SUB, TILE):
+                conv = scaled[start : start + TILE, :]
+                for tap in range(3):
+                    gather(sums, 0, start, tap, conv * shifted[tap, start : start + TILE, :])
+
+        for block in range(0, CHUNK + 2 * SUB, SUB):
             if block < CHUNK:
                 mix(block)
-            if block:
+            if 0 <= block - SUB < CHUNK:
                 back(block - SUB)
-        every_row = jnp.ones((8, CHUNK), BF16)
-        for tap in range(3):
-            corr[tap] += jnp.dot(every_row, products[tap], preferred_element_type=F32)
-        moments[...] += lax.dot_general(
-            grad_low[...], shifted[...], over_tokens, preferred_element_type=F32
+            if block >= 2 * SUB:
+                correlate(block - 2 * SUB)
+        every_row = jnp.ones((8, CHUNK // GROUP * TILE), BF16)
+        for index in range(6):
+            corr[index] += jnp.dot(every_row, products[index], preferred_element_type=F32)
+        point_low[...] += lax.dot_general(
+            mixed_low[...], grad_low[...], over_tokens, preferred_element_type=F32
         )
 
     def emit(low_ref, up_ref):
-        point, rows = 0.0, []
-        for tap in range(3):
-            part = moments[:, tap * width : (tap + 1) * width]
-            rows.append(
-                jnp.sum(part * weight_turned_ref[...].astype(F32), axis=0, keepdims=True)
-            )
-            point = point + mix_gain[tap, 0:1, :] * part
-        rows += [corr[tap, 0:1, :] for tap in range(3)]
+        rows = [corr[index, 0:1, :] for index in range(6)]
         rows.append(jnp.zeros((2, width), F32))
         small = jnp.concatenate(rows, axis=0)
-        low = point.T.astype(BF16)
+        low = point_low[...].astype(BF16)
         up = point_up[...].astype(BF16)
         for part in range(width // LANES):
             lanes = slice(part * LANES, (part + 1) * LANES)
@@ -632,6 +664,7 @@
                 pltpu.VMEM((2, count, 1), jnp.int32),
                 pltpu.VMEM(depth.shape, BF16),
                 pltpu.SemaphoreType.DMA((count // goals,)),
+                pltpu.SMEM((1,), jnp.int32),
             ],
         ),
         compiler_params=pltpu.CompilerParams(
@@ -652,7 +685,6 @@
         jax.ShapeDtypeStruct(half, BF16),
     ]
     specs = [whole(t.shape) for t in tables]
-    specs[6] = pl.BlockSpec((1, width, width), lambda i, *_: (1, 0, 0))
 
     def early(array):
         return pl.BlockSpec(
@@ -685,14 +717,15 @@
                 pltpu.VMEM((CHUNK, width), BF16),
                 pltpu.VMEM((rows + 2 * EDGE, width), BF16),
                 pltpu.VMEM((rows + 2 * EDGE, width), BF16),
-                pltpu.VMEM((CHUNK, 3 * width), BF16),
+                pltpu.VMEM((3, CHUNK, width), BF16),
                 pltpu.VMEM((CHUNK, width), BF16),
-                pltpu.VMEM((4, CHUNK, width), BF16),
-                pltpu.VMEM((3, 8, width), F32),
+                pltpu.VMEM((CHUNK, width), BF16),
+                pltpu.VMEM((6, CHUNK // GROUP * TILE, width), BF16),
+                pltpu.VMEM((CHUNK, width), BF16),
+                pltpu.VMEM((6, 8, width), F32),
                 pltpu.VMEM((width, width), F32),
-                pltpu.VMEM((width, 3 * width), F32),
+                pltpu.VMEM((width, width), F32),
                 pltpu.VMEM((width, embed), BF16),
-                pltpu.VMEM(depth.shape, F32),
                 pltpu.VMEM(depth.shape, BF16),
                 pltpu.SemaphoreType.DMA((1,)),
             ],
@@ -785,7 +818,6 @@
         depth,
         block_norm_gains,
         pointwise_weights,
-        pointwise_weights[0].T,
     )
     loss, keep, send = run_backward(scalars, tables, residuals)
     depth_grad, gain_grad, point_grad, head_grad = reduce_everywhere(

time: 133 us -> 133 us (level)
  starting transfers between devices: 15.9 us -> 17.8 us
  blocking collectives: 42.8 us -> 41.4 us
    ppermute x1, starting transfers between devices: 2.34 us -> 6.35 us  [reduce_everywhere(): got = lax.ppermute(send, 'core', swap)]
    all_to_all x1, starting transfers between devices: 10.7 us -> 8.54 us  [local(): gathered = lax.all_to_all(spread, 'neg', 0, 0).reshape(N_NEG * count, -1)]
    pallas_call x1, Pallas kernels: 27.7 us -> 26.3 us  [run_backward(): pl.pallas_call(backward_kernel, name='backward', out_shape=outs, grid_spe...]
    all_to_all x1, blocking collectives: 23.8 us -> 22.5 us  [reduce_everywhere(): parts = lax.all_to_all(pair.reshape(peers, SLICE, LANES), axes, 0, 0)]
    unnamed x10 -> x9, local copies, waits for them, and re-layouts: 3.14 us -> 2.15 us
  transfers between devices with their start and end apart: 3 -> 3, of which waited for: 3 -> 3; matrix products, arithmetic and copies ran while one was open for 3% -> 2% of each run, Pallas kernels for 0% -> 0%
where the time goes in v5:
time: 133 us; the launch traced here: 131 us
  Pallas kernels  54.8 us (41%)
  blocking collectives  41.4 us (31%)
  starting transfers between devices  17.8 us (13%)
  waiting for transfers between devices  8.46 us (6%)
  local copies, waits for them, and re-layouts  4.21 us (3%)
  other arithmetic  3.55 us (3%)
    pallas_call x1, Pallas kernels, run_backward(): pl.pallas_call(backward_kernel, name='backward', out_shape=outs, grid_spe...  26.3 us
    pallas_call x1, Pallas kernels, run_forward(): pl.pallas_call(forward_kernel, name='forward', out_shape=[o[0] for o in o...  23.1 us
    all_to_all x1, blocking collectives, reduce_everywhere(): parts = lax.all_to_all(pair.reshape(peers, SLICE, LANES), axes, 0, 0)  22.5 us
    all_to_all x1, blocking collectives, reduce_everywhere(): mine = lax.all_to_all(spread, axes, 0, 0).reshape(peers * SLICE, LANES)  18.9 us
    all_to_all x1, starting transfers between devices, local(): gathered = lax.all_to_all(spread, 'neg', 0, 0).reshape(N_NEG * count, -1)  8.54 us
    ppermute x1, starting transfers between devices, reduce_everywhere(): got = lax.ppermute(send, 'core', swap)  6.35 us
    all_to_all x1, waiting for transfers between devices, local(): gathered = lax.all_to_all(spread, 'neg', 0, 0).reshape(N_NEG * count, -1)  5.72 us
    pallas_call x1, Pallas kernels, reduce_everywhere(): pl.pallas_call(unpack_kernel, name='unpack', in_specs=[pl.BlockSpec(memor...  3.21 us
  transfers between devices with their start and end apart: 3, of which 3 were waited for; matrix products, arithmetic and copies ran while one was open for 2% of the time, Pallas kernels for 0%

profile of v5, /device:TPU:1, one launch (start us, length us, event | category | flops | bytes accessed | tf_op | source)
XLA Modules:
  0.0 130.9 jit_solution(475720941947583619)
XLA Ops:
  0.6 0.8 convert_reduce_fusion
  1.5 0.1 select_reduce_fusion
  1.6 0.6 pad_add_fusion.scalars
  2.2 23.1 %forward.1 = (bf16[6144,512]{1,0:T(8,128)(2,1)}, bf16[6144,512]{1,0:T(8,128)(2,1)}, bf16[6144,512]{1,0:T(8,128)(2,1)}, bf16[6144,128]{1,0:T(8,128)(2,1)}, bf16[6...) custom-call(s32[83]{0:T(128)} %pad_add_fusion.scalars, ...), custom_call_target="tpu_custom_call" | custom-call | tf_op jit(solution)/shard_map/forward/pallas_call | solution.py:638
  25.3 8.5 %all-to-all-start = ((bf16[16,40,256]{2,1,0:T(8,128)(2,1)}), bf16[16,40,256]{2,1,0:T(8,128)(2,1)S(1)}, u32[]{:S(2)}, u32[]{:S(2)}) async-start(bf16[16,40,256]{2,1,0:T(8,128)(2,1)} %get-tuple-element.20), calls=%async_computation | async-start | bytes 655360 | tf_op jit(solution)/shard_map/all_to_all | solution.py:804
  33.9 0.5 broadcast.75
  34.4 0.0 copy-done.3
  34.4 0.7 reduce.5
  35.0 0.1 squeeze.12
  35.2 0.7 reshape.45.column_target_ref
  35.8 5.7 %all-to-all-done = bf16[16,40,256]{2,1,0:T(8,128)(2,1)S(1)} async-done(((bf16[16,40,256]{2,1,0:T(8,128)(2,1)}), bf16[16,40,256]{2,1,0:T(8,128)(2,1)S(1)}, u32[]{:S(2)}, u32[]{:S(2)}) %all-to-all-start) | async-done | bytes 327712 | tf_op jit(solution)/shard_map/all_to_all | solution.py:804
  41.6 0.7 copy-done.1
  42.3 26.3 %backward.1 = (f32[40,128]{1,0:T(8,128)}, bf16[3072,128]{1,0:T(8,128)(2,1)}, bf16[3072,128]{1,0:T(8,128)(2,1)}) custom-call(s32[83]{0:T(128)} %pad_add_fusion.scalars, bf16[640,256]{1,0:T(8,128)(2,1)} %bitcast.14, f32[40,896]{1,0:T(8,128)} %get-tuple-element.21.summary_ref, s32[1,640]{1,0:T(1,128)} %reshape.45.column_target_ref, bf16[512,256]{1,0:T(8,128)(2,1)} %head_ref.3, ...), custom_call_target="tpu_custom_call" | custom-call | tf_op jit(solution)/shard_map/backward/pallas_call | solution.py:700
  68.6 6.4 %collective-permute-start = (bf16[3072,128]{1,0:T(8,128)(2,1)}, bf16[3072,128]{1,0:T(8,128)(2,1)S(1)}, u32[]{:S(2)}, u32[]{:S(2)}) collective-permute-start(bf16[3072,128]{1,0:T(8,128)(2,1)} %get-tuple-element.30), channel_id=1, source_target_pairs={{0,1},{1,0},{2,3},{3,2},{4,5},{5,4},{6,7},{7,6},{8,9},{9,8},{10,11... | collective-permute-start | bytes 2359304 | tf_op jit(solution)/shard_map/ppermute | solution.py:744
  74.9 2.1 %collective-permute-done = bf16[3072,128]{1,0:T(8,128)(2,1)S(1)} collective-permute-done((bf16[3072,128]{1,0:T(8,128)(2,1)}, bf16[3072,128]{1,0:T(8,128)(2,1)S(1)}, u32[]{:S(2)}, u32[]{:S(2)}) %collective-permute-start) | collective-permute-done | bytes 786464 | tf_op jit(solution)/shard_map/ppermute | solution.py:744
  77.0 1.3 %add_convert_fusion = bf16[3072,128]{1,0:T(8,128)(2,1)S(1)} fusion(bf16[3072,128]{1,0:T(8,128)(2,1)S(1)} %collective-permute-done, bf16[3072,128]{1,0:T(8,128)(2,1)} %get-tuple-element.29), kind=kLoop, calls=%fused_computation | loop fusion | flops 1572864 | bytes 2359296 | tf_op jit(solution)/shard_map/convert_element_type | solution.py:745
  78.4 22.5 %all_to_all.15.parts_ref = bf16[64,48,128]{2,1,0:T(8,128)(2,1)} all-to-all(bf16[64,48,128]{2,1,0:T(8,128)(2,1)S(1)} %bitcast.13), channel_id=1, replica_groups=mesh['neg'=16,'chip'=4,'core'=2] {'neg','chip'}, dimensions={0} | all-to-all | bytes 1572864 | tf_op jit(solution)/shard_map/all_to_all | solution.py:746
  100.9 2.2 %spread.1 = bf16[64,48,128]{2,1,0:T(8,128)(2,1)} custom-call(bf16[64,48,128]{2,1,0:T(8,128)(2,1)} %all_to_all.15.parts_ref), custom_call_target="tpu_custom_call" | custom-call | tf_op jit(solution)/shard_map/spread/pallas_call | solution.py:747
  103.0 18.9 %all_to_all.16 = bf16[64,48,128]{2,1,0:T(8,128)(2,1)S(1)} all-to-all(bf16[64,48,128]{2,1,0:T(8,128)(2,1)} %spread.1), channel_id=1, replica_groups=mesh['neg'=16,'chip'=4,'core'=2] {'neg','chip'}, dimensions={0} | all-to-all | bytes 1572864 | tf_op jit(solution)/shard_map/all_to_all | solution.py:750
  122.0 2.9 %collective-permute-start.1 = (bf16[3072,128]{1,0:T(8,128)(2,1)S(1)}, bf16[3072,128]{1,0:T(8,128)(2,1)S(1)}, u32[]{:S(2)}, u32[]{:S(2)}) collective-permute-start(bf16[3072,128]{1,0:T(8,128)(2,1)S(1)} %bitcast.11), channel_id=1, source_target_pairs={{0,1},{1,0},{2,3},{3,2},{4,5},{5,4},{6,7},{7,6},{8,9},{9,8},{10,11... | collective-permute-start | bytes 2359304 | tf_op jit(solution)/shard_map/ppermute | solution.py:751
  124.9 1.3 slice_reduce_fusion
  126.2 0.6 collective-permute-done.1.other_ref
  126.8 0.9 copy-done.2
  127.7 3.2 %unpack.1 = (f32[3,2,512]{2,1,0:T(2,128)}, f32[2,512]{1,0:T(2,128)}, f32[2,512,512]{2,1,0:T(8,128)}, f32[512,256]{1,0:T(8,128)}) custom-call(s32[83]{0:T(128)} %pad_add_fusion.scalars, bf16[3072,128]{1,0:T(8,128)(2,1)} %bitcast.12, bf16[3072,128]{1,0:T(8,128)(2,1)} %copy-done.2, f32[3,2,512]{2,1,0:T(2,128)} %bitcast.17, f32[2,512]{1,0:T(2,128)} %gain_ref.5), custom_call_target="tpu_custom_call" | custom-call | tf_op jit(solution)/shard_map/unpack/pallas_call | solution.py:753
  (9 shorter events, 0.1 us)
Async XLA Ops:
  0.6 33.7 %copy-start.3 = (s32[1,128]{1,0:T(1,128)S(1)}, s32[1,128]{1,0:T(1,128)}, u32[]{:S(2)}) copy-start(s32[1,128]{1,0:T(1,128)} %param.13) | copy-start | bytes 1540
  25.3 16.2 %all-to-all-start = ((bf16[16,40,256]{2,1,0:T(8,128)(2,1)}), bf16[16,40,256]{2,1,0:T(8,128)(2,1)S(1)}, u32[]{:S(2)}, u32[]{:S(2)}) async-start(bf16[16,40,256]{2,1,0:T(8,128)(2,1)} %get-tuple-element.20), calls=%async_computation | async-start | bytes 655360 | tf_op jit(solution)/shard_map/all_to_all | solution.py:804
  41.6 0.7 copy-start.1
  68.6 8.5 %collective-permute-start = (bf16[3072,128]{1,0:T(8,128)(2,1)}, bf16[3072,128]{1,0:T(8,128)(2,1)S(1)}, u32[]{:S(2)}, u32[]{:S(2)}) collective-permute-start(bf16[3072,128]{1,0:T(8,128)(2,1)} %get-tuple-element.30), channel_id=1, source_target_pairs={{0,1},{1,0},{2,3},{3,2},{4,5},{5,4},{6,7},{7,6},{8,9},{9,8},{10,11... | collective-permute-start | bytes 2359304 | tf_op jit(solution)/shard_map/ppermute | solution.py:744
  122.0 4.8 %copy-start = (bf16[64,48,128]{2,1,0:T(8,128)(2,1)}, bf16[64,48,128]{2,1,0:T(8,128)(2,1)S(1)}, u32[]{:S(2)}) copy-start(bf16[64,48,128]{2,1,0:T(8,128)(2,1)S(1)} %all_to_all.16) | copy-start | bytes 2359300
  122.0 4.8 %collective-permute-start.1 = (bf16[3072,128]{1,0:T(8,128)(2,1)S(1)}, bf16[3072,128]{1,0:T(8,128)(2,1)S(1)}, u32[]{:S(2)}, u32[]{:S(2)}) collective-permute-start(bf16[3072,128]{1,0:T(8,128)(2,1)S(1)} %bitcast.11), channel_id=1, source_target_pairs={{0,1},{1,0},{2,3},{3,2},{4,5},{5,4},{6,7},{7,6},{8,9},{9,8},{10,11... | collective-permute-start | bytes 2359304 | tf_op jit(solution)/shard_map/ppermute | solution.py:751
  126.8 0.9 copy-start.2

commit v6 on v5

--- a/solution.py
+++ b/solution.py
@@ -388,7 +388,11 @@
         )
         score_grad = (score_grad / float(goal_total)).astype(BF16)
         chosen = jnp.sum(jnp.where(hit_goal, scores, 0.0), axis=1, keepdims=True)
-        loss_ref[...] = jnp.broadcast_to(jnp.log(own_total) - chosen, loss_ref.shape)
+        lane = lax.broadcasted_iota(jnp.int32, (own_count, LANES), 1)
+        diagonal = lane == lax.broadcasted_iota(jnp.int32, (own_count, LANES), 0)
+        loss_ref[...] = jnp.sum(
+            jnp.where(diagonal, jnp.log(own_total) - chosen, 0.0), axis=0, keepdims=True
+        )
         unit_grad = logit_scale * jnp.dot(score_grad, every, preferred_element_type=F32)
         along = jnp.sum(unit * unit_grad, axis=-1, keepdims=True)
         embed_grad = ((unit_grad - unit * along) / magnitude).astype(BF16)
@@ -559,33 +563,31 @@
     head_out,
 ):
     core = scalars[scalars.shape[0] - 1]
-    width = gain_ref.shape[1]
+    part = pl.program_id(0)
+    width = point_out.shape[1]
     base = width * width // LANES
 
     def emit(low_ref, up_ref):
-        for part in range(width // LANES):
-            lanes = slice(part * LANES, (part + 1) * LANES)
-            rows = slice(part * width, (part + 1) * width)
-            point_out[0, :, lanes] = low_ref[rows, :].astype(F32)
-            point_out[1, :, lanes] = up_ref[rows, :].astype(F32)
-        for part in range(head_out.shape[1] // LANES):
-            lanes = slice(part * LANES, (part + 1) * LANES)
-            head_out[:, lanes] = low_ref[
-                base + part * width : base + (part + 1) * width, :
-            ].astype(F32)
+        rows = pl.ds(pl.multiple_of(part * width, width), width)
+        point_out[0] = low_ref[rows, :].astype(F32)
+        point_out[1] = up_ref[rows, :].astype(F32)
+
+        @pl.when(part < 2)
+        def _():
+            head_rows = pl.ds(pl.multiple_of(base + part * width, width), width)
+            head_out[...] = low_ref[head_rows, :].astype(F32)
+
         small = up_ref[base : base + 32, :].astype(F32)
-        for part in range(width // LANES):
-            lanes = slice(part * LANES, (part + 1) * LANES)
-            rows = small[part * 8 : (part + 1) * 8, :]
-            for block in range(2):
-                total = 0.0
-                for tap in range(3):
-                    row = rows[block * 3 + tap : block * 3 + tap + 1, :]
-                    depth_out[tap, block : block + 1, lanes] = (
-                        row * gain_ref[block : block + 1, lanes]
-                    )
-                    total = total + row * depth_ref[tap, block : block + 1, lanes]
-                gain_out[block : block + 1, lanes] = total
+        chosen = small[:8]
+        for other in range(1, width // LANES):
+            chosen = jnp.where(part == other, small[other * 8 : other * 8 + 8], chosen)
+        for block in range(2):
+            total = 0.0
+            for tap in range(3):
+                row = chosen[block * 3 + tap : block * 3 + tap + 1, :]
+                depth_out[tap, block : block + 1, :] = row * gain_ref[block : block + 1, :]
+                total = total + row * depth_ref[tap, block : block + 1, :]
+            gain_out[block : block + 1, :] = total
 
     @pl.when(core == 0)
     def _():
@@ -680,7 +682,7 @@
     depth = tables[4]
     half = (N_NEG * N_REP // 2 * SLICE, LANES)
     outs = [
-        jax.ShapeDtypeStruct((count, LANES), F32),
+        jax.ShapeDtypeStruct((1, LANES), F32),
         jax.ShapeDtypeStruct(half, BF16),
         jax.ShapeDtypeStruct(half, BF16),
     ]
@@ -753,8 +755,20 @@
     return pl.pallas_call(
         unpack_kernel,
         name="unpack",
-        in_specs=[pl.BlockSpec(memory_space=pltpu.SMEM)] + [vmem] * 4,
-        out_specs=[vmem] * 4,
+        grid=(width // LANES,),
+        in_specs=[
+            pl.BlockSpec(memory_space=pltpu.SMEM),
+            vmem,
+            vmem,
+            pl.BlockSpec((3, 2, LANES), lambda i: (0, 0, i)),
+            pl.BlockSpec((2, LANES), lambda i: (0, i)),
+        ],
+        out_specs=[
+            pl.BlockSpec((3, 2, LANES), lambda i: (0, 0, i)),
+            pl.BlockSpec((2, LANES), lambda i: (0, i)),
+            pl.BlockSpec((2, width, LANES), lambda i: (0, 0, i)),
+            pl.BlockSpec((width, LANES), lambda i: (0, jnp.minimum(i, 1))),
+        ],
         out_shape=[
             jax.ShapeDtypeStruct(depth.shape, F32),
             jax.ShapeDtypeStruct(gains.shape, F32),
@@ -824,7 +838,7 @@
         scalars, keep, send, depth, block_norm_gains, head_weight.shape[1]
     )
     return (
-        loss[:goals, 0][None, :],
+        loss[:, :goals],
         depth_grad.transpose(1, 0, 2),
         gain_grad,
         point_grad,

time: 133 us -> 132 us (level); the launches traced: 131 us -> 132 us
  starting transfers between devices: 17.8 us -> 11.4 us
  Pallas kernels: 54.8 us -> 60 us
  waiting for transfers between devices: 8.46 us -> 11.2 us
    ppermute x1, starting transfers between devices: 6.35 us -> 0.08 us  [reduce_everywhere(): got = lax.ppermute(send, 'core', swap)]
    pallas_call x1, Pallas kernels: 26.3 us -> 28.5 us  [run_backward(): pl.pallas_call(backward_kernel, name='backward', out_shape=outs, grid_spe...]
    pallas_call x1, Pallas kernels: 23.1 us -> 25.2 us  [run_forward(): pl.pallas_call(forward_kernel, name='forward', out_shape=[o[0] for o in o...]
  transfers between devices with their start and end apart: 3 -> 3, of which waited for: 3 -> 3; matrix products, arithmetic and copies ran while one was open for 2% -> 1% of each run, Pallas kernels for 0% -> 0%
where the time goes in v6:
time: 132 us
  Pallas kernels  60 us (45%)
  blocking collectives  41.9 us (32%)
  starting transfers between devices  11.4 us (9%)
  waiting for transfers between devices  11.2 us (8%)
  other arithmetic  3.58 us (3%)
  local copies, waits for them, and re-layouts  2.9 us (2%)
    pallas_call x1, Pallas kernels, run_backward(): pl.pallas_call(backward_kernel, name='backward', out_shape=outs, grid_spe...  28.5 us
    pallas_call x1, Pallas kernels, run_forward(): pl.pallas_call(forward_kernel, name='forward', out_shape=[o[0] for o in o...  25.2 us
    all_to_all x1, blocking collectives, reduce_everywhere(): parts = lax.all_to_all(pair.reshape(peers, SLICE, LANES), axes, 0, 0)  23 us
    all_to_all x1, blocking collectives, reduce_everywhere(): mine = lax.all_to_all(spread, axes, 0, 0).reshape(peers * SLICE, LANES)  18.9 us
    all_to_all x1, starting transfers between devices, local(): gathered = lax.all_to_all(spread, 'neg', 0, 0).reshape(N_NEG * count, -1)  8.39 us
    all_to_all x1, waiting for transfers between devices, local(): gathered = lax.all_to_all(spread, 'neg', 0, 0).reshape(N_NEG * count, -1)  6.82 us
    pallas_call x1, Pallas kernels, reduce_everywhere(): pl.pallas_call(unpack_kernel, name='unpack', grid=(width // LANES,), in_s...  4.03 us
    ppermute x1, starting transfers between devices, reduce_everywhere(): other = lax.ppermute(mine, 'core', swap)  2.89 us
  transfers between devices with their start and end apart: 3, of which 3 were waited for; matrix products, arithmetic and copies ran while one was open for 1% of the time, Pallas kernels for 0%

profile of v6, /device:TPU:1, one launch (start us, length us, event | category | flops | bytes accessed | tf_op | source)
XLA Modules:
  0.0 131.7 jit_solution(13162235127297091735)
XLA Ops:
  0.6 0.0 copy-start.3
  0.6 0.8 convert_reduce_fusion
  1.5 0.1 select_reduce_fusion
  1.6 0.6 pad_add_fusion.scalars
  2.2 25.2 %forward.1 = (bf16[6144,512]{1,0:T(8,128)(2,1)}, bf16[6144,512]{1,0:T(8,128)(2,1)}, bf16[6144,512]{1,0:T(8,128)(2,1)}, bf16[6144,128]{1,0:T(8,128)(2,1)}, bf16[6...) custom-call(s32[83]{0:T(128)} %pad_add_fusion.scalars, ...), custom_call_target="tpu_custom_call" | custom-call | tf_op jit(solution)/shard_map/forward/pallas_call | solution.py:640
  27.5 8.4 %all-to-all-start = ((bf16[16,40,256]{2,1,0:T(8,128)(2,1)}), bf16[16,40,256]{2,1,0:T(8,128)(2,1)S(1)}, u32[]{:S(2)}, u32[]{:S(2)}) async-start(bf16[16,40,256]{2,1,0:T(8,128)(2,1)} %get-tuple-element.20), calls=%async_computation | async-start | bytes 655360 | tf_op jit(solution)/shard_map/all_to_all | solution.py:818
  35.9 0.5 broadcast.74
  36.4 0.7 reduce.3
  37.0 0.1 squeeze.12
  37.2 0.7 reshape.45.column_target_ref
  37.8 6.8 %all-to-all-done = bf16[16,40,256]{2,1,0:T(8,128)(2,1)S(1)} async-done(((bf16[16,40,256]{2,1,0:T(8,128)(2,1)}), bf16[16,40,256]{2,1,0:T(8,128)(2,1)S(1)}, u32[]{:S(2)}, u32[]{:S(2)}) %all-to-all-start) | async-done | bytes 327712 | tf_op jit(solution)/shard_map/all_to_all | solution.py:818
  44.7 0.7 copy-done.1
  45.4 28.5 %backward.1 = (f32[1,128]{1,0:T(1,128)}, bf16[3072,128]{1,0:T(8,128)(2,1)}, bf16[3072,128]{1,0:T(8,128)(2,1)}) custom-call(s32[83]{0:T(128)} %pad_add_fusion.scalars, bf16[640,256]{1,0:T(8,128)(2,1)} %bitcast.14, f32[40,896]{1,0:T(8,128)} %get-tuple-element.21.summary_ref, s32[1,640]{1,0:T(1,128)} %reshape.45.column_target_ref, bf16[512,256]{1,0:T(8,128)(2,1)} %head_ref.3, ...), custom_call_target="tpu_custom_call" | custom-call | tf_op jit(solution)/shard_map/backward/pallas_call | solution.py:702
  73.9 0.1 collective-permute-start
  74.0 2.5 %collective-permute-done = bf16[3072,128]{1,0:T(8,128)(2,1)S(1)} collective-permute-done((bf16[3072,128]{1,0:T(8,128)(2,1)}, bf16[3072,128]{1,0:T(8,128)(2,1)S(1)}, u32[]{:S(2)}, u32[]{:S(2)}) %collective-permute-start) | collective-permute-done | bytes 786464 | tf_op jit(solution)/shard_map/ppermute | solution.py:746
  76.5 1.3 %add_convert_fusion = bf16[3072,128]{1,0:T(8,128)(2,1)S(1)} fusion(bf16[3072,128]{1,0:T(8,128)(2,1)S(1)} %collective-permute-done, bf16[3072,128]{1,0:T(8,128)(2,1)} %get-tuple-element.29), kind=kLoop, calls=%fused_computation | loop fusion | flops 1572864 | bytes 2359296 | tf_op jit(solution)/shard_map/convert_element_type | solution.py:747
  77.8 23.0 %all_to_all.15.parts_ref = bf16[64,48,128]{2,1,0:T(8,128)(2,1)} all-to-all(bf16[64,48,128]{2,1,0:T(8,128)(2,1)S(1)} %bitcast.13), channel_id=1, replica_groups=mesh['neg'=16,'chip'=4,'core'=2] {'neg','chip'}, dimensions={0} | all-to-all | bytes 1572864 | tf_op jit(solution)/shard_map/all_to_all | solution.py:748
  100.8 2.2 %spread.1 = bf16[64,48,128]{2,1,0:T(8,128)(2,1)} custom-call(bf16[64,48,128]{2,1,0:T(8,128)(2,1)} %all_to_all.15.parts_ref), custom_call_target="tpu_custom_call" | custom-call | tf_op jit(solution)/shard_map/spread/pallas_call | solution.py:749
  103.0 18.9 %all_to_all.16 = bf16[64,48,128]{2,1,0:T(8,128)(2,1)S(1)} all-to-all(bf16[64,48,128]{2,1,0:T(8,128)(2,1)} %spread.1), channel_id=1, replica_groups=mesh['neg'=16,'chip'=4,'core'=2] {'neg','chip'}, dimensions={0} | all-to-all | bytes 1572864 | tf_op jit(solution)/shard_map/all_to_all | solution.py:752
  121.9 2.9 %collective-permute-start.1 = (bf16[3072,128]{1,0:T(8,128)(2,1)S(1)}, bf16[3072,128]{1,0:T(8,128)(2,1)S(1)}, u32[]{:S(2)}, u32[]{:S(2)}) collective-permute-start(bf16[3072,128]{1,0:T(8,128)(2,1)S(1)} %bitcast.11), channel_id=1, source_target_pairs={{0,1},{1,0},{2,3},{3,2},{4,5},{5,4},{6,7},{7,6},{8,9},{9,8},{10,11... | collective-permute-start | bytes 2359304 | tf_op jit(solution)/shard_map/ppermute | solution.py:753
  124.8 1.9 %collective-permute-done.1.other_ref = bf16[3072,128]{1,0:T(8,128)(2,1)S(1)} collective-permute-done((bf16[3072,128]{1,0:T(8,128)(2,1)S(1)}, bf16[3072,128]{1,0:T(8,128)(2,1)S(1)}, u32[]{:S(2)}, u32[]{:S(2)}) %collective-permute-start.1) | collective-permute-done | bytes 786464 | tf_op jit(solution)/shard_map/ppermute | solution.py:753
  126.7 0.0 copy-done
  126.7 0.9 copy-done.2
  127.6 4.0 %unpack.1 = (f32[3,2,512]{2,1,0:T(2,128)}, f32[2,512]{1,0:T(2,128)}, f32[2,512,512]{2,1,0:T(8,128)}, f32[512,256]{1,0:T(8,128)}) custom-call(s32[83]{0:T(128)} %pad_add_fusion.scalars, bf16[3072,128]{1,0:T(8,128)(2,1)} %bitcast.12, bf16[3072,128]{1,0:T(8,128)(2,1)} %copy-done.2, f32[3,2,512]{2,1,0:T(2,128)} %bitcast.17, f32[2,512]{1,0:T(2,128)} %gain_ref.5), custom_call_target="tpu_custom_call" | custom-call | tf_op jit(solution)/shard_map/unpack/pallas_call | solution.py:755
  (8 shorter events, 0.1 us)
Async XLA Ops:
  0.6 35.7 %copy-start.3 = (s32[1,128]{1,0:T(1,128)S(1)}, s32[1,128]{1,0:T(1,128)}, u32[]{:S(2)}) copy-start(s32[1,128]{1,0:T(1,128)} %param.13) | copy-start | bytes 1540
  27.5 17.2 %all-to-all-start = ((bf16[16,40,256]{2,1,0:T(8,128)(2,1)}), bf16[16,40,256]{2,1,0:T(8,128)(2,1)S(1)}, u32[]{:S(2)}, u32[]{:S(2)}) async-start(bf16[16,40,256]{2,1,0:T(8,128)(2,1)} %get-tuple-element.20), calls=%async_computation | async-start | bytes 655360 | tf_op jit(solution)/shard_map/all_to_all | solution.py:818
  44.7 0.7 copy-start.1
  73.9 2.6 %collective-permute-start = (bf16[3072,128]{1,0:T(8,128)(2,1)}, bf16[3072,128]{1,0:T(8,128)(2,1)S(1)}, u32[]{:S(2)}, u32[]{:S(2)}) collective-permute-start(bf16[3072,128]{1,0:T(8,128)(2,1)} %get-tuple-element.30), channel_id=1, source_target_pairs={{0,1},{1,0},{2,3},{3,2},{4,5},{5,4},{6,7},{7,6},{8,9},{9,8},{10,11... | collective-permute-start | bytes 2359304 | tf_op jit(solution)/shard_map/ppermute | solution.py:746
  121.9 4.8 %copy-start = (bf16[64,48,128]{2,1,0:T(8,128)(2,1)}, bf16[64,48,128]{2,1,0:T(8,128)(2,1)S(1)}, u32[]{:S(2)}) copy-start(bf16[64,48,128]{2,1,0:T(8,128)(2,1)S(1)} %all_to_all.16) | copy-start | bytes 2359300
  121.9 4.8 %collective-permute-start.1 = (bf16[3072,128]{1,0:T(8,128)(2,1)S(1)}, bf16[3072,128]{1,0:T(8,128)(2,1)S(1)}, u32[]{:S(2)}, u32[]{:S(2)}) collective-permute-start(bf16[3072,128]{1,0:T(8,128)(2,1)S(1)} %bitcast.11), channel_id=1, source_target_pairs={{0,1},{1,0},{2,3},{3,2},{4,5},{5,4},{6,7},{7,6},{8,9},{9,8},{10,11... | collective-permute-start | bytes 2359304 | tf_op jit(solution)/shard_map/ppermute | solution.py:753
  126.7 0.9 copy-start.2

commit v7 on v5

--- a/solution.py
+++ b/solution.py
@@ -536,15 +536,6 @@
     @pl.when((step == last) & (core == 1))
     def _():
         emit(send_ref, keep_ref)
-
-
-def spread_kernel(parts_ref, spread_ref):
-    total = parts_ref[0].astype(F32)
-    for peer in range(1, parts_ref.shape[0]):
-        total = total + parts_ref[peer].astype(F32)
-    total = total.astype(BF16)
-    for peer in range(parts_ref.shape[0]):
-        spread_ref[peer] = total
 
 
 def unpack_kernel(
@@ -744,9 +735,8 @@
     got = lax.ppermute(send, "core", swap)
     pair = (keep.astype(F32) + got.astype(F32)).astype(BF16)
     parts = lax.all_to_all(pair.reshape(peers, SLICE, LANES), axes, 0, 0)
-    spread = pl.pallas_call(
-        spread_kernel, name="spread", out_shape=jax.ShapeDtypeStruct(parts.shape, BF16)
-    )(parts)
+    total = jnp.sum(parts.astype(F32), axis=0).astype(BF16)
+    spread = jnp.broadcast_to(total[None], parts.shape)
     mine = lax.all_to_all(spread, axes, 0, 0).reshape(peers * SLICE, LANES)
     other = lax.ppermute(mine, "core", swap)
     vmem = pl.BlockSpec(memory_space=pltpu.VMEM)

time: 133 us -> 129 us (0.970)
  starting transfers between devices: 17.8 us -> 13.7 us
  Pallas kernels: 54.8 us -> 57.2 us
  blocking collectives: 41.4 us -> 39.6 us
    ppermute x1, starting transfers between devices: 6.35 us -> 2.34 us  [reduce_everywhere(): got = lax.ppermute(send, 'core', swap)]
    pallas_call x1, Pallas kernels: 26.3 us -> 28.7 us  [run_backward(): pl.pallas_call(backward_kernel, name='backward', out_shape=outs, grid_spe...]
    pallas_call x1, Pallas kernels: 23.1 us -> 25.3 us  [run_forward(): pl.pallas_call(forward_kernel, name='forward', out_shape=[o[0] for o in o...]
    pallas_call x1 -> x0, Pallas kernels: 2.17 us -> none  [reduce_everywhere(): pl.pallas_call(spread_kernel, name='spread', out_shape=jax.ShapeDtypeStru...]
    all_to_all x1, blocking collectives: 22.5 us -> 21 us  [reduce_everywhere(): parts = lax.all_to_all(pair.reshape(peers, SLICE, LANES), axes, 0, 0)]
  transfers between devices with their start and end apart: 3 -> 3, of which waited for: 3 -> 3; matrix products, arithmetic and copies ran while one was open for 2% -> 3% of each run, Pallas kernels for 0% -> 0%
where the time goes in v7:
time: 129 us; the launch traced here: 128 us
  Pallas kernels  57.2 us (44%)
  blocking collectives  39.6 us (31%)
  starting transfers between devices  13.7 us (11%)
  waiting for transfers between devices  8.61 us (7%)
  local copies, waits for them, and re-layouts  4.31 us (3%)
  other arithmetic  3.7 us (3%)
    pallas_call x1, Pallas kernels, run_backward(): pl.pallas_call(backward_kernel, name='backward', out_shape=outs, grid_spe...  28.7 us
    pallas_call x1, Pallas kernels, run_forward(): pl.pallas_call(forward_kernel, name='forward', out_shape=[o[0] for o in o...  25.3 us
    all_to_all x1, blocking collectives, reduce_everywhere(): parts = lax.all_to_all(pair.reshape(peers, SLICE, LANES), axes, 0, 0)  21 us
    all_to_all x1, blocking collectives, reduce_everywhere(): mine = lax.all_to_all(spread, axes, 0, 0).reshape(peers * SLICE, LANES)  18.6 us
    all_to_all x1, starting transfers between devices, local(): gathered = lax.all_to_all(spread, 'neg', 0, 0).reshape(N_NEG * count, -1)  8.47 us
    all_to_all x1, waiting for transfers between devices, local(): gathered = lax.all_to_all(spread, 'neg', 0, 0).reshape(N_NEG * count, -1)  5.87 us
    pallas_call x1, Pallas kernels, reduce_everywhere(): pl.pallas_call(unpack_kernel, name='unpack', in_specs=[pl.BlockSpec(memor...  3.21 us
    ppermute x1, starting transfers between devices, reduce_everywhere(): other = lax.ppermute(mine, 'core', swap)  2.87 us
  transfers between devices with their start and end apart: 3, of which 3 were waited for; matrix products, arithmetic and copies ran while one was open for 3% of the time, Pallas kernels for 0%

profile of v7, /device:TPU:1, one launch (start us, length us, event | category | flops | bytes accessed | tf_op | source)
XLA Modules:
  0.0 127.8 jit_solution(7474667039845982316)
XLA Ops:
  0.6 0.8 convert_reduce_fusion
  1.5 0.1 select_reduce_fusion
  1.6 0.6 pad_add_fusion.scalars
  2.2 25.3 %forward.1 = (bf16[6144,512]{1,0:T(8,128)(2,1)}, bf16[6144,512]{1,0:T(8,128)(2,1)}, bf16[6144,512]{1,0:T(8,128)(2,1)}, bf16[6144,128]{1,0:T(8,128)(2,1)}, bf16[6...) custom-call(s32[83]{0:T(128)} %pad_add_fusion.scalars, ...), custom_call_target="tpu_custom_call" | custom-call | tf_op jit(solution)/shard_map/forward/pallas_call | solution.py:629
  27.5 8.5 %all-to-all-start = ((bf16[16,40,256]{2,1,0:T(8,128)(2,1)}), bf16[16,40,256]{2,1,0:T(8,128)(2,1)S(1)}, u32[]{:S(2)}, u32[]{:S(2)}) async-start(bf16[16,40,256]{2,1,0:T(8,128)(2,1)} %get-tuple-element.20), calls=%async_computation | async-start | bytes 655360 | tf_op jit(solution)/shard_map/all_to_all | solution.py:794
  36.0 0.5 broadcast.76
  36.5 0.7 reduce.6
  37.1 0.1 squeeze.12
  37.3 0.7 reshape.46.column_target_ref
  37.9 5.9 %all-to-all-done = bf16[16,40,256]{2,1,0:T(8,128)(2,1)S(1)} async-done(((bf16[16,40,256]{2,1,0:T(8,128)(2,1)}), bf16[16,40,256]{2,1,0:T(8,128)(2,1)S(1)}, u32[]{:S(2)}, u32[]{:S(2)}) %all-to-all-start) | async-done | bytes 327712 | tf_op jit(solution)/shard_map/all_to_all | solution.py:794
  43.8 0.7 copy-done.1
  44.5 28.7 %backward.1 = (f32[40,128]{1,0:T(8,128)}, bf16[3072,128]{1,0:T(8,128)(2,1)}, bf16[3072,128]{1,0:T(8,128)(2,1)}) custom-call(s32[83]{0:T(128)} %pad_add_fusion.scalars, bf16[640,256]{1,0:T(8,128)(2,1)} %bitcast.14, f32[40,896]{1,0:T(8,128)} %get-tuple-element.21.summary_ref, s32[1,640]{1,0:T(1,128)} %reshape.46.column_target_ref, bf16[512,256]{1,0:T(8,128)(2,1)} %head_ref.3, ...), custom_call_target="tpu_custom_call" | custom-call | tf_op jit(solution)/shard_map/backward/pallas_call | solution.py:691
  73.2 2.3 %collective-permute-start = (bf16[3072,128]{1,0:T(8,128)(2,1)}, bf16[3072,128]{1,0:T(8,128)(2,1)S(1)}, u32[]{:S(2)}, u32[]{:S(2)}) collective-permute-start(bf16[3072,128]{1,0:T(8,128)(2,1)} %get-tuple-element.30), channel_id=1, source_target_pairs={{0,1},{1,0},{2,3},{3,2},{4,5},{5,4},{6,7},{7,6},{8,9},{9,8},{10,11... | collective-permute-start | bytes 2359304 | tf_op jit(solution)/shard_map/ppermute | solution.py:735
  75.6 2.1 %collective-permute-done = bf16[3072,128]{1,0:T(8,128)(2,1)S(1)} collective-permute-done((bf16[3072,128]{1,0:T(8,128)(2,1)}, bf16[3072,128]{1,0:T(8,128)(2,1)S(1)}, u32[]{:S(2)}, u32[]{:S(2)}) %collective-permute-start) | collective-permute-done | bytes 786464 | tf_op jit(solution)/shard_map/ppermute | solution.py:735
  77.7 1.3 %add_convert_fusion = bf16[3072,128]{1,0:T(8,128)(2,1)S(1)} fusion(bf16[3072,128]{1,0:T(8,128)(2,1)S(1)} %collective-permute-done, bf16[3072,128]{1,0:T(8,128)(2,1)} %get-tuple-element.29), kind=kLoop, calls=%fused_computation | loop fusion | flops 1572864 | bytes 2359296 | tf_op jit(solution)/shard_map/convert_element_type | solution.py:736
  79.0 21.0 %all_to_all.15 = bf16[64,48,128]{2,1,0:T(8,128)(2,1)S(1)} all-to-all(bf16[64,48,128]{2,1,0:T(8,128)(2,1)S(1)} %bitcast.13), channel_id=1, replica_groups=mesh['neg'=16,'chip'=4,'core'=2] {'neg','chip'}, dimensions={0} | all-to-all | bytes 1572864 | tf_op jit(solution)/shard_map/all_to_all | solution.py:737
  100.1 0.1 reduce_sum.32
  100.2 0.1 broadcast_in_dim.24
  100.3 18.6 %all_to_all.16 = bf16[64,48,128]{2,1,0:T(8,128)(2,1)S(1)} all-to-all(bf16[64,48,128]{2,1,0:T(8,128)(2,1)S(1)} %broadcast_in_dim.24), channel_id=1, replica_groups=mesh['neg'=16,'chip'=4,'core'=2] {'neg','chip'}, dimensions={0} | all-to-all | bytes 1572864 | tf_op jit(solution)/shard_map/all_to_all | solution.py:740
  118.9 2.9 %collective-permute-start.1 = (bf16[3072,128]{1,0:T(8,128)(2,1)S(1)}, bf16[3072,128]{1,0:T(8,128)(2,1)S(1)}, u32[]{:S(2)}, u32[]{:S(2)}) collective-permute-start(bf16[3072,128]{1,0:T(8,128)(2,1)S(1)} %bitcast.11), channel_id=1, source_target_pairs={{0,1},{1,0},{2,3},{3,2},{4,5},{5,4},{6,7},{7,6},{8,9},{9,8},{10,11... | collective-permute-start | bytes 2359304 | tf_op jit(solution)/shard_map/ppermute | solution.py:741
  121.8 1.3 %slice_reduce_fusion = f32[8]{0:T(128)} fusion(f32[40,128]{1,0:T(8,128)} %get-tuple-element.28), kind=kLoop, calls=%fused_computation.18 | loop fusion | bytes 64 | tf_op jit(solution)/shard_map/slice | solution.py:817
  123.1 0.6 collective-permute-done.1.other_ref
  123.7 0.9 copy-done.2
  124.6 3.2 %unpack.1 = (f32[3,2,512]{2,1,0:T(2,128)}, f32[2,512]{1,0:T(2,128)}, f32[2,512,512]{2,1,0:T(8,128)}, f32[512,256]{1,0:T(8,128)}) custom-call(s32[83]{0:T(128)} %pad_add_fusion.scalars, bf16[3072,128]{1,0:T(8,128)(2,1)} %bitcast.12, bf16[3072,128]{1,0:T(8,128)(2,1)} %copy-done.2, f32[3,2,512]{2,1,0:T(2,128)} %bitcast.17, f32[2,512]{1,0:T(2,128)} %gain_ref.5), custom_call_target="tpu_custom_call" | custom-call | tf_op jit(solution)/shard_map/unpack/pallas_call | solution.py:743
  (10 shorter events, 0.1 us)
Async XLA Ops:
  0.6 35.8 %copy-start.3 = (s32[1,128]{1,0:T(1,128)S(1)}, s32[1,128]{1,0:T(1,128)}, u32[]{:S(2)}) copy-start(s32[1,128]{1,0:T(1,128)} %param.13) | copy-start | bytes 1540
  27.5 16.3 %all-to-all-start = ((bf16[16,40,256]{2,1,0:T(8,128)(2,1)}), bf16[16,40,256]{2,1,0:T(8,128)(2,1)S(1)}, u32[]{:S(2)}, u32[]{:S(2)}) async-start(bf16[16,40,256]{2,1,0:T(8,128)(2,1)} %get-tuple-element.20), calls=%async_computation | async-start | bytes 655360 | tf_op jit(solution)/shard_map/all_to_all | solution.py:794
  43.8 0.7 copy-start.1
  73.2 4.5 %collective-permute-start = (bf16[3072,128]{1,0:T(8,128)(2,1)}, bf16[3072,128]{1,0:T(8,128)(2,1)S(1)}, u32[]{:S(2)}, u32[]{:S(2)}) collective-permute-start(bf16[3072,128]{1,0:T(8,128)(2,1)} %get-tuple-element.30), channel_id=1, source_target_pairs={{0,1},{1,0},{2,3},{3,2},{4,5},{5,4},{6,7},{7,6},{8,9},{9,8},{10,11... | collective-permute-start | bytes 2359304 | tf_op jit(solution)/shard_map/ppermute | solution.py:735
  118.9 4.8 %copy-start = (bf16[64,48,128]{2,1,0:T(8,128)(2,1)}, bf16[64,48,128]{2,1,0:T(8,128)(2,1)S(1)}, u32[]{:S(2)}) copy-start(bf16[64,48,128]{2,1,0:T(8,128)(2,1)S(1)} %all_to_all.16) | copy-start | bytes 2359300
  118.9 4.8 %collective-permute-start.1 = (bf16[3072,128]{1,0:T(8,128)(2,1)S(1)}, bf16[3072,128]{1,0:T(8,128)(2,1)S(1)}, u32[]{:S(2)}, u32[]{:S(2)}) collective-permute-start(bf16[3072,128]{1,0:T(8,128)(2,1)S(1)} %bitcast.11), channel_id=1, source_target_pairs={{0,1},{1,0},{2,3},{3,2},{4,5},{5,4},{6,7},{7,6},{8,9},{9,8},{10,11... | collective-permute-start | bytes 2359304 | tf_op jit(solution)/shard_map/ppermute | solution.py:741
  123.7 0.9 copy-start.2
